TPU v7x, 128 devices: a whole 4x4x4 slice. The times are simulated.
128 devices in a mesh: req: 8 (over x, core), seq: 16 (over y, z).
Axes of the slice: x: 4, y: 4, z: 4, core: 2. Of those that a mesh axis runs over, the one named last changes fastest.
Arguments:
- conv_input: bfloat16 [8, 8192, 5120], P('req', 'seq'), may hold values from -6 to 6
- gate_projected: bfloat16 [8, 8192, 4096], P('req', 'seq'), may hold values from -6 to 6
- step_raw: float32 [8, 8192, 64], P('req', 'seq'), may hold values from -1.5 to 6.5
- step_bias: float32 [64], replicated, may hold values from -16 to -3
- decay_log: float32 [64], replicated, may hold values from -0.35 to 0.35
- head_direct_gain: float32 [64], replicated, may hold values from 0.2 to 1
- conv_weight: float32 [4, 5120], replicated, may hold values from -3 to 3
- convolution_bias: float32 [5120], replicated, may hold values from -0.5 to 0.5
- norm_weight: float32 [4096], replicated, may hold values from 0.5 to 1.5
- lengths: int32 [8, 4], P('req'), may hold values from 1 to 4096, 8192 in all within a row
- out_weight: bfloat16 [4096, 4096], P(('req', 'seq')), may hold values from -0.375 to 0.375
- residual_last: bfloat16 [8, 4, 4096], replicated, may hold values from -6 to 6
- final_gain: float32 [4096], replicated, may hold values from 0.5 to 1.5
- vocab_weight: bfloat16 [131072, 4096], P(('req', 'seq')), may hold values from -0.25 to 0.25
Outputs:
- y_gated: bfloat16 [8, 8192, 4096], P('req', 'seq')
- final_states: float32 [8, 4, 64, 64, 128], P('req', None, 'seq')
- last_hidden: bfloat16 [8, 4, 4096], P('req')
- max_logit: float32 [8, 4], P('req')
Inputs may be any that keep to these rules, and one draw needn't show every extreme that they name: The 4 lengths of a row sum to 8192.
All inputs are finite; a program needn't handle non-finite values.
Results may differ from a plain program's by a relative error of at most 0.0046.
Values may be sent and summed in bfloat16 or wider, within the bound.
A program may use at most 256 MiB of HBM per device.

v0:
```python
import jax
import jax.numpy as jnp
from jax import lax
from jax.sharding import PartitionSpec as P

D = 4096
HEADS = 64
CHANNEL_WIDTH = 64
GROUPS = 4
STATE = 128
KERNEL = 4
BLOCK = 256
SEQS = 4


TINY_FLOOR = 1e-05


def from_behind(block, axis, distance):
    devices = range(lax.axis_size(axis))
    route = [(i - distance, i) for i in devices if i - distance in devices]
    return lax.ppermute(block, axis, route)


def segment_of(places, lengths):
    bounds = jnp.cumsum(lengths)[:-1]
    return jnp.sum((places[:, None] >= bounds[None, :]).astype(jnp.int32), axis=1)


def convolve(padded, padded_seg, conv_weight, convolution_bias, count):
    target = padded_seg[KERNEL - 1 :]
    total = jnp.zeros((count, padded.shape[1]), jnp.float32) + convolution_bias
    for kernel_tap in range(KERNEL):
        same_seg = (padded_seg[kernel_tap : kernel_tap + count] == target).astype(jnp.float32)
        total = (
            total
            + conv_weight[kernel_tap]
            * padded[kernel_tap : kernel_tap + count].astype(jnp.float32)
            * same_seg[:, None]
        )
    return jax.nn.silu(total)


def block_parts(
    feature_matrix,
    state_inputs,
    input_map,
    state_map,
    output_map,
    step_size,
    decays,
    segment,
    before,
):
    length = feature_matrix.shape[0]
    per_group = HEADS // GROUPS
    cum_decay = jnp.cumsum(decays, axis=0)
    places = jnp.arange(length)
    allowed = (places[:, None] >= places[None, :]) & (segment[:, None] == segment[None, :])
    spread = cum_decay.T[:, :, None] - cum_decay.T[:, None, :]
    weights = jnp.exp(jnp.where(allowed[None], spread, -jnp.inf)) * step_size.T[:, None, :]
    scores = jnp.einsum("tgn,sgn->gts", output_map, input_map, preferred_element_type=jnp.float32)
    mixing = (weights.reshape(GROUPS, per_group, length, length) * scores[:, None]).astype(
        jnp.bfloat16
    )
    grouped = feature_matrix.reshape(length, GROUPS, per_group, CHANNEL_WIDTH)
    y_intra = jnp.einsum(
        "gjts,sgjp->tgjp", mixing, grouped, preferred_element_type=jnp.float32
    ).reshape(length, HEADS, CHANNEL_WIDTH)
    tail_seg = (segment == segment[length - 1]).astype(jnp.float32)
    tail_weight = (
        jnp.exp(cum_decay[length - 1][None, :] - cum_decay) * step_size * tail_seg[:, None]
    )
    scaled = state_inputs * tail_weight[:, :, None]
    state = jnp.einsum(
        "sgjp,sgn->gjpn",
        scaled.reshape(length, GROUPS, per_group, CHANNEL_WIDTH),
        state_map,
        precision=lax.Precision.HIGHEST,
    ).reshape(HEADS, CHANNEL_WIDTH, STATE)
    within_tile = (segment == before).astype(jnp.float32)
    lead = jnp.exp(cum_decay) * within_tile[:, None]
    carry = jnp.exp(cum_decay[length - 1]) * within_tile[length - 1]
    return (y_intra, lead, state, carry)


def block_output(y_intra, lead, entering, output_map, feature_matrix, head_direct_gain):
    length = feature_matrix.shape[0]
    per_group = HEADS // GROUPS
    inter = jnp.einsum(
        "tgn,gjpn->tgjp",
        output_map.astype(jnp.float32),
        entering.reshape(GROUPS, per_group, CHANNEL_WIDTH, STATE),
        precision=lax.Precision.HIGHEST,
    ).reshape(length, HEADS, CHANNEL_WIDTH)
    return (
        y_intra
        + lead[:, :, None] * inter
        + head_direct_gain[None, :, None] * feature_matrix.astype(jnp.float32)
    )


def gate_norm(values, gate, norm_weight):
    length = values.shape[0]
    flat = values.reshape(length, -1) * jax.nn.silu(gate.astype(jnp.float32))
    grouped = flat.reshape(length, GROUPS, -1)
    scale = lax.rsqrt(jnp.mean(grouped * grouped, axis=-1, keepdims=True) + TINY_FLOOR)
    return ((grouped * scale).reshape(length, -1) * norm_weight).astype(jnp.bfloat16)


def state_at(state_inputs, state_map, step_size, decays, segment, before, within, entering):
    length = state_inputs.shape[0]
    per_group = HEADS // GROUPS
    cum_decay = jnp.cumsum(decays, axis=0)
    places = jnp.arange(length)
    allowed = (segment == segment[within]) & (places <= within)
    tail_weight = (
        jnp.exp(jnp.where(allowed[:, None], cum_decay[within][None, :] - cum_decay, -jnp.inf))
        * step_size
    )
    scaled = state_inputs * tail_weight[:, :, None]
    state = jnp.einsum(
        "sgjp,sgn->gjpn",
        scaled.reshape(length, GROUPS, per_group, CHANNEL_WIDTH),
        state_map,
        precision=lax.Precision.HIGHEST,
    ).reshape(HEADS, CHANNEL_WIDTH, STATE)
    lead = jnp.exp(cum_decay[within]) * (segment[within] == before).astype(jnp.float32)
    return lead[:, None, None] * entering + state


def body(
    conv_input,
    gate_projected,
    step_raw,
    step_bias,
    decay_log,
    head_direct_gain,
    conv_weight,
    convolution_bias,
    norm_weight,
    lengths,
    out_weight,
    residual_last,
    final_gain,
    vocab_weight,
):
    local_len = conv_input.shape[1]
    inner = HEADS * CHANNEL_WIDTH
    split_at = inner + GROUPS * STATE
    count = local_len // BLOCK
    seq_count = lax.axis_size("seq")
    seq_place = lax.axis_index("seq")
    req_place = lax.axis_index("req")
    first = seq_place * local_len
    length_row = lengths[0]
    own_rows = conv_input[0]
    edge = from_behind(own_rows[local_len - (KERNEL - 1) :], "seq", 1)
    padded = jnp.concatenate([edge, own_rows], axis=0)
    padded_places = first - (KERNEL - 1) + jnp.arange(local_len + KERNEL - 1, dtype=jnp.int32)
    padded_seg = segment_of(padded_places, length_row)
    segment = padded_seg[KERNEL - 1 :]
    mixed_full = convolve(padded, padded_seg, conv_weight, convolution_bias, local_len)
    mixed = mixed_full.astype(jnp.bfloat16)
    feature_matrix = mixed[:, :inner].reshape(local_len, HEADS, CHANNEL_WIDTH)
    input_map = mixed[:, inner:split_at].reshape(local_len, GROUPS, STATE)
    output_map = mixed[:, split_at:].reshape(local_len, GROUPS, STATE)
    state_inputs = mixed_full[:, :inner].reshape(local_len, HEADS, CHANNEL_WIDTH)
    state_map = mixed_full[:, inner:split_at].reshape(local_len, GROUPS, STATE)
    step_size = jax.nn.softplus(step_raw[0] + step_bias)
    decays = -jnp.exp(decay_log) * step_size
    befores = segment_of(first - 1 + BLOCK * jnp.arange(count, dtype=jnp.int32), length_row)
    block_inputs = feature_matrix.reshape(count, BLOCK, HEADS, CHANNEL_WIDTH)
    block_out_map = output_map.reshape(count, BLOCK, GROUPS, STATE)

    def local_pass(block):
        (
            part_inputs,
            part_state_inputs,
            part_in_map,
            part_state_map,
            part_out_map,
            part_step,
            part_decay,
            prompt_stretch,
            before,
        ) = block
        return block_parts(
            part_inputs,
            part_state_inputs,
            part_in_map,
            part_state_map,
            part_out_map,
            part_step,
            part_decay,
            prompt_stretch,
            before,
        )

    y_intra, leads, states, carries = lax.map(
        local_pass,
        (
            block_inputs,
            state_inputs.reshape(count, BLOCK, HEADS, CHANNEL_WIDTH),
            input_map.reshape(count, BLOCK, GROUPS, STATE),
            state_map.reshape(count, BLOCK, GROUPS, STATE),
            block_out_map,
            step_size.reshape(count, BLOCK, HEADS),
            decays.reshape(count, BLOCK, HEADS),
            segment.reshape(count, BLOCK),
            befores,
        ),
    )

    def fold(summary, block):
        carry, state = block
        return ((summary[0] * carry, carry[:, None, None] * summary[1] + state), None)

    (span_carry, span_state), _ = lax.scan(
        fold,
        (jnp.ones((HEADS,), jnp.float32), jnp.zeros((HEADS, CHANNEL_WIDTH, STATE), jnp.float32)),
        (carries, states),
    )

    def relay(turn, incoming):
        return from_behind(span_carry[:, None, None] * incoming + span_state, "seq", 1)

    entry_state = lax.fori_loop(0, seq_count - 1, relay, jnp.zeros_like(span_state))

    def enter(incoming, block):
        carry, state = block
        return (carry[:, None, None] * incoming + state, incoming)

    _, entering = lax.scan(enter, entry_state, (carries, states))

    def finish(block):
        part_intra, part_lead, part_enter, part_out_map, part_inputs, section_gate = block
        values = block_output(
            part_intra, part_lead, part_enter, part_out_map, part_inputs, head_direct_gain
        )
        return gate_norm(values, section_gate, norm_weight)

    gated = lax.map(
        finish,
        (
            y_intra,
            leads,
            entering,
            block_out_map,
            block_inputs,
            gate_projected[0].reshape(count, BLOCK, inner),
        ),
    ).reshape(local_len, inner)
    ends = jnp.cumsum(length_row) - 1
    finals = []
    lasts = []
    for request in range(SEQS):
        local_end = ends[request] - first
        owned = (local_end >= 0) & (local_end < local_len)
        spot = jnp.clip(local_end, 0, local_len - 1)
        index = spot // BLOCK
        start = index * BLOCK
        within = spot - start
        reached = state_at(
            lax.dynamic_slice_in_dim(state_inputs, start, BLOCK, 0),
            lax.dynamic_slice_in_dim(state_map, start, BLOCK, 0),
            lax.dynamic_slice_in_dim(step_size, start, BLOCK, 0),
            lax.dynamic_slice_in_dim(decays, start, BLOCK, 0),
            lax.dynamic_slice_in_dim(segment, start, BLOCK, 0),
            befores[index],
            within,
            entering[index],
        )
        finals.append(jnp.where(owned, reached, 0.0))
        lasts.append(jnp.where(owned, gated[spot].astype(jnp.float32), 0.0))
    final_terms = jnp.stack(finals)
    final_states = lax.psum_scatter(final_terms, "seq", scatter_dimension=1, tiled=True)[None]
    last_local = jnp.stack(lasts)
    rows_total = residual_last.shape[0]
    group_rows = lax.psum(last_local.astype(jnp.bfloat16), "seq")[None]
    all_rows = lax.all_gather(group_rows, "req", axis=0, tiled=True)
    share = out_weight.shape[0]
    flat_place = req_place * seq_count + seq_place
    columns = lax.dynamic_slice_in_dim(all_rows.reshape(-1, inner), flat_place * share, share, 1)
    partial_value = jnp.dot(columns, out_weight, preferred_element_type=jnp.float32)
    summed = lax.psum(partial_value, ("req", "seq"))
    hidden = residual_last.reshape(-1, D).astype(jnp.float32) + summed
    last_hidden = hidden.astype(jnp.bfloat16).reshape(rows_total, SEQS, D)
    own_hidden = lax.dynamic_slice_in_dim(last_hidden, req_place, 1, 0)
    scale = lax.rsqrt(jnp.mean(hidden * hidden, axis=-1, keepdims=True) + TINY_FLOOR)
    normed = (hidden * scale * final_gain).astype(jnp.bfloat16)
    logits = lax.dot_general(
        normed, vocab_weight, (((1,), (1,)), ((), ())), preferred_element_type=jnp.float32
    )
    local_top = jnp.max(logits, axis=1)
    top_all = lax.pmax(local_top, ("req", "seq"))
    max_logit = lax.dynamic_slice_in_dim(top_all.reshape(rows_total, SEQS), req_place, 1, 0)
    return (gated[None], final_states, own_hidden, max_logit)


def solution(mesh):
    return jax.shard_map(
        body,
        mesh=mesh,
        in_specs=(
            P("req", "seq", None),
            P("req", "seq", None),
            P("req", "seq", None),
            P(),
            P(),
            P(),
            P(),
            P(),
            P(),
            P("req", None),
            P(("req", "seq"), None),
            P(),
            P(),
            P(("req", "seq"), None),
        ),
        out_specs=(
            P("req", "seq", None),
            P("req", None, "seq", None, None),
            P("req", None, None),
            P("req", None),
        ),
        check_vma=False,
    )
```

profile of v0, /device:TPU:1, one launch (start us, length us, event | category | flops | bytes accessed | tf_op | source)
XLA Modules:
  0.0 1393.4 jit_solution(17689072998252525378)
XLA Ops:
  8.2 4.4 collective-permute-start.1
  40.7 8.0 copy.137
  50.9 19.7 %fusion.71 = (bf16[512,5120]{0,1:T(8,128)(2,1)S(1)}, f32[512,5120]{0,1:T(8,128)S(1)}) fusion(bf16[512,5120]{0,1:T(8,128)(2,1)} %bitcast.387, f32[5120]{0:T(1024)S(1)} %bitcast.406, f32[512]{0:T(512)S(1)} %get-tuple-element.516, bf16[3,5120]{0,1:T(8,128)(2,1)} %copy.138, f32[5120]{0:T(1024)S(1)} %bitcast.407, f32[512]{0:T(512)S(1)} %get-tuple-element.517, ...), kind=kLoop, calls=%fused_computation.191 | loop fusion | flops 76021760 | bytes 21110784 | tf_op jit(solution)/shard_map/convert_element_type | solution.py:164
  73.9 4.2 slice.158
  82.5 10.6 reshape_reshape.18
  93.1 6.9 reshape_reshape.15
  100.0 5.1 copy.142
  113.2 90.7 %while.61 = (s32[]{:T(128)}, f32[2,256,64,64]{1,3,2,0:T(8,128)}, f32[2,256,64]{1,2,0:T(8,128)}, f32[2,64,64,128]{3,2,1,0:T(8,128)}, f32[2,64]{1,0:T(2,128)}, /*i...) while((s32[]{:T(128)}, f32[2,256,64,64]{1,3,2,0:T(8,128)}, ...), condition=%wide.region_6.7_spmd, body=%wide.region_3.6_spmd.sunk | while | flops 2239022336 | bytes 152852832 | solution.py:200
  122.6 9.8 constant_dynamic-slice_fusion.22
  132.3 4.8 copy.259
  138.1 5.7 fusion.121
  149.5 4.5 fusion.119
  167.8 9.8 constant_dynamic-slice_fusion.22
  177.6 4.8 copy.259
  183.3 5.7 fusion.121
  194.8 4.5 fusion.119
  203.8 5.1 while.65
  210.6 706.7 %while.62 = (s32[]{:T(128)}, f32[64,64,128]{2,1,0:T(8,128)S(1)}, f32[64]{0:T(128)S(1)}, f32[64,64,128]{2,1,0:T(8,128)}, s32[]{:T(128)}) while((s32[]{:T(128)}, f32[64,64,128]{2,1,0:T(8,128)S(1)}, f32[64]{0:T(128)S(1)}, f32[64,64,128]{2,1,0:T(8,128)}, s32[]{:T(128)}) %tuple.170), condition=%wide.region_10.11_spmd, body=%wide.region_9.10_spmd.sunk | while | flops 1048578 | bytes 14680421 | solution.py:228
  217.7 44.2 %collective-permute-done = f32[64,64,128]{2,1,0:T(8,128)S(1)} collective-permute-done((f32[64,64,128]{2,1,0:T(8,128)}, f32[64,64,128]{2,1,0:T(8,128)S(1)}, u32[]{:S(2)}, u32[]{:S(2)}) %collective-permute-start) | collective-permute-done | bytes 2097184 | tf_op jit(solution)/shard_map/while/body/eval_jaxpr/ppermute | solution.py:22
  265.0 4.1 collective-permute-start
  269.1 43.3 %collective-permute-done = f32[64,64,128]{2,1,0:T(8,128)S(1)} collective-permute-done((f32[64,64,128]{2,1,0:T(8,128)}, f32[64,64,128]{2,1,0:T(8,128)S(1)}, u32[]{:S(2)}, u32[]{:S(2)}) %collective-permute-start) | collective-permute-done | bytes 2097184 | tf_op jit(solution)/shard_map/while/body/eval_jaxpr/ppermute | solution.py:22
  315.6 4.1 collective-permute-start
  319.8 42.5 %collective-permute-done = f32[64,64,128]{2,1,0:T(8,128)S(1)} collective-permute-done((f32[64,64,128]{2,1,0:T(8,128)}, f32[64,64,128]{2,1,0:T(8,128)S(1)}, u32[]{:S(2)}, u32[]{:S(2)}) %collective-permute-start) | collective-permute-done | bytes 2097184 | tf_op jit(solution)/shard_map/while/body/eval_jaxpr/ppermute | solution.py:22
  365.4 4.1 collective-permute-start
  369.5 41.6 %collective-permute-done = f32[64,64,128]{2,1,0:T(8,128)S(1)} collective-permute-done((f32[64,64,128]{2,1,0:T(8,128)}, f32[64,64,128]{2,1,0:T(8,128)S(1)}, u32[]{:S(2)}, u32[]{:S(2)}) %collective-permute-start) | collective-permute-done | bytes 2097184 | tf_op jit(solution)/shard_map/while/body/eval_jaxpr/ppermute | solution.py:22
  414.3 4.1 collective-permute-start
  418.4 40.8 %collective-permute-done = f32[64,64,128]{2,1,0:T(8,128)S(1)} collective-permute-done((f32[64,64,128]{2,1,0:T(8,128)}, f32[64,64,128]{2,1,0:T(8,128)S(1)}, u32[]{:S(2)}, u32[]{:S(2)}) %collective-permute-start) | collective-permute-done | bytes 2097184 | tf_op jit(solution)/shard_map/while/body/eval_jaxpr/ppermute | solution.py:22
  462.4 4.9 collective-permute-start
  467.3 39.9 %collective-permute-done = f32[64,64,128]{2,1,0:T(8,128)S(1)} collective-permute-done((f32[64,64,128]{2,1,0:T(8,128)}, f32[64,64,128]{2,1,0:T(8,128)S(1)}, u32[]{:S(2)}, u32[]{:S(2)}) %collective-permute-start) | collective-permute-done | bytes 2097184 | tf_op jit(solution)/shard_map/while/body/eval_jaxpr/ppermute | solution.py:22
  510.4 6.2 collective-permute-start
  516.6 39.1 %collective-permute-done = f32[64,64,128]{2,1,0:T(8,128)S(1)} collective-permute-done((f32[64,64,128]{2,1,0:T(8,128)}, f32[64,64,128]{2,1,0:T(8,128)S(1)}, u32[]{:S(2)}, u32[]{:S(2)}) %collective-permute-start) | collective-permute-done | bytes 2097184 | tf_op jit(solution)/shard_map/while/body/eval_jaxpr/ppermute | solution.py:22
  558.8 6.2 collective-permute-start
  565.1 38.2 %collective-permute-done = f32[64,64,128]{2,1,0:T(8,128)S(1)} collective-permute-done((f32[64,64,128]{2,1,0:T(8,128)}, f32[64,64,128]{2,1,0:T(8,128)S(1)}, u32[]{:S(2)}, u32[]{:S(2)}) %collective-permute-start) | collective-permute-done | bytes 2097184 | tf_op jit(solution)/shard_map/while/body/eval_jaxpr/ppermute | solution.py:22
  606.4 6.2 collective-permute-start
  612.7 37.3 %collective-permute-done = f32[64,64,128]{2,1,0:T(8,128)S(1)} collective-permute-done((f32[64,64,128]{2,1,0:T(8,128)}, f32[64,64,128]{2,1,0:T(8,128)S(1)}, u32[]{:S(2)}, u32[]{:S(2)}) %collective-permute-start) | collective-permute-done | bytes 2097184 | tf_op jit(solution)/shard_map/while/body/eval_jaxpr/ppermute | solution.py:22
  653.2 6.2 collective-permute-start
  659.4 36.5 %collective-permute-done = f32[64,64,128]{2,1,0:T(8,128)S(1)} collective-permute-done((f32[64,64,128]{2,1,0:T(8,128)}, f32[64,64,128]{2,1,0:T(8,128)S(1)}, u32[]{:S(2)}, u32[]{:S(2)}) %collective-permute-start) | collective-permute-done | bytes 2097184 | tf_op jit(solution)/shard_map/while/body/eval_jaxpr/ppermute | solution.py:22
  699.0 6.2 collective-permute-start
  705.3 35.6 %collective-permute-done = f32[64,64,128]{2,1,0:T(8,128)S(1)} collective-permute-done((f32[64,64,128]{2,1,0:T(8,128)}, f32[64,64,128]{2,1,0:T(8,128)S(1)}, u32[]{:S(2)}, u32[]{:S(2)}) %collective-permute-start) | collective-permute-done | bytes 2097184 | tf_op jit(solution)/shard_map/while/body/eval_jaxpr/ppermute | solution.py:22
  744.1 6.2 collective-permute-start
  750.3 34.8 %collective-permute-done = f32[64,64,128]{2,1,0:T(8,128)S(1)} collective-permute-done((f32[64,64,128]{2,1,0:T(8,128)}, f32[64,64,128]{2,1,0:T(8,128)S(1)}, u32[]{:S(2)}, u32[]{:S(2)}) %collective-permute-start) | collective-permute-done | bytes 2097184 | tf_op jit(solution)/shard_map/while/body/eval_jaxpr/ppermute | solution.py:22
  788.2 6.2 collective-permute-start
  794.5 34.7 %collective-permute-done = f32[64,64,128]{2,1,0:T(8,128)S(1)} collective-permute-done((f32[64,64,128]{2,1,0:T(8,128)}, f32[64,64,128]{2,1,0:T(8,128)S(1)}, u32[]{:S(2)}, u32[]{:S(2)}) %collective-permute-start) | collective-permute-done | bytes 2097184 | tf_op jit(solution)/shard_map/while/body/eval_jaxpr/ppermute | solution.py:22
  832.3 6.2 collective-permute-start
  838.6 34.7 %collective-permute-done = f32[64,64,128]{2,1,0:T(8,128)S(1)} collective-permute-done((f32[64,64,128]{2,1,0:T(8,128)}, f32[64,64,128]{2,1,0:T(8,128)S(1)}, u32[]{:S(2)}, u32[]{:S(2)}) %collective-permute-start) | collective-permute-done | bytes 2097184 | tf_op jit(solution)/shard_map/while/body/eval_jaxpr/ppermute | solution.py:22
  876.4 6.2 collective-permute-start
  882.7 34.7 %collective-permute-done = f32[64,64,128]{2,1,0:T(8,128)S(1)} collective-permute-done((f32[64,64,128]{2,1,0:T(8,128)}, f32[64,64,128]{2,1,0:T(8,128)S(1)}, u32[]{:S(2)}, u32[]{:S(2)}) %collective-permute-start) | collective-permute-done | bytes 2097184 | tf_op jit(solution)/shard_map/while/body/eval_jaxpr/ppermute | solution.py:22
  919.8 6.8 while.63
  926.7 62.9 %while.64 = (s32[]{:T(128)}, bf16[2,256,4096]{2,1,0:T(8,128)(2,1)}, f32[2,256,64,64]{1,3,2,0:T(8,128)}, f32[2,256,64]{1,2,0:T(8,128)S(1)}, f32[2,64,64,128]{3,2,...) while((s32[]{:T(128)}, bf16[2,256,4096]{2,1,0:T(8,128)(2,1)}, ...), condition=%wide.region_16.17_spmd, body=%wide.region_13.16_spmd.sunk | while | flops 1638925312 | bytes 101418176 | solution.py:243
  937.1 6.9 fusion.126
  946.7 7.1 fusion.127
  968.5 6.9 fusion.126
  978.1 7.1 fusion.127
  990.8 66.0 %psum.14 = bf16[1,4,4096]{2,1,0:T(4,128)(2,1)S(1)} all-reduce(bf16[1,4,4096]{2,1,0:T(4,128)(2,1)S(1)} %maximum_bitcast_fusion), channel_id=1, replica_groups=mesh['req'=8,'seq'=16] {'seq'}, use_global_device_ids=true, to_apply=%region_26.27 | all-reduce | flops 16384 | bytes 65536 | tf_op jit(solution)/shard_map/psum | solution.py:280
  1056.7 40.4 %all_gather.3 = bf16[8,4,4096]{2,1,0:T(4,128)(2,1)S(1)} all-gather(bf16[1,4,4096]{2,1,0:T(4,128)(2,1)S(1)} %psum.14), channel_id=1, replica_groups=mesh['req'=8,'seq'=16] {'req'}, dimensions={0}, use_global_device_ids=true | all-gather | bytes 294912 | tf_op jit(solution)/shard_map/all_gather | solution.py:281
  1098.4 8.4 dynamic-slice_multiply_fusion.3
  1106.9 3.9 fusion.46
  1110.8 3.9 fusion.44
  1114.7 3.9 fusion.42
  1118.7 4.1 fusion.48
  1129.5 110.8 %all-reduce.4.cloned.1.call-done = f32[32,4096]{1,0:T(8,128)} async-done(((f32[32,4096]{1,0:T(8,128)}), f32[32,4096]{1,0:T(8,128)}) %all-reduce.4.cloned.1.call-update) | async-done | bytes 524304 | tf_op jit(solution)/shard_map/psum | solution.py:286
  1241.5 6.1 convolution_reduce_fusion
  1248.4 66.5 %pmax.7 = f32[8,4]{1,0:T(8,128)S(1)} all-reduce(f32[8,4]{1,0:T(8,128)S(1)} %reshape.504), channel_id=1, replica_groups=mesh['req'=8,'seq'=16] {'req','seq'}, use_global_device_ids=true, to_apply=%region_30.31 | all-reduce | flops 32 | bytes 256 | tf_op jit(solution)/shard_map/pmax | solution.py:296
  1316.1 68.4 %all-reduce.6.cloned.1.call-done = f32[4,64,64,128]{3,2,1,0:T(8,128)} async-done(((f32[4,64,64,128]{3,2,1,0:T(8,128)}), f32[4,64,64,128]{3,2,1,0:T(8,128)}) %all-reduce.6.cloned.1.call-update) | async-done | bytes 8388624
  (303 shorter events, 194.7 us)
Async XLA Ops:
  7.2 1090.1 %copy-start = (bf16[32,4096]{1,0:T(8,128)(2,1)S(1)}, bf16[32,4096]{1,0:T(8,128)(2,1)}, u32[]{:S(2)}) copy-start(bf16[32,4096]{1,0:T(8,128)(2,1)} %param.34) | copy-start | bytes 786436
  7.2 1233.1 %all-reduce.4.cloned.1.call-start = ((), (), s32[]{:S(2)}) async-start(), calls=%async_computation | async-start | bytes 1048576 | tf_op jit(solution)/shard_map/psum | solution.py:286
  8.2 41.1 %collective-permute-start.1 = (bf16[3,5120]{1,0:T(4,128)(2,1)S(1)}, bf16[3,5120]{1,0:T(4,128)(2,1)S(1)}, u32[]{:S(2)}, u32[]{:S(2)}) collective-permute-start(bf16[3,5120]{1,0:T(4,128)(2,1)S(1)} %slice_bitcast_fusion), channel_id=1, source_target_pairs={{0,1},{1,2},{2,3},{3,4},{4,5},{5,6},{6,7},{7,8},{8,9},{9,10},{10,1... | collective-permute-start | bytes 92168 | tf_op jit(solution)/shard_map/ppermute | solution.py:22
  40.7 10.2 copy-start.25
  78.2 30.8 %copy-start.11 = (f32[512,512]{0,1:T(8,128)}, f32[512,512]{0,1:T(8,128)S(1)}, u32[]{:S(2)}) copy-start(f32[512,512]{0,1:T(8,128)S(1)} %slice.159) | copy-start | bytes 3145732
  132.3 4.8 copy-start.13
  138.0 5.7 copy-start.3
  138.1 8.3 copy-start.9
  144.1 1.9 copy-start.4
  147.6 6.4 slice-start
  149.5 4.5 slice-start.1
  154.1 3.8 copy-start.14
  154.1 3.9 copy-start.27
  154.7 3.2 copy-start.7
  177.6 4.8 copy-start.13
  183.3 5.7 copy-start.3
  183.3 8.3 copy-start.9
  189.3 1.9 copy-start.4
  192.9 6.4 slice-start
  194.8 4.5 slice-start.1
  199.3 3.8 copy-start.14
  199.3 3.9 copy-start.27
  199.9 3.2 copy-start.7
  209.0 1.4 copy-start.2
  214.0 47.9 %collective-permute-start = (f32[64,64,128]{2,1,0:T(8,128)}, f32[64,64,128]{2,1,0:T(8,128)S(1)}, u32[]{:S(2)}, u32[]{:S(2)}) collective-permute-start(f32[64,64,128]{2,1,0:T(8,128)} %multiply_add_fusion.3), channel_id=1, source_target_pairs={{0,1},{1,2},{2,3},{3,4},{4,5},{5,6},{6,7},{7,8},{8,9},{9,10},{10,1... | collective-permute-start | bytes 6291464 | tf_op jit(solution)/shard_map/while/body/eval_jaxpr/ppermute | solution.py:22
  265.0 47.5 %collective-permute-start = (f32[64,64,128]{2,1,0:T(8,128)}, f32[64,64,128]{2,1,0:T(8,128)S(1)}, u32[]{:S(2)}, u32[]{:S(2)}) collective-permute-start(f32[64,64,128]{2,1,0:T(8,128)} %multiply_add_fusion.3), channel_id=1, source_target_pairs={{0,1},{1,2},{2,3},{3,4},{4,5},{5,6},{6,7},{7,8},{8,9},{9,10},{10,1... | collective-permute-start | bytes 6291464 | tf_op jit(solution)/shard_map/while/body/eval_jaxpr/ppermute | solution.py:22
  315.6 46.6 %collective-permute-start = (f32[64,64,128]{2,1,0:T(8,128)}, f32[64,64,128]{2,1,0:T(8,128)S(1)}, u32[]{:S(2)}, u32[]{:S(2)}) collective-permute-start(f32[64,64,128]{2,1,0:T(8,128)} %multiply_add_fusion.3), channel_id=1, source_target_pairs={{0,1},{1,2},{2,3},{3,4},{4,5},{5,6},{6,7},{7,8},{8,9},{9,10},{10,1... | collective-permute-start | bytes 6291464 | tf_op jit(solution)/shard_map/while/body/eval_jaxpr/ppermute | solution.py:22
  365.4 45.8 %collective-permute-start = (f32[64,64,128]{2,1,0:T(8,128)}, f32[64,64,128]{2,1,0:T(8,128)S(1)}, u32[]{:S(2)}, u32[]{:S(2)}) collective-permute-start(f32[64,64,128]{2,1,0:T(8,128)} %multiply_add_fusion.3), channel_id=1, source_target_pairs={{0,1},{1,2},{2,3},{3,4},{4,5},{5,6},{6,7},{7,8},{8,9},{9,10},{10,1... | collective-permute-start | bytes 6291464 | tf_op jit(solution)/shard_map/while/body/eval_jaxpr/ppermute | solution.py:22
  414.3 44.9 %collective-permute-start = (f32[64,64,128]{2,1,0:T(8,128)}, f32[64,64,128]{2,1,0:T(8,128)S(1)}, u32[]{:S(2)}, u32[]{:S(2)}) collective-permute-start(f32[64,64,128]{2,1,0:T(8,128)} %multiply_add_fusion.3), channel_id=1, source_target_pairs={{0,1},{1,2},{2,3},{3,4},{4,5},{5,6},{6,7},{7,8},{8,9},{9,10},{10,1... | collective-permute-start | bytes 6291464 | tf_op jit(solution)/shard_map/while/body/eval_jaxpr/ppermute | solution.py:22
  462.4 44.9 %collective-permute-start = (f32[64,64,128]{2,1,0:T(8,128)}, f32[64,64,128]{2,1,0:T(8,128)S(1)}, u32[]{:S(2)}, u32[]{:S(2)}) collective-permute-start(f32[64,64,128]{2,1,0:T(8,128)} %multiply_add_fusion.3), channel_id=1, source_target_pairs={{0,1},{1,2},{2,3},{3,4},{4,5},{5,6},{6,7},{7,8},{8,9},{9,10},{10,1... | collective-permute-start | bytes 6291464 | tf_op jit(solution)/shard_map/while/body/eval_jaxpr/ppermute | solution.py:22
  510.4 45.3 %collective-permute-start = (f32[64,64,128]{2,1,0:T(8,128)}, f32[64,64,128]{2,1,0:T(8,128)S(1)}, u32[]{:S(2)}, u32[]{:S(2)}) collective-permute-start(f32[64,64,128]{2,1,0:T(8,128)} %multiply_add_fusion.3), channel_id=1, source_target_pairs={{0,1},{1,2},{2,3},{3,4},{4,5},{5,6},{6,7},{7,8},{8,9},{9,10},{10,1... | collective-permute-start | bytes 6291464 | tf_op jit(solution)/shard_map/while/body/eval_jaxpr/ppermute | solution.py:22
  558.8 44.4 %collective-permute-start = (f32[64,64,128]{2,1,0:T(8,128)}, f32[64,64,128]{2,1,0:T(8,128)S(1)}, u32[]{:S(2)}, u32[]{:S(2)}) collective-permute-start(f32[64,64,128]{2,1,0:T(8,128)} %multiply_add_fusion.3), channel_id=1, source_target_pairs={{0,1},{1,2},{2,3},{3,4},{4,5},{5,6},{6,7},{7,8},{8,9},{9,10},{10,1... | collective-permute-start | bytes 6291464 | tf_op jit(solution)/shard_map/while/body/eval_jaxpr/ppermute | solution.py:22
  606.4 43.6 %collective-permute-start = (f32[64,64,128]{2,1,0:T(8,128)}, f32[64,64,128]{2,1,0:T(8,128)S(1)}, u32[]{:S(2)}, u32[]{:S(2)}) collective-permute-start(f32[64,64,128]{2,1,0:T(8,128)} %multiply_add_fusion.3), channel_id=1, source_target_pairs={{0,1},{1,2},{2,3},{3,4},{4,5},{5,6},{6,7},{7,8},{8,9},{9,10},{10,1... | collective-permute-start | bytes 6291464 | tf_op jit(solution)/shard_map/while/body/eval_jaxpr/ppermute | solution.py:22
  653.2 42.7 %collective-permute-start = (f32[64,64,128]{2,1,0:T(8,128)}, f32[64,64,128]{2,1,0:T(8,128)S(1)}, u32[]{:S(2)}, u32[]{:S(2)}) collective-permute-start(f32[64,64,128]{2,1,0:T(8,128)} %multiply_add_fusion.3), channel_id=1, source_target_pairs={{0,1},{1,2},{2,3},{3,4},{4,5},{5,6},{6,7},{7,8},{8,9},{9,10},{10,1... | collective-permute-start | bytes 6291464 | tf_op jit(solution)/shard_map/while/body/eval_jaxpr/ppermute | solution.py:22
  699.0 41.9 %collective-permute-start = (f32[64,64,128]{2,1,0:T(8,128)}, f32[64,64,128]{2,1,0:T(8,128)S(1)}, u32[]{:S(2)}, u32[]{:S(2)}) collective-permute-start(f32[64,64,128]{2,1,0:T(8,128)} %multiply_add_fusion.3), channel_id=1, source_target_pairs={{0,1},{1,2},{2,3},{3,4},{4,5},{5,6},{6,7},{7,8},{8,9},{9,10},{10,1... | collective-permute-start | bytes 6291464 | tf_op jit(solution)/shard_map/while/body/eval_jaxpr/ppermute | solution.py:22
  744.1 41.0 %collective-permute-start = (f32[64,64,128]{2,1,0:T(8,128)}, f32[64,64,128]{2,1,0:T(8,128)S(1)}, u32[]{:S(2)}, u32[]{:S(2)}) collective-permute-start(f32[64,64,128]{2,1,0:T(8,128)} %multiply_add_fusion.3), channel_id=1, source_target_pairs={{0,1},{1,2},{2,3},{3,4},{4,5},{5,6},{6,7},{7,8},{8,9},{9,10},{10,1... | collective-permute-start | bytes 6291464 | tf_op jit(solution)/shard_map/while/body/eval_jaxpr/ppermute | solution.py:22
  788.2 40.9 %collective-permute-start = (f32[64,64,128]{2,1,0:T(8,128)}, f32[64,64,128]{2,1,0:T(8,128)S(1)}, u32[]{:S(2)}, u32[]{:S(2)}) collective-permute-start(f32[64,64,128]{2,1,0:T(8,128)} %multiply_add_fusion.3), channel_id=1, source_target_pairs={{0,1},{1,2},{2,3},{3,4},{4,5},{5,6},{6,7},{7,8},{8,9},{9,10},{10,1... | collective-permute-start | bytes 6291464 | tf_op jit(solution)/shard_map/while/body/eval_jaxpr/ppermute | solution.py:22
  832.3 40.9 %collective-permute-start = (f32[64,64,128]{2,1,0:T(8,128)}, f32[64,64,128]{2,1,0:T(8,128)S(1)}, u32[]{:S(2)}, u32[]{:S(2)}) collective-permute-start(f32[64,64,128]{2,1,0:T(8,128)} %multiply_add_fusion.3), channel_id=1, source_target_pairs={{0,1},{1,2},{2,3},{3,4},{4,5},{5,6},{6,7},{7,8},{8,9},{9,10},{10,1... | collective-permute-start | bytes 6291464 | tf_op jit(solution)/shard_map/while/body/eval_jaxpr/ppermute | solution.py:22
  876.4 40.9 %collective-permute-start = (f32[64,64,128]{2,1,0:T(8,128)}, f32[64,64,128]{2,1,0:T(8,128)S(1)}, u32[]{:S(2)}, u32[]{:S(2)}) collective-permute-start(f32[64,64,128]{2,1,0:T(8,128)} %multiply_add_fusion.3), channel_id=1, source_target_pairs={{0,1},{1,2},{2,3},{3,4},{4,5},{5,6},{6,7},{7,8},{8,9},{9,10},{10,1... | collective-permute-start | bytes 6291464 | tf_op jit(solution)/shard_map/while/body/eval_jaxpr/ppermute | solution.py:22
  917.3 2.5 copy-start.29
  917.3 9.3 copy-start.10
  917.3 9.3 copy-start.17
  919.8 6.8 copy-start.18
  919.8 6.8 copy-start.24
  919.8 3.0 copy-start.5
  923.3 2.9 copy-start.5
  926.7 171.7 %copy-start.19 = (f32[256,64]{0,1:T(8,128)S(1)}, f32[256,64]{0,1:T(8,128)}, u32[]{:S(2)}) copy-start(f32[256,64]{0,1:T(8,128)} %get-tuple-element.503) | copy-start | bytes 196612
  926.7 171.7 %copy-start.20 = (f32[256,64]{0,1:T(8,128)S(1)}, f32[256,64]{0,1:T(8,128)}, u32[]{:S(2)}) copy-start(f32[256,64]{0,1:T(8,128)} %get-tuple-element.504) | copy-start | bytes 196612
  926.7 171.7 %copy-start.21 = (f32[256,64]{0,1:T(8,128)S(1)}, f32[256,64]{0,1:T(8,128)}, u32[]{:S(2)}) copy-start(f32[256,64]{0,1:T(8,128)} %get-tuple-element.505) | copy-start | bytes 196612
  926.7 171.7 %copy-start.22 = (f32[256,64]{0,1:T(8,128)S(1)}, f32[256,64]{0,1:T(8,128)}, u32[]{:S(2)}) copy-start(f32[256,64]{0,1:T(8,128)} %get-tuple-element.506) | copy-start | bytes 196612
  928.5 3.8 copy-start.8
  937.1 6.9 copy-start.1
  959.9 3.8 copy-start.8
  968.5 6.9 copy-start.1
  1098.3 286.2 %all-reduce.6.cloned.1.call-start = ((), (), s32[]{:S(2)}) async-start(), calls=%async_computation.1 | async-start | bytes 16777216
  1098.4 8.4 copy-start.12
  1118.7 4.2 copy-start.6
  1118.7 4.2 copy-start.30
  1118.7 4.2 copy-start.31
  1118.7 4.2 copy-start.32
  1118.7 4.2 copy-start.33
  1127.9 0.9 copy-start.23
  1127.9 1.0 copy-start.34
  1127.9 113.6 %copy-start.26 = (f32[4096]{0:T(1024)S(1)}, f32[4096]{0:T(1024)}, u32[]{:S(2)}) copy-start(f32[4096]{0:T(1024)} %param.36) | copy-start | bytes 49156
  (6 other events, 4.2 us)
Sparse Core Ops, SparseCore 0:
  1098.5 141.7 all-reduce.3
  1243.9 140.5 all-reduce.5
where the time goes:
time: 1400 us; the launch traced here: 1390 us
  waiting for transfers between devices  757 us (54%)
  blocking collectives  173 us (12%)
  local copies, waits for them, and re-layouts  155 us (11%)
  other arithmetic  145 us (10%)
  starting transfers between devices  85.6 us (6%)
  matrix products  53.5 us (4%)
  between operations  23.3 us (2%)
    ppermute x16, waiting for transfers between devices, from_behind(): return lax.ppermute(block, axis, route)  578 us
    psum x1, waiting for transfers between devices, body(): summed = lax.psum(partial_value, ('req', 'seq'))  111 us
    ppermute x16, starting transfers between devices, from_behind(): return lax.ppermute(block, axis, route)  85.5 us
    unnamed x3, waiting for transfers between devices  68.4 us
    pmax x1, blocking collectives, body(): top_all = lax.pmax(local_top, ('req', 'seq'))  66.5 us
    psum x1, blocking collectives, body(): group_rows = lax.psum(last_local.astype(jnp.bfloat16), 'seq')[None]  66 us
    add x15, other arithmetic, relay(): span_carry[:, None, None] * incoming + span_state  47.3 us
    dynamic_slice x18, local copies, waits for them, and re-layouts, body(): lax.map(local_pass, (block_inputs, state_inputs.reshape(count, BLOCK, HEA...  40.7 us
  transfers between devices with their start and end apart: 18, of which 17 were waited for; matrix products, arithmetic and copies ran while one was open for 5% of the time, Pallas kernels for 0%

commit v1 on v0

v1 whole, which is shorter than its diff:
```python
import functools

import jax
import jax.numpy as jnp
from jax import lax
from jax.experimental import pallas as pl
from jax.experimental.pallas import tpu as pltpu
from jax.sharding import PartitionSpec as P

D = 4096
HEADS = 64
CHANNEL_WIDTH = 64
GROUPS = 4
STATE = 128
KERNEL = 4
BLOCK = 256
SEQS = 4
PER_GROUP = HEADS // GROUPS
GW = PER_GROUP * CHANNEL_WIDTH
TINY_FLOOR = 1e-05
LOG2E = 1.4426950408889634
MESH = pl.DeviceIdType.MESH
F32 = jnp.float32
BF16 = jnp.bfloat16
VMEM_LIMIT = 60 * 1024 * 1024


def dot(a, b):
    return lax.dot_general(a, b, (((1,), (0,)), ((), ())), preferred_element_type=F32)


def dot_nt(a, b):
    return lax.dot_general(a, b, (((1,), (1,)), ((), ())), preferred_element_type=F32)


def split2(x):
    hi = x.astype(BF16)
    return hi, (x - hi.astype(F32)).astype(BF16)


def split3(x):
    hi = x.astype(BF16)
    rest = x - hi.astype(F32)
    mid = rest.astype(BF16)
    return hi, mid, (rest - mid.astype(F32)).astype(BF16)


def seg_of(place, b1, b2, b3):
    one = lambda b: (place >= b).astype(jnp.int32)
    return one(b1) + one(b2) + one(b3)


def spread_matrix():
    lane = lax.broadcasted_iota(jnp.int32, (128, GW), 0)
    col = lax.broadcasted_iota(jnp.int32, (128, GW), 1)
    hit = (lane < 48) & (lane % PER_GROUP == col // CHANNEL_WIDTH)
    return jnp.where(hit, 1.0, 0.0).astype(BF16)


def spread(v, spread_ref):
    hi, mid, lo = split3(v)
    lane = lax.broadcasted_iota(jnp.int32, v.shape, 1)
    parts = jnp.where(
        lane < 16, hi.astype(F32), jnp.where(lane < 32, mid.astype(F32), lo.astype(F32))
    ).astype(BF16)
    return dot(parts, spread_ref[...])


def silu(x):
    return x * jax.nn.sigmoid(x)


def local_kernel(
    meta,
    x_ref,
    b_ref,
    c_ref,
    xh_ref,
    bh_ref,
    ch_ref,
    wx_ref,
    wb_ref,
    wc_ref,
    vx_ref,
    vb_ref,
    vc_ref,
    dt_ref,
    dtt_ref,
    a_ref,
    at_ref,
    dx_ref,
    y_ref,
    st_ref,
    pt_ref,
    aux_ref,
    co_ref,
    ld_ref,
    xext,
    xf,
    s0,
    c0,
    cumr,
    sp,
):
    g = pl.program_id(0)
    j = pl.program_id(1)
    first = meta[0]
    b1, b2, b3 = meta[1], meta[2], meta[3]
    start = first + j * BLOCK

    @pl.when((g == 0) & (j == 0))
    def _():
        sp[...] = spread_matrix()

    @pl.when(j == 0)
    def _():
        xext[0:8, 0:GW] = xh_ref[...].astype(F32)
        xext[0:8, GW : GW + 128] = bh_ref[...].astype(F32)
        xext[0:8, GW + 128 : GW + 256] = ch_ref[...].astype(F32)
        pt_ref[...] = jnp.zeros_like(pt_ref)
        aux_ref[...] = jnp.zeros_like(aux_ref)

    @pl.when(j == 1)
    def _():
        xext[0:8, :] = xext[BLOCK : BLOCK + 8, :]

    xext[8 : BLOCK + 8, 0:GW] = x_ref[...].astype(F32)
    xext[8 : BLOCK + 8, GW : GW + 128] = b_ref[...].astype(F32)
    xext[8 : BLOCK + 8, GW + 128 : GW + 256] = c_ref[...].astype(F32)

    row = lax.broadcasted_iota(jnp.int32, (BLOCK, 128), 0) + start
    seg = seg_of(row, b1, b2, b3)
    same = [(seg_of(row - k, b1, b2, b3) == seg).astype(F32) for k in (3, 2, 1)]
    for c in range(10):
        cols = slice(c * 128, c * 128 + 128)
        w_ref, v_ref, lo = (
            (wx_ref, vx_ref, c * 128) if c < 8 else ((wb_ref, vb_ref, 0) if c == 8 else (wc_ref, vc_ref, 0))
        )
        part = slice(lo, lo + 128)
        total = jnp.broadcast_to(v_ref[0:1, part], (BLOCK, 128))
        for k in range(3):
            total = total + w_ref[k : k + 1, part] * xext[5 + k : 5 + k + BLOCK, cols] * same[k]
        total = total + w_ref[3:4, part] * xext[8 : 8 + BLOCK, cols]
        xf[:, cols] = silu(total)

    bf = xf[:, GW : GW + 128]
    cb = xf[:, GW + 128 : GW + 256].astype(BF16)
    co_ref[...] = cb

    i0 = lax.broadcasted_iota(jnp.int32, (BLOCK, BLOCK), 0)
    i1 = lax.broadcasted_iota(jnp.int32, (BLOCK, BLOCK), 1)
    tri = jnp.where(i0 >= i1, 1.0, 0.0).astype(BF16)
    triu = jnp.where(i0 <= i1, 1.0, 0.0).astype(BF16)
    dt = dt_ref[0, 0]
    dh, dm, dl = split3(dt * a_ref[0])
    cum = (dot(tri, dl) + dot(tri, dm)) + dot(tri, dh)
    logdt = jnp.log(dt) * LOG2E
    dtt = dtt_ref[0, 0]
    th, tm, tl = split3(dtt * at_ref[0])
    cumt = (dot(tl, triu) + dot(tm, triu)) + dot(th, triu)
    rt = jnp.log(dtt) * LOG2E - cumt
    cumr[...] = cum
    last = cum[BLOCK - 1 : BLOCK, :]

    seg_before_span = seg_of(first - 1, b1, b2, b3)
    seg_before = seg_of(start - 1, b1, b2, b3)
    seg_end = seg_of(start + BLOCK - 1, b1, b2, b3)

    @pl.when(j == 0)
    def _():
        c0[...] = jnp.zeros_like(c0)

    prior = c0[0:1, :]
    ld_ref[0, 0] = jnp.where(seg == seg_before_span, jnp.exp2(cum + prior), 0.0)

    bh, bl = split2(bf)
    sc = dot_nt(cb, bh)
    t_seg = seg_of(i0 + start, b1, b2, b3)
    s_seg = seg_of(i1 + start, b1, b2, b3)
    sc = jnp.where((i0 >= i1) & (t_seg == s_seg), sc, 0.0)

    @pl.when(j == 0)
    def _():
        y_ref[...] = jnp.zeros_like(y_ref)

    @pl.when(j == 1)
    def _():
        lead = jnp.where(seg == seg_before, jnp.exp2(cum), 0.0)
        sh, sl = split2(s0[...])
        y_ref[...] = spread(lead, sp) * (dot(cb, sh) + dot(cb, sl))

    lane = lax.broadcasted_iota(jnp.int32, (BLOCK, 128), 1)
    half = BLOCK // 2
    sc_t = sc[:half, :half]
    sc_l = sc[half:, :half]
    sc_r = sc[half:, half:]
    for pair in range(PER_GROUP // 2):
        cols = slice(pair * 128, pair * 128 + 128)
        xb = xf[:, cols].astype(BF16)
        res = []
        for h in (2 * pair, 2 * pair + 1):
            col = cum[:, h : h + 1]
            r = rt[h : h + 1, :]
            top = jnp.exp2(jnp.minimum(col[:half] + r[:, :half], 100.0)) * sc_t
            left = jnp.exp2(col[half:] + r[:, :half]) * sc_l
            right = jnp.exp2(jnp.minimum(col[half:] + r[:, half:], 100.0)) * sc_r
            bottom = jnp.concatenate([left.astype(BF16), right.astype(BF16)], axis=1)
            res.append(
                jnp.concatenate([dot(top.astype(BF16), xb[:half]), dot(bottom, xb)], axis=0)
            )
        intra = jnp.where(lane < CHANNEL_WIDTH, res[0], res[1])
        y_ref[:, cols] = y_ref[:, cols] + (intra + dx_ref[0:1, cols] * xb.astype(F32))

    bht, blt = split2(bf.T)

    def state_of(weights):
        xs = xf[:, 0:GW] * spread(weights, sp)
        xs_h, xs_l = split2(xs)
        return dot(bht, xs_h) + (dot(blt, xs_h) + dot(bht, xs_l))

    def at_end(seg_e):
        return jnp.where(seg == seg_e, jnp.exp2(last - cum + logdt), 0.0)

    own = state_of(at_end(seg_end))

    for r in range(SEQS - 1):
        end = meta[1 + r] - 1
        local = end - start
        owned = (local >= 0) & (local < BLOCK)

        @pl.when(owned)
        def _():
            ce = cumr[pl.ds(jnp.clip(local, 0, BLOCK - 1), 1), :]
            inside = (row <= end) & (seg == r)
            w = jnp.exp2(jnp.where(inside, ce - cum + logdt, -1e30))
            reach = jnp.where(seg_before == r, jnp.exp2(ce), 0.0)
            tail = state_of(w)
            keep = jnp.where(j == 1, 1.0, 0.0)
            reach8 = spread(jnp.broadcast_to(reach * keep, (8, 128)), sp)
            tail = tail + jnp.where(j == 1, reach8[0:1] * s0[...], 0.0)
            pt_ref[r] = tail.astype(BF16)
            full = jnp.where(seg_before_span == r, jnp.exp2(ce + prior), 0.0)
            aux_ref[1 + r : 2 + r, :] = spread(jnp.broadcast_to(full, (8, 128)), sp)[0:1]

    @pl.when(j == 0)
    def _():
        s0[...] = own
        c0[...] = jnp.broadcast_to(last, c0.shape)

    @pl.when(j == 1)
    def _():
        carry = jnp.where(seg_end == seg_before, jnp.exp2(last), 0.0)
        whole = jnp.where(seg_end == seg_before_span, jnp.exp2(last + prior), 0.0)
        carry8 = spread(jnp.broadcast_to(carry, (8, 128)), sp)
        whole8 = spread(jnp.broadcast_to(whole, (8, 128)), sp)
        st_ref[...] = (carry8[0:1] * s0[...] + own).astype(BF16)
        aux_ref[0:1, :] = whole8[0:1]


def local_pass(meta, conv, halo, conv_weight, conv_bias, dt, dtt, a, at, dx):
    length = conv.shape[0]
    blocks = length // BLOCK
    maps = D // 128
    grid = (GROUPS, blocks)
    xs = lambda rows: [
        pl.BlockSpec((rows, GW), lambda g, j: (0, g)),
        pl.BlockSpec((rows, 128), lambda g, j: (0, maps + g)),
        pl.BlockSpec((rows, 128), lambda g, j: (0, maps + GROUPS + g)),
    ]
    in_specs = (
        [
            pl.BlockSpec(memory_space=pltpu.SMEM),
            pl.BlockSpec((BLOCK, GW), lambda g, j: (j, g)),
            pl.BlockSpec((BLOCK, 128), lambda g, j: (j, maps + g)),
            pl.BlockSpec((BLOCK, 128), lambda g, j: (j, maps + GROUPS + g)),
        ]
        + xs(8)
        + xs(KERNEL)
        + xs(1)
        + [
            pl.BlockSpec((1, 1, BLOCK, 128), lambda g, j: (g, j, 0, 0)),
            pl.BlockSpec((1, 1, PER_GROUP, BLOCK), lambda g, j: (g, j, 0, 0)),
            pl.BlockSpec((1, 1, 128), lambda g, j: (g, 0, 0)),
            pl.BlockSpec((1, PER_GROUP, 1), lambda g, j: (g, 0, 0)),
            pl.BlockSpec((1, GW), lambda g, j: (0, g)),
        ]
    )
    out_specs = [
        pl.BlockSpec((BLOCK, GW), lambda g, j: (j, g)),
        pl.BlockSpec((STATE, GW), lambda g, j: (0, g)),
        pl.BlockSpec((SEQS - 1, STATE, GW), lambda g, j: (0, 0, g)),
        pl.BlockSpec((8, GW), lambda g, j: (0, g)),
        pl.BlockSpec((BLOCK, 128), lambda g, j: (j, g)),
        pl.BlockSpec((1, 1, BLOCK, 128), lambda g, j: (g, j, 0, 0)),
    ]
    out_shape = [
        jax.ShapeDtypeStruct((length, D), F32),
        jax.ShapeDtypeStruct((STATE, D), BF16),
        jax.ShapeDtypeStruct((SEQS - 1, STATE, D), BF16),
        jax.ShapeDtypeStruct((8, D), F32),
        jax.ShapeDtypeStruct((length, GROUPS * STATE), BF16),
        jax.ShapeDtypeStruct((GROUPS, blocks, BLOCK, 128), F32),
    ]
    return pl.pallas_call(
        local_kernel,
        grid=grid,
        in_specs=in_specs,
        out_specs=out_specs,
        out_shape=out_shape,
        scratch_shapes=[
            pltpu.VMEM((BLOCK + 8, GW + 256), F32),
            pltpu.VMEM((BLOCK, GW + 256), F32),
            pltpu.VMEM((STATE, GW), F32),
            pltpu.VMEM((8, 128), F32),
            pltpu.VMEM((BLOCK, 128), F32),
            pltpu.VMEM((128, GW), BF16),
        ],
        compiler_params=pltpu.CompilerParams(
            vmem_limit_bytes=VMEM_LIMIT, dimension_semantics=("arbitrary", "arbitrary")
        ),
        name="local_pass",
    )(
        meta, conv, conv, conv, halo, halo, halo, conv_weight, conv_weight, conv_weight,
        conv_bias, conv_bias, conv_bias, dt, dtt, a, at, dx,
    )


def exchange_kernel(
    n,
    st_ref,
    aux_ref,
    ent_ref,
    fin_ref,
    rs,
    ra,
    eb,
    send1,
    recv1,
    send2,
    recv2,
    send3,
    recv3,
):
    me = lax.axis_index("seq")
    width = D // n
    barrier = pltpu.get_barrier_semaphore()

    def peer(i):
        return lax.rem(me + i, n)

    def cols(p):
        return pl.ds(pl.multiple_of(p * width, width), width)

    def greet(i, _):
        pl.semaphore_signal(barrier, inc=1, device_id={"seq": peer(i)}, device_id_type=MESH)
        return 0

    lax.fori_loop(1, n, greet, 0)
    pl.semaphore_wait(barrier, n - 1)

    def out(p, slot):
        return (
            pltpu.make_async_remote_copy(
                src_ref=st_ref.at[:, cols(p)],
                dst_ref=rs.at[slot],
                send_sem=send1.at[p],
                recv_sem=recv1.at[slot],
                device_id={"seq": p},
                device_id_type=MESH,
            ),
            pltpu.make_async_remote_copy(
                src_ref=aux_ref.at[:, cols(p)],
                dst_ref=ra.at[slot],
                send_sem=send2.at[p],
                recv_sem=recv2.at[slot],
                device_id={"seq": p},
                device_id_type=MESH,
            ),
        )

    def back(p, slot):
        return pltpu.make_async_remote_copy(
            src_ref=eb.at[p],
            dst_ref=ent_ref.at[:, cols(slot)],
            send_sem=send3.at[p],
            recv_sem=recv3.at[slot],
            device_id={"seq": p},
            device_id_type=MESH,
        )

    def begin(i, _):
        for copy in out(peer(i), me):
            copy.start()
        return 0

    lax.fori_loop(1, n, begin, 0)
    rs[me] = st_ref[:, cols(me)]
    ra[me] = aux_ref[:, cols(me)]

    def arrive(i, _):
        for copy in out(peer(i), peer(i)):
            copy.wait_recv()
        return 0

    lax.fori_loop(1, n, arrive, 0)

    fin_ref[...] = jnp.zeros_like(fin_ref)

    def scan(d, _):
        now = fin_ref[SEQS - 1]
        eb[d] = now.astype(BF16)
        for r in range(SEQS - 1):
            fin_ref[r] = fin_ref[r] + ra[d, 1 + r : 2 + r, :] * now
        fin_ref[SEQS - 1] = ra[d, 0:1, :] * now + rs[d].astype(F32)
        return 0

    lax.fori_loop(0, n, scan, 0)

    def reply(i, _):
        back(peer(i), me).start()
        return 0

    lax.fori_loop(1, n, reply, 0)
    ent_ref[:, cols(me)] = eb[me]

    def done(i, _):
        back(peer(i), peer(i)).wait_recv()
        return 0

    lax.fori_loop(1, n, done, 0)

    def drain(i, _):
        for copy in out(peer(i), me):
            copy.wait_send()
        back(peer(i), me).wait_send()
        return 0

    lax.fori_loop(1, n, drain, 0)


def exchange(states, aux, n):
    width = D // n
    vmem = pl.BlockSpec(memory_space=pltpu.VMEM)
    return pl.pallas_call(
        functools.partial(exchange_kernel, n),
        in_specs=[vmem, vmem],
        out_specs=[vmem, vmem],
        out_shape=[
            jax.ShapeDtypeStruct((STATE, D), BF16),
            jax.ShapeDtypeStruct((SEQS, STATE, width), F32),
        ],
        scratch_shapes=[
            pltpu.VMEM((n, STATE, width), BF16),
            pltpu.VMEM((n, 8, width), F32),
            pltpu.VMEM((n, STATE, width), BF16),
        ]
        + [pltpu.SemaphoreType.DMA((n,)) for _ in range(6)],
        compiler_params=pltpu.CompilerParams(
            collective_id=0, has_side_effects=True, vmem_limit_bytes=VMEM_LIMIT
        ),
        name="exchange",
    )(states, aux)


def finish_kernel(y_ref, c_ref, e_ref, ld_ref, gate_ref, nw_ref, out_ref, sp):
    @pl.when((pl.program_id(0) == 0) & (pl.program_id(1) == 0))
    def _():
        sp[...] = spread_matrix()

    v = y_ref[...] + spread(ld_ref[0, 0], sp) * dot(c_ref[...], e_ref[...])
    v = v * silu(gate_ref[...].astype(F32))
    scale = lax.rsqrt(jnp.mean(v * v, axis=1, keepdims=True) + TINY_FLOOR)
    out_ref[...] = (v * scale * nw_ref[...]).astype(BF16)


def finish(y, c, entering, lead, gate, norm_weight):
    length = y.shape[0]
    block = lambda width: pl.BlockSpec((BLOCK, width), lambda g, j: (j, g))
    return pl.pallas_call(
        finish_kernel,
        grid=(GROUPS, length // BLOCK),
        in_specs=[
            block(GW),
            block(STATE),
            pl.BlockSpec((STATE, GW), lambda g, j: (0, g)),
            pl.BlockSpec((1, 1, BLOCK, 128), lambda g, j: (g, j, 0, 0)),
            block(GW),
            pl.BlockSpec((1, GW), lambda g, j: (0, g)),
        ],
        out_specs=block(GW),
        out_shape=jax.ShapeDtypeStruct((length, D), BF16),
        scratch_shapes=[pltpu.VMEM((128, GW), BF16)],
        compiler_params=pltpu.CompilerParams(
            vmem_limit_bytes=VMEM_LIMIT, dimension_semantics=("arbitrary", "arbitrary")
        ),
        name="finish",
    )(y, c, entering, lead, gate, norm_weight)


def body(
    conv_input,
    gate_projected,
    step_raw,
    step_bias,
    decay_log,
    head_direct_gain,
    conv_weight,
    convolution_bias,
    norm_weight,
    lengths,
    out_weight,
    residual_last,
    final_gain,
    vocab_weight,
):
    local_len = conv_input.shape[1]
    inner = HEADS * CHANNEL_WIDTH
    count = local_len // BLOCK
    seq_count = lax.axis_size("seq")
    seq_place = lax.axis_index("seq")
    req_place = lax.axis_index("req")
    first = seq_place * local_len
    conv = conv_input[0]
    route = [(i, i + 1) for i in range(seq_count - 1)]
    halo = lax.ppermute(conv[local_len - 8 :], "seq", route)
    bounds = jnp.cumsum(lengths[0]).astype(jnp.int32)
    meta = jnp.concatenate([first.astype(jnp.int32)[None], bounds])

    step = jax.nn.softplus(step_raw[0] + step_bias)
    step = step.reshape(count, BLOCK, GROUPS, PER_GROUP)
    dt = jnp.tile(step.transpose(2, 0, 1, 3), (1, 1, 1, 128 // PER_GROUP))
    dtt = step.transpose(2, 0, 3, 1)
    rate = (-jnp.exp(decay_log) * LOG2E).reshape(GROUPS, PER_GROUP)
    a = jnp.tile(rate, (1, 128 // PER_GROUP))[:, None, :]
    at = rate[:, :, None]
    dx = jnp.repeat(head_direct_gain, CHANNEL_WIDTH)[None]

    y, states, tails, aux, c, lead = local_pass(
        meta, conv, halo, conv_weight, convolution_bias[None], dt, dtt, a, at, dx
    )
    tail_share = lax.psum_scatter(tails, "seq", scatter_dimension=2, tiled=True)
    entering, reached = exchange(states, aux, seq_count)
    gated = finish(y, c, entering, lead, gate_projected[0], norm_weight[None])

    final = jnp.concatenate(
        [reached[: SEQS - 1] + tail_share.astype(F32), reached[SEQS - 1 :]], axis=0
    )
    final_states = final.reshape(SEQS, STATE, HEADS // seq_count, CHANNEL_WIDTH)
    final_states = final_states.transpose(0, 2, 3, 1)[None]

    lasts = []
    for request in range(SEQS):
        local_end = bounds[request] - 1 - first
        owned = (local_end >= 0) & (local_end < local_len)
        spot = jnp.clip(local_end, 0, local_len - 1)
        lasts.append(jnp.where(owned, gated[spot].astype(jnp.float32), 0.0))
    last_local = jnp.stack(lasts)
    rows_total = residual_last.shape[0]
    group_rows = lax.psum(last_local.astype(jnp.bfloat16), "seq")[None]
    all_rows = lax.all_gather(group_rows, "req", axis=0, tiled=True)
    share = out_weight.shape[0]
    flat_place = req_place * seq_count + seq_place
    columns = lax.dynamic_slice_in_dim(all_rows.reshape(-1, inner), flat_place * share, share, 1)
    partial_value = jnp.dot(columns, out_weight, preferred_element_type=jnp.float32)
    summed = lax.psum(partial_value, ("req", "seq"))
    hidden = residual_last.reshape(-1, D).astype(jnp.float32) + summed
    last_hidden = hidden.astype(jnp.bfloat16).reshape(rows_total, SEQS, D)
    own_hidden = lax.dynamic_slice_in_dim(last_hidden, req_place, 1, 0)
    scale = lax.rsqrt(jnp.mean(hidden * hidden, axis=-1, keepdims=True) + TINY_FLOOR)
    normed = (hidden * scale * final_gain).astype(jnp.bfloat16)
    logits = lax.dot_general(
        normed, vocab_weight, (((1,), (1,)), ((), ())), preferred_element_type=jnp.float32
    )
    local_top = jnp.max(logits, axis=1)
    top_all = lax.pmax(local_top, ("req", "seq"))
    max_logit = lax.dynamic_slice_in_dim(top_all.reshape(rows_total, SEQS), req_place, 1, 0)
    return (gated[None], final_states, own_hidden, max_logit)


def solution(mesh):
    return jax.shard_map(
        body,
        mesh=mesh,
        in_specs=(
            P("req", "seq", None),
            P("req", "seq", None),
            P("req", "seq", None),
            P(),
            P(),
            P(),
            P(),
            P(),
            P(),
            P("req", None),
            P(("req", "seq"), None),
            P(),
            P(),
            P(("req", "seq"), None),
        ),
        out_specs=(
            P("req", "seq", None),
            P("req", None, "seq", None, None),
            P("req", None, None),
            P("req", None),
        ),
        check_vma=False,
    )
```

time: 1400 us -> 431 us (0.31)
  waiting for transfers between devices: 757 us -> 142 us
  local copies, waits for them, and re-layouts: 155 us -> 10.8 us
  other arithmetic: 145 us -> 6.37 us
  Pallas kernels: 0 us -> 90.2 us
  starting transfers between devices: 85.6 us -> 4.43 us
  matrix products: 53.5 us -> 7.17 us
  blocking collectives: 173 us -> 150 us
    ppermute x16 -> x1, waiting for transfers between devices: 578 us -> 0.01 us  [body(): halo = lax.ppermute(conv[local_len - 8:], 'seq', route)]
    pallas_call x0 -> x3, Pallas kernels: none -> 90.2 us  [the longest x1 44.1 us: exchange(): pl.pallas_call(functools.partial(exchange_kernel, n), in_specs=[vmem, vme...]
    ppermute x16 -> x1, starting transfers between devices: 85.5 us -> 4.35 us  [body(): halo = lax.ppermute(conv[local_len - 8:], 'seq', route)]
    unnamed x3 -> x2, waiting for transfers between devices: 68.4 us -> 0.54 us
    dynamic_slice x26 -> x0, local copies, waits for them, and re-layouts: 55.8 us -> none  [the longest x18 40.7 us: body(): lax.map(local_pass, (block_inputs, state_inputs.reshape(count, BLOCK, HEA...]
    add x21 -> x1, other arithmetic: 51.9 us -> 0.96 us  [body(): reached[:SEQS - 1] + tail_share.astype(F32)]
    dot_general x12 -> x0, matrix products: 46.3 us -> none  [the longest x4 15.9 us: state_at(): jnp.einsum('sgjp,sgn->gjpn', scaled.reshape(length, GROUPS, per_group, CH...]
    convert_element_type x8 -> x0, other arithmetic: 41.5 us -> none  [the longest x1 19.7 us: body(): mixed = mixed_full.astype(jnp.bfloat16)]
  transfers between devices with their start and end apart: 18 -> 3, of which waited for: 17 -> 1; matrix products, arithmetic and copies ran while one was open for 5% -> 4% of each run, Pallas kernels for 0% -> 0%
where the time goes in v1:
time: 431 us; the launch traced here: 430 us
  blocking collectives  150 us (35%)
  waiting for transfers between devices  142 us (33%)
  Pallas kernels  90.2 us (21%)
  between operations  18.3 us (4%)
  local copies, waits for them, and re-layouts  10.8 us (3%)
  matrix products  7.17 us (2%)
  other arithmetic  6.37 us (1%)
  starting transfers between devices  4.43 us (1%)
    psum x1, waiting for transfers between devices, body(): summed = lax.psum(partial_value, ('req', 'seq'))  142 us
    pmax x1, blocking collectives, body(): top_all = lax.pmax(local_top, ('req', 'seq'))  63.9 us
    psum x1, blocking collectives, body(): group_rows = lax.psum(last_local.astype(jnp.bfloat16), 'seq')[None]  58 us
    pallas_call x1, Pallas kernels, exchange(): pl.pallas_call(functools.partial(exchange_kernel, n), in_specs=[vmem, vme...  44.1 us
    pallas_call x1, Pallas kernels, local_pass(): pl.pallas_call(local_kernel, grid=grid, in_specs=in_specs, out_specs=out_...  34.4 us
    all_gather x1, blocking collectives, body(): all_rows = lax.all_gather(group_rows, 'req', axis=0, tiled=True)  28.6 us
    pallas_call x1, Pallas kernels, finish(): pl.pallas_call(finish_kernel, grid=(GROUPS, length // BLOCK), in_specs=[b...  11.7 us
  transfers between devices with their start and end apart: 3, of which 1 were waited for; matrix products, arithmetic and copies ran while one was open for 4% of the time, Pallas kernels for 0%

profile of v1, /device:TPU:1, one launch (start us, length us, event | category | flops | bytes accessed | tf_op | source)
XLA Modules:
  0.0 430.0 jit_solution(13777349518399307680)
XLA Ops:
  8.0 0.0 copy-start
  8.0 0.0 all-reduce.2.cloned.1.call-start
  8.1 0.9 slice_bitcast_fusion
  9.0 4.4 %collective-permute-start = (bf16[8,5120]{1,0:T(8,128)(2,1)S(1)}, bf16[8,5120]{1,0:T(8,128)(2,1)S(1)}, u32[]{:S(2)}, u32[]{:S(2)}) collective-permute-start(bf16[8,5120]{1,0:T(8,128)(2,1)S(1)} %slice_bitcast_fusion), channel_id=1, source_target_pairs={{0,1},{1,2},{2,3},{3,4},{4,5},{5,6},{6,7},{7,8},{8,9},{9,10},{10,1... | collective-permute-start | bytes 245768 | tf_op jit(solution)/shard_map/ppermute | solution.py:525
  13.3 0.8 reduce-window.4
  14.2 0.7 fusion.11
  17.5 0.7 negate_multiply_fusion
  18.2 0.1 tile.20
  18.3 0.8 broadcast_in_dim_reshape.8.at_ref
  19.0 0.7 add.61
  19.8 0.7 tile.22.a_ref
  20.5 0.7 broadcast_in_dim.33
  21.2 0.7 broadcast_in_dim_reshape.7.dx_ref
  21.9 1.0 squeeze.7
  22.9 0.8 fusion.2
  23.7 0.1 tile.18
  23.8 1.3 copy.26.dt_ref
  25.1 0.7 pad_add_fusion.meta
  25.8 0.0 collective-permute-done.xh_ref.bh_ref.ch_ref
  25.8 0.0 copy-start.1
  25.8 0.6 copy-done.1
  26.4 34.4 %local_pass.1 = (f32[512,4096]{1,0:T(8,128)}, bf16[128,4096]{1,0:T(8,128)(2,1)}, bf16[3,128,4096]{2,1,0:T(8,128)(2,1)}, f32[8,4096]{1,0:T(8,128)}, bf16[512,512]{1,0:T(8,128)(2,1)}, /*index=5*/f32[4,2,256,128]{3,2,1,0:T(8,128)}) custom-call(s32[5]{0:T(128)} %pad_add_fusion.meta, bf16[512,5120]{1,0:T(8,128)(2,1)} %bitcast.30, bf16[512,5120]{1,0:T(8,128)(2,1)} %bitcast.31, ...), custom_call_target="tpu_custom_call" | custom-call | tf_op jit(solution)/shard_map/local_pass/pallas_call | solution.py:304
  60.8 44.1 %exchange.1 = (bf16[128,4096]{1,0:T(8,128)(2,1)}, f32[4,128,256]{2,1,0:T(8,128)}) custom-call(bf16[128,4096]{1,0:T(8,128)(2,1)} %get-tuple-element.14.st_ref, f32[8,4096]{1,0:T(8,128)} %get-tuple-element.15.aux_ref), custom_call_target="tpu_custom_call" | custom-call | tf_op jit(solution)/shard_map/exchange/pallas_call | solution.py:444
  104.9 11.7 %finish.1 = bf16[512,4096]{1,0:T(8,128)(2,1)} custom-call(f32[512,4096]{1,0:T(8,128)} %get-tuple-element.12.y_ref, bf16[512,512]{1,0:T(8,128)(2,1)} %get-tuple-element.13.c_ref, bf16[128,4096]{1,0:T(8,128)(2,1)} %get-tuple-element.16.e_ref, f32[4,2,256,128]{3,2,1,0:T(8,128)} %get-tuple-element.17.ld_ref, bf16[512,4096]{1,0:T(8,128)(2,1)} %bitcast.35, ...), custom_call_target="tpu_custom_call" | custom-call | tf_op jit(solution)/shard_map/finish/pallas_call | solution.py:479
  116.6 0.0 copy-start.3
  116.6 0.0 copy-start.4
  116.6 1.1 fusion.4
  117.7 0.1 maximum_bitcast_fusion
  117.8 58.0 %psum.14 = bf16[1,4,4096]{2,1,0:T(4,128)(2,1)S(1)} all-reduce(bf16[1,4,4096]{2,1,0:T(4,128)(2,1)S(1)} %maximum_bitcast_fusion), channel_id=1, replica_groups=mesh['req'=8,'seq'=16] {'seq'}, use_global_device_ids=true, to_apply=%region_2.3 | all-reduce | flops 16384 | bytes 65536 | tf_op jit(solution)/shard_map/psum | solution.py:559
  175.9 28.6 %all_gather.3 = bf16[8,4,4096]{2,1,0:T(4,128)(2,1)S(1)} all-gather(bf16[1,4,4096]{2,1,0:T(4,128)(2,1)S(1)} %psum.14), channel_id=1, replica_groups=mesh['req'=8,'seq'=16] {'req'}, dimensions={0}, use_global_device_ids=true | all-gather | bytes 294912 | tf_op jit(solution)/shard_map/all_gather | solution.py:560
  204.4 0.1 reshape.77
  204.5 0.0 copy-done
  204.5 1.1 fusion.8
  205.6 0.0 all-reduce.2.cloned.1.call-update
  205.6 0.0 reduce-scatter.2.cloned.1.call-start
  205.7 0.5 reduce-scatter.2.cloned.1.call-update
  206.2 0.0 copy-done.3
  206.2 0.0 copy-start.2
  206.2 141.7 %all-reduce.2.cloned.1.call-done = f32[32,4096]{1,0:T(8,128)} async-done(((f32[32,4096]{1,0:T(8,128)}), f32[32,4096]{1,0:T(8,128)}) %all-reduce.2.cloned.1.call-update) | async-done | bytes 524304 | tf_op jit(solution)/shard_map/psum | solution.py:565
  347.9 1.2 multiply_reduce_fusion
  349.2 0.0 copy-done.4
  349.2 6.1 %convolution_reduce_fusion = f32[32]{0:T(128)S(1)} fusion(bf16[1024,4096]{1,0:T(8,128)(2,1)} %param.27, f32[32,4096]{1,0:T(8,128)S(1)} %get-tuple-element.21, f32[4096]{0:T(1024)S(1)} %copy-done.4, f32[32]{0:T(128)S(1)} %add_rsqrt_fusion), kind=kOutput, calls=%fused_computation | convolution fusion | flops 268861408 | bytes 8929536 | tf_op jit(solution)/shard_map/dot_general | solution.py:571
  355.3 0.1 reshape.79
  355.3 0.0 copy-done.2
  355.4 63.9 %pmax.7 = f32[8,4]{1,0:T(8,128)S(1)} all-reduce(f32[8,4]{1,0:T(8,128)S(1)} %reshape.79), channel_id=1, replica_groups=mesh['req'=8,'seq'=16] {'req','seq'}, use_global_device_ids=true, to_apply=%region_6.7 | all-reduce | flops 32 | bytes 256 | tf_op jit(solution)/shard_map/pmax | solution.py:575
  419.3 0.1 reshape.78
  419.4 0.5 constant_dynamic-slice_fusion
  419.9 0.6 constant_dynamic-slice_fusion.1
  420.6 0.0 reduce-scatter.2.cloned.1.call-done
  420.6 1.0 convert_add_fusion
  421.6 1.0 copy.28
  (6 shorter events, 0.1 us)
Async XLA Ops:
  8.0 196.5 %copy-start = (bf16[32,4096]{1,0:T(8,128)(2,1)S(1)}, bf16[32,4096]{1,0:T(8,128)(2,1)}, u32[]{:S(2)}) copy-start(bf16[32,4096]{1,0:T(8,128)(2,1)} %param.24) | copy-start | bytes 786436
  8.0 339.9 %all-reduce.2.cloned.1.call-start = ((), (), s32[]{:S(2)}) async-start(), calls=%async_computation.2 | async-start | bytes 1048576 | tf_op jit(solution)/shard_map/psum | solution.py:565
  9.0 16.8 %collective-permute-start = (bf16[8,5120]{1,0:T(8,128)(2,1)S(1)}, bf16[8,5120]{1,0:T(8,128)(2,1)S(1)}, u32[]{:S(2)}, u32[]{:S(2)}) collective-permute-start(bf16[8,5120]{1,0:T(8,128)(2,1)S(1)} %slice_bitcast_fusion), channel_id=1, source_target_pairs={{0,1},{1,2},{2,3},{3,4},{4,5},{5,6},{6,7},{7,8},{8,9},{9,10},{10,1... | collective-permute-start | bytes 245768 | tf_op jit(solution)/shard_map/ppermute | solution.py:525
  25.8 0.6 copy-start.1
  116.6 89.5 %copy-start.3 = (bf16[8,4,4096]{2,1,0:T(4,128)(2,1)S(1)}, bf16[8,4,4096]{2,1,0:T(4,128)(2,1)}, u32[]{:S(2)}) copy-start(bf16[8,4,4096]{2,1,0:T(4,128)(2,1)} %param.25) | copy-start | bytes 786436
  116.6 232.5 %copy-start.4 = (f32[4096]{0:T(1024)S(1)}, f32[4096]{0:T(1024)}, u32[]{:S(2)}) copy-start(f32[4096]{0:T(1024)} %param.26) | copy-start | bytes 49156
  205.6 214.9 %reduce-scatter.2.cloned.1.call-start = ((), (), s32[]{:S(2)}) async-start(), calls=%async_computation.1 | async-start | bytes 3342336 | tf_op jit(solution)/shard_map/reduce_scatter | solution.py:541
  206.2 149.1 %copy-start.2 = (f32[4,128,256]{2,1,0:T(8,128)S(1)}, f32[4,128,256]{2,1,0:T(8,128)}, u32[]{:S(2)}) copy-start(f32[4,128,256]{2,1,0:T(8,128)} %get-tuple-element.18) | copy-start | bytes 1572868
Sparse Core Ops, SparseCore 0:
  205.7 142.1 all-reduce.1
Sparse Core Ops, SparseCore 1:
  209.4 69.3 reduce-scatter.1

commit v2 on v1

--- a/solution.py
+++ b/solution.py
@@ -497,6 +497,345 @@
     )(y, c, entering, lead, gate, norm_weight)
 
 
+def tail_kernel(
+    n,
+    m,
+    rows_ref,
+    w_ref,
+    tails_ref,
+    reach_ref,
+    resid_ref,
+    gain_ref,
+    vocab_ref,
+    hid_ref,
+    max_ref,
+    fin_ref,
+    vbuf,
+    rrecv,
+    ragg,
+    wbuf,
+    part,
+    precv,
+    h1,
+    h2,
+    hf,
+    mx1,
+    mx2,
+    trecv,
+    vsem,
+    rs_s,
+    rs_r,
+    ag_s,
+    ag_r,
+    w_s,
+    w_r,
+    pt_s,
+    pt_r,
+    h1_s,
+    h1_r,
+    h2_s,
+    h2_r,
+    m1_s,
+    m1_r,
+    m2_s,
+    m2_r,
+    t_s,
+    t_r,
+):
+    s = lax.axis_index("seq")
+    b = lax.axis_index("req")
+    width = D // n
+    depth = D // m
+    w_place = 2 * b + s // 8
+    w_slot = lax.rem(s, 8)
+    to_self = w_place == s
+    from_b = s // 2
+    from_s = 8 * lax.rem(s, 2)
+
+    load = pltpu.make_async_copy(vocab_ref, vbuf, vsem)
+    load.start()
+
+    barrier = pltpu.get_barrier_semaphore()
+
+    def signal(where):
+        pl.semaphore_signal(barrier, inc=1, device_id=where, device_id_type=MESH)
+
+    def seq_peer(i):
+        return lax.rem(s + i, n)
+
+    def req_peer(i):
+        return lax.rem(b + i, m)
+
+    def greet_seq(i, _):
+        signal({"seq": seq_peer(i)})
+        return 0
+
+    def greet_req(i, _):
+        signal({"req": req_peer(i)})
+        return 0
+
+    def greet_w(i, _):
+        @pl.when(jnp.logical_not(to_self & (i == b)))
+        def _():
+            signal({"req": i, "seq": w_place})
+
+        @pl.when(jnp.logical_not((from_b == b) & (from_s + i == s)))
+        def _():
+            signal({"req": from_b, "seq": from_s + i})
+
+        return 0
+
+    lax.fori_loop(1, n, greet_seq, 0)
+    lax.fori_loop(1, m, greet_req, 0)
+    lax.fori_loop(0, m, greet_w, 0)
+    pl.semaphore_wait(barrier, (n - 1) + (m - 1) + 2 * m - 2 * to_self.astype(jnp.int32))
+
+    def remote(src, dst, send, recv, where):
+        return pltpu.make_async_remote_copy(
+            src_ref=src, dst_ref=dst, send_sem=send, recv_sem=recv, device_id=where, device_id_type=MESH
+        )
+
+    def over(count, peer, copy, me):
+        def start(i, _):
+            copy(peer(i), me).start()
+            return 0
+
+        def arrive(i, _):
+            copy(peer(i), peer(i)).wait_recv()
+            return 0
+
+        def drain(i, _):
+            copy(peer(i), me).wait_send()
+            return 0
+
+        return (
+            lambda: lax.fori_loop(1, count, start, 0),
+            lambda: lax.fori_loop(1, count, arrive, 0),
+            lambda: lax.fori_loop(1, count, drain, 0),
+        )
+
+    def rows_copy(p, slot):
+        return remote(rows_ref.at[p], rrecv.at[slot], rs_s.at[p], rs_r.at[slot], {"seq": p})
+
+    def gather_copy(p, slot):
+        return remote(ragg.at[b], ragg.at[slot], ag_s.at[p], ag_r.at[slot], {"req": p})
+
+    def part_copy(p, slot):
+        cols = pl.ds(pl.multiple_of(lax.rem(p, 2) * 256, 256), 256)
+        return remote(part.at[p // 2, :, cols], precv.at[slot], pt_s.at[p], pt_r.at[slot], {"seq": p})
+
+    def h1_copy(p, slot):
+        return remote(h1.at[b], h1.at[slot], h1_s.at[p], h1_r.at[slot], {"req": p})
+
+    def h2_copy(p, slot):
+        return remote(h1, h2.at[slot // 2, lax.rem(slot, 2)], h2_s.at[p], h2_r.at[slot], {"seq": p})
+
+    def m1_copy(p, slot):
+        return remote(mx1.at[b], mx1.at[slot], m1_s.at[p], m1_r.at[slot], {"req": p})
+
+    def m2_copy(p, slot):
+        return remote(mx2.at[s], mx2.at[slot], m2_s.at[p], m2_r.at[slot], {"seq": p})
+
+    def t_copy(p, slot, r):
+        cols = pl.ds(pl.multiple_of(p * width, width), width)
+        return remote(tails_ref.at[r, :, cols], trecv.at[slot, r], t_s.at[p, r], t_r.at[slot, r], {"seq": p})
+
+    def send_tails(lo, hi):
+        def start(i, _):
+            for r in range(SEQS - 1):
+                t_copy(seq_peer(i), s, r).start()
+            return 0
+
+        lax.fori_loop(lo, hi, start, 0)
+
+    rows_go, rows_in, rows_out = over(n, seq_peer, rows_copy, s)
+    ag_go, ag_in, ag_out = over(m, req_peer, gather_copy, b)
+    part_go, part_in, part_out = over(n, seq_peer, part_copy, s)
+    h1_go, h1_in, h1_out = over(m, req_peer, h1_copy, b)
+    h2_go, h2_in, h2_out = over(n, seq_peer, h2_copy, s)
+    m1_go, m1_in, m1_out = over(m, req_peer, m1_copy, b)
+    m2_go, m2_in, m2_out = over(n, seq_peer, m2_copy, s)
+
+    rows_go()
+
+    def w_copy(p):
+        cols = pl.ds(pl.multiple_of(p * depth, depth), depth)
+        return remote(
+            w_ref.at[:, cols], wbuf.at[w_slot], w_s.at[p], w_r.at[w_slot], {"req": p, "seq": w_place}
+        )
+
+    def w_start(i, _):
+        p = lax.rem(b + i, m)
+
+        @pl.when(jnp.logical_not(to_self & (p == b)))
+        def _():
+            w_copy(p).start()
+
+        return 0
+
+    lax.fori_loop(0, m, w_start, 0)
+
+    @pl.when(to_self)
+    def _():
+        wbuf[w_slot] = w_ref[:, pl.ds(pl.multiple_of(b * depth, depth), depth)]
+
+    rrecv[s] = rows_ref[s]
+    send_tails(1, 3)
+    rows_in()
+    ragg[b] = jnp.sum(rrecv[...], axis=0)
+    ag_go()
+    send_tails(3, 4)
+    ag_in()
+
+    def w_arrive(i, _):
+        @pl.when(jnp.logical_not((from_b == b) & (from_s + i == s)))
+        def _():
+            remote(
+                w_ref.at[:, pl.ds(0, depth)], wbuf.at[i], w_s.at[i], w_r.at[i], {"req": i, "seq": w_place}
+            ).wait_recv()
+
+        return 0
+
+    lax.fori_loop(0, m, w_arrive, 0)
+
+    lhs = ragg[...].reshape(8 * m, 128).astype(BF16)
+    weights = wbuf[...].reshape(m * 32, depth)
+    place = lax.broadcasted_iota(jnp.int32, (8 * m, depth), 0)
+    both = jnp.where(place % 8 < 4, dot(lhs, weights[0:128]), dot(lhs, weights[128:256]))
+    both = both + pltpu.roll(both, 4, 0)
+    part[...] = both.reshape(m, 8, depth)
+    part_go()
+    precv[s] = part[s // 2, :, pl.ds(pl.multiple_of(lax.rem(s, 2) * 256, 256), 256)]
+    send_tails(4, 8)
+    part_in()
+    hidden = jnp.sum(precv[...], axis=0) + resid_ref[...].astype(F32)
+    upper = pltpu.roll(hidden[:, 128:256], 4, 0)
+    eight = lax.broadcasted_iota(jnp.int32, (8, 128), 0)
+    h1[b] = jnp.where(eight < 4, upper, hidden[:, 0:128]).astype(BF16)
+    h1_go()
+    send_tails(8, 9)
+    h1_in()
+    h2_go()
+    h2[s // 2, lax.rem(s, 2)] = h1[...]
+    send_tails(9, n)
+    h2_in()
+
+    for k in range(m):
+        for q in range(2):
+            piece = h2[:, q, k].astype(F32).reshape(8 * m, 128)
+            lo = k * depth + q * 256
+            hf[:, lo : lo + 128] = piece
+            hf[:, lo + 128 : lo + 256] = pltpu.roll(piece, 4, 0)
+    h = hf[...]
+    hid_ref[...] = hf[pl.ds(pl.multiple_of(b * 8, 8), 8), :].astype(BF16)
+    scale = lax.rsqrt(jnp.mean(h * h, axis=1, keepdims=True) + TINY_FLOOR)
+    normed = (h * scale * gain_ref[...]).astype(BF16)
+    load.wait()
+    top = jnp.full((1, 8 * m), -jnp.inf, F32)
+    chunk = 256
+    for k in range(vbuf.shape[0] // chunk):
+        logits = dot_nt(vbuf[k * chunk : (k + 1) * chunk, :], normed)
+        top = jnp.maximum(top, jnp.max(logits, axis=0, keepdims=True))
+    top = jnp.concatenate([top, top], axis=1)
+    mx1[b] = jnp.broadcast_to(top, (8, 128))
+    m1_go()
+    m1_in()
+    mx2[s] = jnp.max(mx1[...], axis=0)
+    m2_go()
+
+    def t_arrive(i, _):
+        for r in range(SEQS - 1):
+            t_copy(seq_peer(i), seq_peer(i), r).wait_recv()
+        return 0
+
+    lax.fori_loop(1, n, t_arrive, 0)
+    trecv[s] = tails_ref[:, :, pl.ds(pl.multiple_of(s * width, width), width)]
+
+    def collect(r, _):
+        total = reach_ref[r]
+        for d in range(n):
+            total = total + trecv[d, r].astype(F32)
+        fin_ref[r] = total.T
+        return 0
+
+    lax.fori_loop(0, SEQS - 1, collect, 0)
+    fin_ref[SEQS - 1] = reach_ref[SEQS - 1].T
+    m2_in()
+    max_ref[...] = jnp.max(mx2[...], axis=0)
+
+    for drain in (rows_out, ag_out, part_out, h1_out, h2_out, m1_out, m2_out):
+        drain()
+
+    def w_drain(p, _):
+        @pl.when(jnp.logical_not(to_self & (p == b)))
+        def _():
+            w_copy(p).wait_send()
+
+        return 0
+
+    lax.fori_loop(0, m, w_drain, 0)
+
+    def t_drain(i, _):
+        for r in range(SEQS - 1):
+            t_copy(seq_peer(i), s, r).wait_send()
+        return 0
+
+    lax.fori_loop(1, n, t_drain, 0)
+
+
+def tail(rows, out_weight, tails, reached, resid, gain, vocab, n, m):
+    width = D // n
+    vmem = pl.BlockSpec(memory_space=pltpu.VMEM)
+    dma = pltpu.SemaphoreType.DMA
+    return pl.pallas_call(
+        functools.partial(tail_kernel, n, m),
+        in_specs=[vmem] * 6 + [pl.BlockSpec(memory_space=pl.ANY)],
+        out_specs=[vmem] * 3,
+        out_shape=[
+            jax.ShapeDtypeStruct((8, D), BF16),
+            jax.ShapeDtypeStruct((8, 128), F32),
+            jax.ShapeDtypeStruct((SEQS, width, STATE), F32),
+        ],
+        scratch_shapes=[
+            pltpu.VMEM(vocab.shape, BF16),
+            pltpu.VMEM((n, 8, 128), F32),
+            pltpu.VMEM((m, 8, 128), F32),
+            pltpu.VMEM((m, 32, D // m), BF16),
+            pltpu.VMEM((m, 8, D // m), F32),
+            pltpu.VMEM((n, 8, 256), F32),
+            pltpu.VMEM((m, 8, 128), BF16),
+            pltpu.VMEM((n // 2, 2, m, 8, 128), BF16),
+            pltpu.VMEM((8 * m, D), F32),
+            pltpu.VMEM((m, 8, 128), F32),
+            pltpu.VMEM((n, 8, 128), F32),
+            pltpu.VMEM((n, SEQS - 1, STATE, width), BF16),
+            dma,
+            dma((n,)),
+            dma((n,)),
+            dma((m,)),
+            dma((m,)),
+            dma((m,)),
+            dma((m,)),
+            dma((n,)),
+            dma((n,)),
+            dma((m,)),
+            dma((m,)),
+            dma((n,)),
+            dma((n,)),
+            dma((m,)),
+            dma((m,)),
+            dma((n,)),
+            dma((n,)),
+            dma((n, SEQS - 1)),
+            dma((n, SEQS - 1)),
+        ],
+        compiler_params=pltpu.CompilerParams(
+            collective_id=1, has_side_effects=True, vmem_limit_bytes=VMEM_LIMIT
+        ),
+        name="tail",
+    )(rows, out_weight, tails, reached, resid, gain, vocab)
+
+
 def body(
     conv_input,
     gate_projected,
@@ -538,15 +877,8 @@
     y, states, tails, aux, c, lead = local_pass(
         meta, conv, halo, conv_weight, convolution_bias[None], dt, dtt, a, at, dx
     )
-    tail_share = lax.psum_scatter(tails, "seq", scatter_dimension=2, tiled=True)
     entering, reached = exchange(states, aux, seq_count)
     gated = finish(y, c, entering, lead, gate_projected[0], norm_weight[None])
-
-    final = jnp.concatenate(
-        [reached[: SEQS - 1] + tail_share.astype(F32), reached[SEQS - 1 :]], axis=0
-    )
-    final_states = final.reshape(SEQS, STATE, HEADS // seq_count, CHANNEL_WIDTH)
-    final_states = final_states.transpose(0, 2, 3, 1)[None]
 
     lasts = []
     for request in range(SEQS):
@@ -555,25 +887,20 @@
         spot = jnp.clip(local_end, 0, local_len - 1)
         lasts.append(jnp.where(owned, gated[spot].astype(jnp.float32), 0.0))
     last_local = jnp.stack(lasts)
-    rows_total = residual_last.shape[0]
-    group_rows = lax.psum(last_local.astype(jnp.bfloat16), "seq")[None]
-    all_rows = lax.all_gather(group_rows, "req", axis=0, tiled=True)
-    share = out_weight.shape[0]
-    flat_place = req_place * seq_count + seq_place
-    columns = lax.dynamic_slice_in_dim(all_rows.reshape(-1, inner), flat_place * share, share, 1)
-    partial_value = jnp.dot(columns, out_weight, preferred_element_type=jnp.float32)
-    summed = lax.psum(partial_value, ("req", "seq"))
-    hidden = residual_last.reshape(-1, D).astype(jnp.float32) + summed
-    last_hidden = hidden.astype(jnp.bfloat16).reshape(rows_total, SEQS, D)
-    own_hidden = lax.dynamic_slice_in_dim(last_hidden, req_place, 1, 0)
-    scale = lax.rsqrt(jnp.mean(hidden * hidden, axis=-1, keepdims=True) + TINY_FLOOR)
-    normed = (hidden * scale * final_gain).astype(jnp.bfloat16)
-    logits = lax.dot_general(
-        normed, vocab_weight, (((1,), (1,)), ((), ())), preferred_element_type=jnp.float32
+    req_count = lax.axis_size("req")
+    rows = last_local.reshape(SEQS, seq_count, 2, 128).transpose(1, 2, 0, 3).reshape(seq_count, 8, 128)
+    resid = lax.dynamic_slice(
+        residual_last,
+        (seq_place // 2, 0, req_place * (D // req_count) + (seq_place % 2) * 256),
+        (1, SEQS, 256),
+    )[0]
+    resid = jnp.concatenate([jnp.zeros_like(resid), resid], axis=0)
+    hid, top, final = tail(
+        rows, out_weight, tails, reached, resid, final_gain[None], vocab_weight, seq_count, req_count
     )
-    local_top = jnp.max(logits, axis=1)
-    top_all = lax.pmax(local_top, ("req", "seq"))
-    max_logit = lax.dynamic_slice_in_dim(top_all.reshape(rows_total, SEQS), req_place, 1, 0)
+    own_hidden = hid[None, SEQS:]
+    max_logit = lax.dynamic_slice(top, (0, req_place * 8 + SEQS), (1, SEQS))
+    final_states = final.reshape(SEQS, HEADS // seq_count, CHANNEL_WIDTH, STATE)[None]
     return (gated[None], final_states, own_hidden, max_logit)
 
 

time: 431 us -> 219 us (0.51)
  blocking collectives: 150 us -> 0 us
  waiting for transfers between devices: 142 us -> 0.01 us
  Pallas kernels: 90.2 us -> 192 us
  between operations: 18.3 us -> 3.31 us
  matrix products: 7.17 us -> 0 us
    psum x1 -> x0, waiting for transfers between devices: 142 us -> none  [body(): summed = lax.psum(partial_value, ('req', 'seq'))]
    pallas_call x0 -> x1, Pallas kernels: none -> 103 us  [tail(): pl.pallas_call(functools.partial(tail_kernel, n, m), in_specs=[vmem] * 6...]
    pmax x1 -> x0, blocking collectives: 63.9 us -> none  [body(): top_all = lax.pmax(local_top, ('req', 'seq'))]
    psum x1 -> x0, blocking collectives: 58 us -> none  [body(): group_rows = lax.psum(last_local.astype(jnp.bfloat16), 'seq')[None]]
    all_gather x1 -> x0, blocking collectives: 28.6 us -> none  [body(): all_rows = lax.all_gather(group_rows, 'req', axis=0, tiled=True)]
    dot_general x2 -> x0, matrix products: 7.17 us -> none  [the longest x1 6.1 us: body(): lax.dot_general(normed, vocab_weight, (((1,), (1,)), ((), ())), preferred...]
  transfers between devices with their start and end apart: 3 -> 1, of which waited for: 1 -> 0; matrix products, arithmetic and copies ran while one was open for 4% -> 5% of each run, Pallas kernels for 0% -> 0%
where the time goes in v2:
time: 219 us; the launch traced here: 218 us
  Pallas kernels  192 us (88%)
  local copies, waits for them, and re-layouts  13.5 us (6%)
  other arithmetic  4.61 us (2%)
  starting transfers between devices  4.35 us (2%)
  between operations  3.31 us (2%)
    pallas_call x1, Pallas kernels, tail(): pl.pallas_call(functools.partial(tail_kernel, n, m), in_specs=[vmem] * 6...  103 us
    pallas_call x1, Pallas kernels, exchange(): pl.pallas_call(functools.partial(exchange_kernel, n), in_specs=[vmem, vme...  43.5 us
    pallas_call x1, Pallas kernels, local_pass(): pl.pallas_call(local_kernel, grid=grid, in_specs=in_specs, out_specs=out_...  34.4 us
    pallas_call x1, Pallas kernels, finish(): pl.pallas_call(finish_kernel, grid=(GROUPS, length // BLOCK), in_specs=[b...  11.7 us
  transfers between devices with their start and end apart: 1, of which 0 were waited for; matrix products, arithmetic and copies ran while one was open for 5% of the time, Pallas kernels for 0%

profile of v2, /device:TPU:1, one launch (start us, length us, event | category | flops | bytes accessed | tf_op | source)
XLA Modules:
  0.0 218.2 jit_solution(3202323692558548149)
XLA Ops:
  0.6 0.0 copy-start
  0.6 0.9 slice_bitcast_fusion
  1.6 4.4 %collective-permute-start = (bf16[8,5120]{1,0:T(8,128)(2,1)S(1)}, bf16[8,5120]{1,0:T(8,128)(2,1)S(1)}, u32[]{:S(2)}, u32[]{:S(2)}) collective-permute-start(bf16[8,5120]{1,0:T(8,128)(2,1)S(1)} %slice_bitcast_fusion), channel_id=1, source_target_pairs={{0,1},{1,2},{2,3},{3,4},{4,5},{5,6},{6,7},{7,8},{8,9},{9,10},{10,1... | collective-permute-start | bytes 245768 | tf_op jit(solution)/shard_map/ppermute | solution.py:864
  5.9 0.7 negate_multiply_fusion
  6.6 0.8 broadcast_in_dim_reshape.12.at_ref
  7.4 0.1 tile.20
  7.5 0.8 reduce-window.4
  8.3 0.7 fusion.2
  11.6 1.0 squeeze.9
  12.6 0.7 add.52
  13.3 0.8 fusion
  14.1 0.1 tile.18
  14.2 1.3 copy.25.dt_ref
  15.5 0.7 tile.22.a_ref
  16.2 0.7 broadcast_in_dim.32
  16.9 0.7 broadcast_in_dim_reshape.10.dx_ref
  17.6 0.0 copy-done
  17.6 0.6 concatenate.8.resid_ref
  18.2 0.6 pad_add_fusion.meta
  18.8 0.0 collective-permute-done.xh_ref.bh_ref.ch_ref
  18.8 0.0 copy-start.1
  18.8 0.6 copy-done.1
  19.4 34.4 %local_pass.1 = (f32[512,4096]{1,0:T(8,128)}, bf16[128,4096]{1,0:T(8,128)(2,1)}, bf16[3,128,4096]{2,1,0:T(8,128)(2,1)}, f32[8,4096]{1,0:T(8,128)}, bf16[512,512]{1,0:T(8,128)(2,1)}, /*index=5*/f32[4,2,256,128]{3,2,1,0:T(8,128)}) custom-call(s32[5]{0:T(128)} %pad_add_fusion.meta, bf16[512,5120]{1,0:T(8,128)(2,1)} %bitcast.42, bf16[512,5120]{1,0:T(8,128)(2,1)} %bitcast.43, ...), custom_call_target="tpu_custom_call" | custom-call | tf_op jit(solution)/shard_map/local_pass/pallas_call | solution.py:304
  53.8 43.5 %exchange.1 = (bf16[128,4096]{1,0:T(8,128)(2,1)}, f32[4,128,256]{2,1,0:T(8,128)}) custom-call(bf16[128,4096]{1,0:T(8,128)(2,1)} %get-tuple-element.17.st_ref, f32[8,4096]{1,0:T(8,128)} %get-tuple-element.18.aux_ref), custom_call_target="tpu_custom_call" | custom-call | tf_op jit(solution)/shard_map/exchange/pallas_call | solution.py:444
  97.3 11.7 %finish.1 = bf16[512,4096]{1,0:T(8,128)(2,1)} custom-call(f32[512,4096]{1,0:T(8,128)} %get-tuple-element.15.y_ref, bf16[512,512]{1,0:T(8,128)(2,1)} %get-tuple-element.16.c_ref, bf16[128,4096]{1,0:T(8,128)(2,1)} %get-tuple-element.19.e_ref, f32[4,2,256,128]{3,2,1,0:T(8,128)} %get-tuple-element.20.ld_ref, bf16[512,4096]{1,0:T(8,128)(2,1)} %bitcast.47, ...), custom_call_target="tpu_custom_call" | custom-call | tf_op jit(solution)/shard_map/finish/pallas_call | solution.py:479
  109.1 1.1 broadcast_select_fusion.3
  110.1 0.7 pad_maximum_fusion
  110.8 102.7 %tail.1 = (bf16[8,4096]{1,0:T(8,128)(2,1)}, f32[8,128]{1,0:T(8,128)}, f32[4,256,128]{2,1,0:T(8,128)}) custom-call(f32[16,8,128]{2,1,0:T(8,128)} %bitcast.49, bf16[32,4096]{1,0:T(8,128)(2,1)} %w_ref.1, bf16[3,128,4096]{2,1,0:T(8,128)(2,1)} %get-tuple-element.21.tails_ref, f32[4,128,256]{2,1,0:T(8,128)} %get-tuple-element.22.reach_ref, ...), custom_call_target="tpu_custom_call" | custom-call | tf_op jit(solution)/shard_map/tail/pallas_call | solution.py:790
  213.6 1.5 slice_bitcast_fusion.1
  215.0 1.3 constant_dynamic-slice_fusion
  216.3 1.9 copy.39
  (2 shorter events, 0.0 us)
Async XLA Ops:
  0.6 17.0 %copy-start = (bf16[8,4,4096]{2,1,0:T(4,128)(2,1)S(1)}, bf16[8,4,4096]{2,1,0:T(4,128)(2,1)}, u32[]{:S(2)}) copy-start(bf16[8,4,4096]{2,1,0:T(4,128)(2,1)} %param.25) | copy-start | bytes 786436
  1.6 17.2 %collective-permute-start = (bf16[8,5120]{1,0:T(8,128)(2,1)S(1)}, bf16[8,5120]{1,0:T(8,128)(2,1)S(1)}, u32[]{:S(2)}, u32[]{:S(2)}) collective-permute-start(bf16[8,5120]{1,0:T(8,128)(2,1)S(1)} %slice_bitcast_fusion), channel_id=1, source_target_pairs={{0,1},{1,2},{2,3},{3,4},{4,5},{5,6},{6,7},{7,8},{8,9},{9,10},{10,1... | collective-permute-start | bytes 245768 | tf_op jit(solution)/shard_map/ppermute | solution.py:864
  18.8 0.6 copy-start.1

commit v3 on v2

--- a/solution.py
+++ b/solution.py
@@ -521,7 +521,10 @@
     hf,
     mx1,
     mx2,
-    trecv,
+    p1,
+    p2,
+    p3,
+    p4,
     vsem,
     rs_s,
     rs_r,
@@ -539,8 +542,14 @@
     m1_r,
     m2_s,
     m2_r,
-    t_s,
-    t_r,
+    p1_s,
+    p1_r,
+    p2_s,
+    p2_r,
+    p3_s,
+    p3_r,
+    p4_s,
+    p4_r,
 ):
     s = lax.axis_index("seq")
     b = lax.axis_index("req")
@@ -636,17 +645,97 @@
     def m2_copy(p, slot):
         return remote(mx2.at[s], mx2.at[slot], m2_s.at[p], m2_r.at[slot], {"seq": p})
 
-    def t_copy(p, slot, r):
-        cols = pl.ds(pl.multiple_of(p * width, width), width)
-        return remote(tails_ref.at[r, :, cols], trecv.at[slot, r], t_s.at[p, r], t_r.at[slot, r], {"seq": p})
-
-    def send_tails(lo, hi):
-        def start(i, _):
-            for r in range(SEQS - 1):
-                t_copy(seq_peer(i), s, r).start()
-            return 0
-
-        lax.fori_loop(lo, hi, start, 0)
+    sy, sz = s // 4, lax.rem(s, 4)
+
+    def even(c):
+        return c + 1 - 2 * lax.rem(c, 2)
+
+    def odd(c):
+        return 3 - c
+
+    orders = []
+    for v in range(4):
+        first_is_z = v % 2 == 0
+        near, far = (even, odd) if v < 2 else (odd, even)
+        c, e = (sz, sy) if first_is_z else (sy, sz)
+        orders.append((first_is_z, near, far, c, e))
+
+    def spot_of(v, c, e):
+        return e * 4 + c if orders[v][0] else c * 4 + e
+
+    def block(v, c, e):
+        cols = pl.ds(pl.multiple_of(spot_of(v, c, e) * width, width), width)
+        return (slice(None), pl.ds(32 * v, 32), cols)
+
+    def stage1(v, i, q):
+        _, near, far, c, _ = orders[v]
+        p = near(c)
+        src = tails_ref.at[block(v, p if i == 0 else far(p), q)]
+        _, _, _, _, e = orders[v]
+        return remote(src, p1.at[v, i, q], p1_s.at[v, i, q], p1_r.at[v, i, q], {"seq": spot_of(v, p, e)})
+
+    def stage2(v, q):
+        _, _, far, c, e = orders[v]
+        return remote(
+            p1.at[v, 1, q], p2.at[v, q], p2_s.at[v, q], p2_r.at[v, q], {"seq": spot_of(v, far(c), e)}
+        )
+
+    def stage3(v, i):
+        _, near, far, c, e = orders[v]
+        p = near(e)
+        src = p2.at[v, p if i == 0 else far(p)]
+        return remote(src, p3.at[v, i], p3_s.at[v, i], p3_r.at[v, i], {"seq": spot_of(v, c, p)})
+
+    def stage4(v):
+        _, _, far, c, e = orders[v]
+        return remote(p3.at[v, 1], p4.at[v], p4_s.at[v], p4_r.at[v], {"seq": spot_of(v, c, far(e))})
+
+    def each(act, one):
+        for v in range(4):
+            for i in range(2):
+                if act == 1:
+
+                    def step(q, _):
+                        one(stage1(v, i, q))
+                        return 0
+
+                    lax.fori_loop(0, 4, step, 0)
+                elif act == 2 and i == 0:
+
+                    def step(q, _):
+                        one(stage2(v, q))
+                        return 0
+
+                    lax.fori_loop(0, 4, step, 0)
+                elif act == 3:
+                    one(stage3(v, i))
+                elif act == 4 and i == 0:
+                    one(stage4(v))
+
+    go = lambda copy: copy.start()
+    got = lambda copy: copy.wait_recv()
+    sent = lambda copy: copy.wait_send()
+
+    def add1():
+        for v in range(4):
+            _, _, far, c, _ = orders[v]
+            for i in range(2):
+
+                def step(q, _):
+                    p1[v, i, q] = p1[v, i, q] + tails_ref[block(v, c if i == 0 else far(c), q)]
+                    return 0
+
+                lax.fori_loop(0, 4, step, 0)
+
+    def add2():
+        for v in range(4):
+            p2[v] = p2[v] + p1[v, 0]
+
+    def add3():
+        for v in range(4):
+            _, _, far, _, e = orders[v]
+            p3[v, 0] = p3[v, 0] + p2[v, e]
+            p3[v, 1] = p3[v, 1] + p2[v, far(e)]
 
     rows_go, rows_in, rows_out = over(n, seq_peer, rows_copy, s)
     ag_go, ag_in, ag_out = over(m, req_peer, gather_copy, b)
@@ -680,11 +769,10 @@
         wbuf[w_slot] = w_ref[:, pl.ds(pl.multiple_of(b * depth, depth), depth)]
 
     rrecv[s] = rows_ref[s]
-    send_tails(1, 3)
+    each(1, go)
     rows_in()
     ragg[b] = jnp.sum(rrecv[...], axis=0)
     ag_go()
-    send_tails(3, 4)
     ag_in()
 
     def w_arrive(i, _):
@@ -706,18 +794,21 @@
     part[...] = both.reshape(m, 8, depth)
     part_go()
     precv[s] = part[s // 2, :, pl.ds(pl.multiple_of(lax.rem(s, 2) * 256, 256), 256)]
-    send_tails(4, 8)
+    each(1, got)
+    add1()
+    each(2, go)
     part_in()
     hidden = jnp.sum(precv[...], axis=0) + resid_ref[...].astype(F32)
     upper = pltpu.roll(hidden[:, 128:256], 4, 0)
     eight = lax.broadcasted_iota(jnp.int32, (8, 128), 0)
     h1[b] = jnp.where(eight < 4, upper, hidden[:, 0:128]).astype(BF16)
     h1_go()
-    send_tails(8, 9)
     h1_in()
     h2_go()
     h2[s // 2, lax.rem(s, 2)] = h1[...]
-    send_tails(9, n)
+    each(2, got)
+    add2()
+    each(3, go)
     h2_in()
 
     for k in range(m):
@@ -739,26 +830,19 @@
     top = jnp.concatenate([top, top], axis=1)
     mx1[b] = jnp.broadcast_to(top, (8, 128))
     m1_go()
+    each(3, got)
+    add3()
+    each(4, go)
     m1_in()
     mx2[s] = jnp.max(mx1[...], axis=0)
     m2_go()
 
-    def t_arrive(i, _):
-        for r in range(SEQS - 1):
-            t_copy(seq_peer(i), seq_peer(i), r).wait_recv()
-        return 0
-
-    lax.fori_loop(1, n, t_arrive, 0)
-    trecv[s] = tails_ref[:, :, pl.ds(pl.multiple_of(s * width, width), width)]
-
-    def collect(r, _):
-        total = reach_ref[r]
-        for d in range(n):
-            total = total + trecv[d, r].astype(F32)
-        fin_ref[r] = total.T
-        return 0
-
-    lax.fori_loop(0, SEQS - 1, collect, 0)
+    each(4, got)
+    for v in range(4):
+        p4[v] = p4[v] + p3[v, 0]
+    for r in range(SEQS - 1):
+        share = jnp.concatenate([p4[v, r].astype(F32) for v in range(4)], axis=0)
+        fin_ref[r] = (reach_ref[r] + share).T
     fin_ref[SEQS - 1] = reach_ref[SEQS - 1].T
     m2_in()
     max_ref[...] = jnp.max(mx2[...], axis=0)
@@ -775,12 +859,8 @@
 
     lax.fori_loop(0, m, w_drain, 0)
 
-    def t_drain(i, _):
-        for r in range(SEQS - 1):
-            t_copy(seq_peer(i), s, r).wait_send()
-        return 0
-
-    lax.fori_loop(1, n, t_drain, 0)
+    for act in range(1, 5):
+        each(act, sent)
 
 
 def tail(rows, out_weight, tails, reached, resid, gain, vocab, n, m):
@@ -808,7 +888,10 @@
             pltpu.VMEM((8 * m, D), F32),
             pltpu.VMEM((m, 8, 128), F32),
             pltpu.VMEM((n, 8, 128), F32),
-            pltpu.VMEM((n, SEQS - 1, STATE, width), BF16),
+            pltpu.VMEM((4, 2, 4, SEQS - 1, 32, width), BF16),
+            pltpu.VMEM((4, 4, SEQS - 1, 32, width), BF16),
+            pltpu.VMEM((4, 2, SEQS - 1, 32, width), BF16),
+            pltpu.VMEM((4, SEQS - 1, 32, width), BF16),
             dma,
             dma((n,)),
             dma((n,)),
@@ -826,8 +909,14 @@
             dma((m,)),
             dma((n,)),
             dma((n,)),
-            dma((n, SEQS - 1)),
-            dma((n, SEQS - 1)),
+            dma((4, 2, 4)),
+            dma((4, 2, 4)),
+            dma((4, 4)),
+            dma((4, 4)),
+            dma((4, 2)),
+            dma((4, 2)),
+            dma((4,)),
+            dma((4,)),
         ],
         compiler_params=pltpu.CompilerParams(
             collective_id=1, has_side_effects=True, vmem_limit_bytes=VMEM_LIMIT

time: 219 us -> 169 us (0.77)
  Pallas kernels: 192 us -> 143 us
    pallas_call x1, Pallas kernels: 103 us -> 55 us  [tail(): pl.pallas_call(functools.partial(tail_kernel, n, m), in_specs=[vmem] * 6...]
  transfers between devices with their start and end apart: 1 -> 1, of which waited for: 0 -> 0; matrix products, arithmetic and copies ran while one was open for 5% -> 6% of each run, Pallas kernels for 0% -> 0%
where the time goes in v3:
time: 169 us; the launch traced here: 168 us
  Pallas kernels  143 us (85%)
  local copies, waits for them, and re-layouts  13.5 us (8%)
  other arithmetic  4.61 us (3%)
  starting transfers between devices  4.35 us (3%)
  between operations  3.31 us (2%)
    pallas_call x1, Pallas kernels, tail(): pl.pallas_call(functools.partial(tail_kernel, n, m), in_specs=[vmem] * 6...  55 us
    pallas_call x1, Pallas kernels, exchange(): pl.pallas_call(functools.partial(exchange_kernel, n), in_specs=[vmem, vme...  41.4 us
    pallas_call x1, Pallas kernels, local_pass(): pl.pallas_call(local_kernel, grid=grid, in_specs=in_specs, out_specs=out_...  34.4 us
    pallas_call x1, Pallas kernels, finish(): pl.pallas_call(finish_kernel, grid=(GROUPS, length // BLOCK), in_specs=[b...  11.7 us
    ppermute x1, starting transfers between devices, body(): halo = lax.ppermute(conv[local_len - 8:], 'seq', route)  4.35 us
  transfers between devices with their start and end apart: 1, of which 0 were waited for; matrix products, arithmetic and copies ran while one was open for 6% of the time, Pallas kernels for 0%

profile of v3, /device:TPU:1, one launch (start us, length us, event | category | flops | bytes accessed | tf_op | source)
XLA Modules:
  0.0 168.4 jit_solution(8101194109989885715)
XLA Ops:
  0.6 0.0 copy-start
  0.6 0.9 slice_bitcast_fusion
  1.6 4.4 %collective-permute-start = (bf16[8,5120]{1,0:T(8,128)(2,1)S(1)}, bf16[8,5120]{1,0:T(8,128)(2,1)S(1)}, u32[]{:S(2)}, u32[]{:S(2)}) collective-permute-start(bf16[8,5120]{1,0:T(8,128)(2,1)S(1)} %slice_bitcast_fusion), channel_id=1, source_target_pairs={{0,1},{1,2},{2,3},{3,4},{4,5},{5,6},{6,7},{7,8},{8,9},{9,10},{10,1... | collective-permute-start | bytes 245768 | tf_op jit(solution)/shard_map/ppermute | solution.py:953
  5.9 0.7 negate_multiply_fusion
  6.6 0.8 broadcast_in_dim_reshape.12.at_ref
  7.4 0.1 tile.20
  7.5 0.8 reduce-window.4
  8.3 0.7 fusion.2
  11.6 1.0 squeeze.9
  12.6 0.7 add.52
  13.3 0.8 fusion
  14.1 0.1 tile.18
  14.2 1.3 copy.25.dt_ref
  15.5 0.7 tile.22.a_ref
  16.2 0.7 broadcast_in_dim.32
  16.9 0.7 broadcast_in_dim_reshape.10.dx_ref
  17.6 0.0 copy-done
  17.6 0.6 concatenate.8.resid_ref
  18.2 0.6 pad_add_fusion.meta
  18.8 0.0 collective-permute-done.xh_ref.bh_ref.ch_ref
  18.8 0.0 copy-start.1
  18.8 0.6 copy-done.1
  19.4 34.4 %local_pass.1 = (f32[512,4096]{1,0:T(8,128)}, bf16[128,4096]{1,0:T(8,128)(2,1)}, bf16[3,128,4096]{2,1,0:T(8,128)(2,1)}, f32[8,4096]{1,0:T(8,128)}, bf16[512,512]{1,0:T(8,128)(2,1)}, /*index=5*/f32[4,2,256,128]{3,2,1,0:T(8,128)}) custom-call(s32[5]{0:T(128)} %pad_add_fusion.meta, bf16[512,5120]{1,0:T(8,128)(2,1)} %bitcast.42, bf16[512,5120]{1,0:T(8,128)(2,1)} %bitcast.43, ...), custom_call_target="tpu_custom_call" | custom-call | tf_op jit(solution)/shard_map/local_pass/pallas_call | solution.py:304
  53.8 41.4 %exchange.1 = (bf16[128,4096]{1,0:T(8,128)(2,1)}, f32[4,128,256]{2,1,0:T(8,128)}) custom-call(bf16[128,4096]{1,0:T(8,128)(2,1)} %get-tuple-element.17.st_ref, f32[8,4096]{1,0:T(8,128)} %get-tuple-element.18.aux_ref), custom_call_target="tpu_custom_call" | custom-call | tf_op jit(solution)/shard_map/exchange/pallas_call | solution.py:444
  95.3 11.7 %finish.1 = bf16[512,4096]{1,0:T(8,128)(2,1)} custom-call(f32[512,4096]{1,0:T(8,128)} %get-tuple-element.15.y_ref, bf16[512,512]{1,0:T(8,128)(2,1)} %get-tuple-element.16.c_ref, bf16[128,4096]{1,0:T(8,128)(2,1)} %get-tuple-element.19.e_ref, f32[4,2,256,128]{3,2,1,0:T(8,128)} %get-tuple-element.20.ld_ref, bf16[512,4096]{1,0:T(8,128)(2,1)} %bitcast.47, ...), custom_call_target="tpu_custom_call" | custom-call | tf_op jit(solution)/shard_map/finish/pallas_call | solution.py:479
  107.0 1.1 broadcast_select_fusion.3
  108.0 0.7 pad_maximum_fusion
  108.7 55.0 %tail.1 = (bf16[8,4096]{1,0:T(8,128)(2,1)}, f32[8,128]{1,0:T(8,128)}, f32[4,256,128]{2,1,0:T(8,128)}) custom-call(f32[16,8,128]{2,1,0:T(8,128)} %bitcast.49, bf16[32,4096]{1,0:T(8,128)(2,1)} %w_ref.1, bf16[3,128,4096]{2,1,0:T(8,128)(2,1)} %get-tuple-element.21.tails_ref, f32[4,128,256]{2,1,0:T(8,128)} %get-tuple-element.22.reach_ref, ...), custom_call_target="tpu_custom_call" | custom-call | tf_op jit(solution)/shard_map/tail/pallas_call | solution.py:870
  163.7 1.5 slice_bitcast_fusion.1
  165.2 1.3 constant_dynamic-slice_fusion
  166.5 1.9 %copy.39 = f32[1,4,4,64,128]{4,3,2,1,0:T(8,128)} copy(f32[1,4,4,64,128]{4,3,2,1,0:T(8,128)} %bitcast.48) | data formatting | bytes 1048576
  (2 shorter events, 0.0 us)
Async XLA Ops:
  0.6 17.0 %copy-start = (bf16[8,4,4096]{2,1,0:T(4,128)(2,1)S(1)}, bf16[8,4,4096]{2,1,0:T(4,128)(2,1)}, u32[]{:S(2)}) copy-start(bf16[8,4,4096]{2,1,0:T(4,128)(2,1)} %param.25) | copy-start | bytes 786436
  1.6 17.2 %collective-permute-start = (bf16[8,5120]{1,0:T(8,128)(2,1)S(1)}, bf16[8,5120]{1,0:T(8,128)(2,1)S(1)}, u32[]{:S(2)}, u32[]{:S(2)}) collective-permute-start(bf16[8,5120]{1,0:T(8,128)(2,1)S(1)} %slice_bitcast_fusion), channel_id=1, source_target_pairs={{0,1},{1,2},{2,3},{3,4},{4,5},{5,6},{6,7},{7,8},{8,9},{9,10},{10,1... | collective-permute-start | bytes 245768 | tf_op jit(solution)/shard_map/ppermute | solution.py:953
  18.8 0.6 copy-start.1

commit v4 on v3

--- a/solution.py
+++ b/solution.py
@@ -66,12 +66,25 @@
     return dot(parts, spread_ref[...])
 
 
-def silu(x):
-    return x * jax.nn.sigmoid(x)
+def halves(h):
+    return h + h * jnp.tanh(h)
+
+
+def softplus(x):
+    e = jnp.exp(-jnp.abs(x))
+    w = 1.0 + e
+    d = w - 1.0
+    return jnp.maximum(x, 0.0) + jnp.where(d == 0.0, e, jnp.log(w) * (e / jnp.where(d == 0.0, 1.0, d)))
+
+
+def bounds_of(len_ref):
+    b1 = len_ref[0, 0]
+    b2 = b1 + len_ref[0, 1]
+    return b1, b2, b2 + len_ref[0, 2]
 
 
 def local_kernel(
-    meta,
+    len_ref,
     x_ref,
     b_ref,
     c_ref,
@@ -84,11 +97,10 @@
     vx_ref,
     vb_ref,
     vc_ref,
-    dt_ref,
-    dtt_ref,
-    a_ref,
-    at_ref,
-    dx_ref,
+    raw_ref,
+    bias_ref,
+    log_ref,
+    gain_ref,
     y_ref,
     st_ref,
     pt_ref,
@@ -101,24 +113,75 @@
     c0,
     cumr,
     sp,
+    msk,
+    alw,
+    sgs,
+    cums,
+    lds,
+    dxs,
+    wst,
 ):
     g = pl.program_id(0)
     j = pl.program_id(1)
-    first = meta[0]
-    b1, b2, b3 = meta[1], meta[2], meta[3]
+    span = pl.num_programs(1) * BLOCK
+    first = lax.axis_index("seq") * span
+    b1, b2, b3 = bounds_of(len_ref)
+    bounds = (b1, b2, b3)
     start = first + j * BLOCK
 
     @pl.when((g == 0) & (j == 0))
     def _():
         sp[...] = spread_matrix()
+
+    row = lax.broadcasted_iota(jnp.int32, (BLOCK, 128), 0) + start
+
+    @pl.when(g == 0)
+    def _():
+        near = jnp.full((BLOCK, 128), 8, jnp.int32)
+        for bound in bounds:
+            gap = row - bound
+            near = jnp.where(gap >= 0, jnp.minimum(near, gap), near)
+        for k in range(3):
+            msk[j, k] = (near >= 3 - k).astype(F32)
+        sgs[j] = seg_of(row, b1, b2, b3)
+        i0 = lax.broadcasted_iota(jnp.int32, (BLOCK, BLOCK), 0)
+        i1 = lax.broadcasted_iota(jnp.int32, (BLOCK, BLOCK), 1)
+        t_seg = seg_of(i0 + start, b1, b2, b3)
+        s_seg = seg_of(i1 + start, b1, b2, b3)
+        alw[j] = ((i0 >= i1) & (t_seg == s_seg)).astype(F32)
+        tri = jnp.where(i0 >= i1, 1.0, 0.0).astype(BF16)
+        dt = softplus(raw_ref[...] + bias_ref[...])
+        dh, dm, dl = split3(dt * (jnp.exp(log_ref[...]) * -LOG2E))
+        cums[j] = (dot(tri, dl) + dot(tri, dm)) + dot(tri, dh)
+        lds[j] = jnp.log(dt) * LOG2E
+
+    l0 = lax.broadcasted_iota(jnp.int32, (HEADS, 128), 0)
+    l1 = lax.broadcasted_iota(jnp.int32, (HEADS, 128), 1)
+    pick = jnp.where(l0 == g * PER_GROUP + l1 % PER_GROUP, 1.0, 0.0).astype(BF16)
+    t0 = lax.broadcasted_iota(jnp.int32, (PER_GROUP, HEADS), 0)
+    t1 = lax.broadcasted_iota(jnp.int32, (PER_GROUP, HEADS), 1)
+    pickt = jnp.where(t1 == g * PER_GROUP + t0, 1.0, 0.0).astype(BF16)
+
+    def group(v):
+        hi, mid, lo = split3(v)
+        return (dot(lo, pick) + dot(mid, pick)) + dot(hi, pick)
 
     @pl.when(j == 0)
     def _():
         xext[0:8, 0:GW] = xh_ref[...].astype(F32)
         xext[0:8, GW : GW + 128] = bh_ref[...].astype(F32)
         xext[0:8, GW + 128 : GW + 256] = ch_ref[...].astype(F32)
+        for lo, hi, w_ref, v_ref in (
+            (0, GW, wx_ref, vx_ref),
+            (GW, GW + 128, wb_ref, vb_ref),
+            (GW + 128, GW + 256, wc_ref, vc_ref),
+        ):
+            wst[0:KERNEL, lo:hi] = w_ref[...] * 0.5
+            wst[KERNEL : KERNEL + 1, lo:hi] = v_ref[...] * 0.5
         pt_ref[...] = jnp.zeros_like(pt_ref)
         aux_ref[...] = jnp.zeros_like(aux_ref)
+        c0[...] = jnp.zeros_like(c0)
+        dxs[...] = spread(group(jnp.broadcast_to(gain_ref[...], (8, HEADS))), sp)
 
     @pl.when(j == 1)
     def _():
@@ -128,56 +191,42 @@
     xext[8 : BLOCK + 8, GW : GW + 128] = b_ref[...].astype(F32)
     xext[8 : BLOCK + 8, GW + 128 : GW + 256] = c_ref[...].astype(F32)
 
-    row = lax.broadcasted_iota(jnp.int32, (BLOCK, 128), 0) + start
-    seg = seg_of(row, b1, b2, b3)
-    same = [(seg_of(row - k, b1, b2, b3) == seg).astype(F32) for k in (3, 2, 1)]
-    for c in range(10):
-        cols = slice(c * 128, c * 128 + 128)
-        w_ref, v_ref, lo = (
-            (wx_ref, vx_ref, c * 128) if c < 8 else ((wb_ref, vb_ref, 0) if c == 8 else (wc_ref, vc_ref, 0))
-        )
-        part = slice(lo, lo + 128)
-        total = jnp.broadcast_to(v_ref[0:1, part], (BLOCK, 128))
-        for k in range(3):
-            total = total + w_ref[k : k + 1, part] * xext[5 + k : 5 + k + BLOCK, cols] * same[k]
-        total = total + w_ref[3:4, part] * xext[8 : 8 + BLOCK, cols]
-        xf[:, cols] = silu(total)
-
+    tile = 64
+
+    def convolve(c, _):
+        cols = pl.ds(pl.multiple_of(c * 128, 128), 128)
+        w = [wst[k : k + 1, cols] for k in range(KERNEL)]
+        bias = wst[KERNEL : KERNEL + 1, cols]
+        for lo in range(0, BLOCK, tile):
+            total = jnp.broadcast_to(bias, (tile, 128))
+            for k in range(3):
+                total = total + w[k] * xext[lo + 5 + k : lo + 5 + k + tile, cols] * msk[j, k, lo : lo + tile]
+            total = total + w[3] * xext[lo + 8 : lo + 8 + tile, cols]
+            xf[lo : lo + tile, cols] = halves(total)
+        return 0
+
+    lax.fori_loop(0, 10, convolve, 0)
+
+    seg = sgs[j]
     bf = xf[:, GW : GW + 128]
     cb = xf[:, GW + 128 : GW + 256].astype(BF16)
     co_ref[...] = cb
 
-    i0 = lax.broadcasted_iota(jnp.int32, (BLOCK, BLOCK), 0)
-    i1 = lax.broadcasted_iota(jnp.int32, (BLOCK, BLOCK), 1)
-    tri = jnp.where(i0 >= i1, 1.0, 0.0).astype(BF16)
-    triu = jnp.where(i0 <= i1, 1.0, 0.0).astype(BF16)
-    dt = dt_ref[0, 0]
-    dh, dm, dl = split3(dt * a_ref[0])
-    cum = (dot(tri, dl) + dot(tri, dm)) + dot(tri, dh)
-    logdt = jnp.log(dt) * LOG2E
-    dtt = dtt_ref[0, 0]
-    th, tm, tl = split3(dtt * at_ref[0])
-    cumt = (dot(tl, triu) + dot(tm, triu)) + dot(th, triu)
-    rt = jnp.log(dtt) * LOG2E - cumt
+    cum = group(cums[j])
+    logdt = group(lds[j])
+    rh, rm, rl = split3(lds[j] - cums[j])
+    rt = (dot_nt(pickt, rl) + dot_nt(pickt, rm)) + dot_nt(pickt, rh)
     cumr[...] = cum
     last = cum[BLOCK - 1 : BLOCK, :]
 
     seg_before_span = seg_of(first - 1, b1, b2, b3)
     seg_before = seg_of(start - 1, b1, b2, b3)
     seg_end = seg_of(start + BLOCK - 1, b1, b2, b3)
-
-    @pl.when(j == 0)
-    def _():
-        c0[...] = jnp.zeros_like(c0)
-
     prior = c0[0:1, :]
     ld_ref[0, 0] = jnp.where(seg == seg_before_span, jnp.exp2(cum + prior), 0.0)
 
     bh, bl = split2(bf)
-    sc = dot_nt(cb, bh)
-    t_seg = seg_of(i0 + start, b1, b2, b3)
-    s_seg = seg_of(i1 + start, b1, b2, b3)
-    sc = jnp.where((i0 >= i1) & (t_seg == s_seg), sc, 0.0)
+    sc = dot_nt(cb, bh) * alw[j]
 
     @pl.when(j == 0)
     def _():
@@ -209,7 +258,7 @@
                 jnp.concatenate([dot(top.astype(BF16), xb[:half]), dot(bottom, xb)], axis=0)
             )
         intra = jnp.where(lane < CHANNEL_WIDTH, res[0], res[1])
-        y_ref[:, cols] = y_ref[:, cols] + (intra + dx_ref[0:1, cols] * xb.astype(F32))
+        y_ref[:, cols] = y_ref[:, cols] + (intra + dxs[0:1, cols] * xb.astype(F32))
 
     bht, blt = split2(bf.T)
 
@@ -224,7 +273,7 @@
     own = state_of(at_end(seg_end))
 
     for r in range(SEQS - 1):
-        end = meta[1 + r] - 1
+        end = bounds[r] - 1
         local = end - start
         owned = (local >= 0) & (local < BLOCK)
 
@@ -257,7 +306,7 @@
         aux_ref[0:1, :] = whole8[0:1]
 
 
-def local_pass(meta, conv, halo, conv_weight, conv_bias, dt, dtt, a, at, dx):
+def local_pass(lengths, conv, halo, conv_weight, conv_bias, raw, bias, log, gain):
     length = conv.shape[0]
     blocks = length // BLOCK
     maps = D // 128
@@ -278,11 +327,10 @@
         + xs(KERNEL)
         + xs(1)
         + [
-            pl.BlockSpec((1, 1, BLOCK, 128), lambda g, j: (g, j, 0, 0)),
-            pl.BlockSpec((1, 1, PER_GROUP, BLOCK), lambda g, j: (g, j, 0, 0)),
-            pl.BlockSpec((1, 1, 128), lambda g, j: (g, 0, 0)),
-            pl.BlockSpec((1, PER_GROUP, 1), lambda g, j: (g, 0, 0)),
-            pl.BlockSpec((1, GW), lambda g, j: (0, g)),
+            pl.BlockSpec((BLOCK, HEADS), lambda g, j: (j, 0)),
+            pl.BlockSpec((1, HEADS), lambda g, j: (0, 0)),
+            pl.BlockSpec((1, HEADS), lambda g, j: (0, 0)),
+            pl.BlockSpec((1, HEADS), lambda g, j: (0, 0)),
         ]
     )
     out_specs = [
@@ -314,14 +362,21 @@
             pltpu.VMEM((8, 128), F32),
             pltpu.VMEM((BLOCK, 128), F32),
             pltpu.VMEM((128, GW), BF16),
+            pltpu.VMEM((blocks, 3, BLOCK, 128), F32),
+            pltpu.VMEM((blocks, BLOCK, BLOCK), F32),
+            pltpu.VMEM((blocks, BLOCK, 128), jnp.int32),
+            pltpu.VMEM((blocks, BLOCK, HEADS), F32),
+            pltpu.VMEM((blocks, BLOCK, HEADS), F32),
+            pltpu.VMEM((8, GW), F32),
+            pltpu.VMEM((8, GW + 256), F32),
         ],
         compiler_params=pltpu.CompilerParams(
             vmem_limit_bytes=VMEM_LIMIT, dimension_semantics=("arbitrary", "arbitrary")
         ),
         name="local_pass",
     )(
-        meta, conv, conv, conv, halo, halo, halo, conv_weight, conv_weight, conv_weight,
-        conv_bias, conv_bias, conv_bias, dt, dtt, a, at, dx,
+        lengths, conv, conv, conv, halo, halo, halo, conv_weight, conv_weight, conv_weight,
+        conv_bias, conv_bias, conv_bias, raw, bias, log, gain,
     )
 
 
@@ -462,24 +517,46 @@
     )(states, aux)
 
 
-def finish_kernel(y_ref, c_ref, e_ref, ld_ref, gate_ref, nw_ref, out_ref, sp):
-    @pl.when((pl.program_id(0) == 0) & (pl.program_id(1) == 0))
+def finish_kernel(len_ref, y_ref, c_ref, e_ref, ld_ref, gate_ref, nw_ref, out_ref, rows_ref, sp, of):
+    g = pl.program_id(0)
+    j = pl.program_id(1)
+
+    @pl.when((g == 0) & (j == 0))
     def _():
         sp[...] = spread_matrix()
 
+    @pl.when(j == 0)
+    def _():
+        rows_ref[...] = jnp.zeros_like(rows_ref)
+
     v = y_ref[...] + spread(ld_ref[0, 0], sp) * dot(c_ref[...], e_ref[...])
-    v = v * silu(gate_ref[...].astype(F32))
+    v = v * halves(0.5 * gate_ref[...].astype(F32))
     scale = lax.rsqrt(jnp.mean(v * v, axis=1, keepdims=True) + TINY_FLOOR)
-    out_ref[...] = (v * scale * nw_ref[...]).astype(BF16)
-
-
-def finish(y, c, entering, lead, gate, norm_weight):
+    out = (v * scale * nw_ref[...]).astype(BF16)
+    out_ref[...] = out
+
+    of[...] = out.astype(F32)
+    start = lax.axis_index("seq") * (pl.num_programs(1) * BLOCK) + j * BLOCK
+    bounds = bounds_of(len_ref)
+    for r, bound in enumerate(bounds + (bounds[2] + len_ref[0, 3],)):
+        local = bound - 1 - start
+
+        @pl.when((local >= 0) & (local < BLOCK))
+        def _():
+            line = of[pl.ds(jnp.clip(local, 0, BLOCK - 1), 1), :]
+            for c in range(GW // 128):
+                place = c % 2 * SEQS + r
+                rows_ref[c // 2, place : place + 1, :] = line[:, c * 128 : c * 128 + 128]
+
+
+def finish(lengths, y, c, entering, lead, gate, norm_weight):
     length = y.shape[0]
     block = lambda width: pl.BlockSpec((BLOCK, width), lambda g, j: (j, g))
     return pl.pallas_call(
         finish_kernel,
         grid=(GROUPS, length // BLOCK),
         in_specs=[
+            pl.BlockSpec(memory_space=pltpu.SMEM),
             block(GW),
             block(STATE),
             pl.BlockSpec((STATE, GW), lambda g, j: (0, g)),
@@ -487,14 +564,17 @@
             block(GW),
             pl.BlockSpec((1, GW), lambda g, j: (0, g)),
         ],
-        out_specs=block(GW),
-        out_shape=jax.ShapeDtypeStruct((length, D), BF16),
-        scratch_shapes=[pltpu.VMEM((128, GW), BF16)],
+        out_specs=[block(GW), pl.BlockSpec((GW // 256, 8, 128), lambda g, j: (g, 0, 0))],
+        out_shape=[
+            jax.ShapeDtypeStruct((length, D), BF16),
+            jax.ShapeDtypeStruct((D // 256, 8, 128), F32),
+        ],
+        scratch_shapes=[pltpu.VMEM((128, GW), BF16), pltpu.VMEM((BLOCK, GW), F32)],
         compiler_params=pltpu.CompilerParams(
             vmem_limit_bytes=VMEM_LIMIT, dimension_semantics=("arbitrary", "arbitrary")
         ),
         name="finish",
-    )(y, c, entering, lead, gate, norm_weight)
+    )(lengths, y, c, entering, lead, gate, norm_weight)
 
 
 def tail_kernel(
@@ -798,7 +878,9 @@
     add1()
     each(2, go)
     part_in()
-    hidden = jnp.sum(precv[...], axis=0) + resid_ref[...].astype(F32)
+    cols = pl.ds(pl.multiple_of(b * depth + lax.rem(s, 2) * 256, 256), 256)
+    resid = resid_ref[s // 2, :, cols].astype(F32)
+    hidden = jnp.sum(precv[...], axis=0) + jnp.concatenate([resid, resid], axis=0)
     upper = pltpu.roll(hidden[:, 128:256], 4, 0)
     eight = lax.broadcasted_iota(jnp.int32, (8, 128), 0)
     h1[b] = jnp.where(eight < 4, upper, hidden[:, 0:128]).astype(BF16)
@@ -818,7 +900,7 @@
             hf[:, lo : lo + 128] = piece
             hf[:, lo + 128 : lo + 256] = pltpu.roll(piece, 4, 0)
     h = hf[...]
-    hid_ref[...] = hf[pl.ds(pl.multiple_of(b * 8, 8), 8), :].astype(BF16)
+    hid_ref[0] = hf[pl.ds(pl.multiple_of(b * 8, 8), 8), :].astype(BF16)[SEQS:]
     scale = lax.rsqrt(jnp.mean(h * h, axis=1, keepdims=True) + TINY_FLOOR)
     normed = (h * scale * gain_ref[...]).astype(BF16)
     load.wait()
@@ -845,7 +927,14 @@
         fin_ref[r] = (reach_ref[r] + share).T
     fin_ref[SEQS - 1] = reach_ref[SEQS - 1].T
     m2_in()
-    max_ref[...] = jnp.max(mx2[...], axis=0)
+    best = jnp.max(mx2[...], axis=0)[0:1]
+    lanes = lax.broadcasted_iota(jnp.int32, (1, 128), 1)
+    four = lax.broadcasted_iota(jnp.int32, (1, SEQS), 1)
+    top = jnp.zeros((1, SEQS), F32)
+    for r in range(SEQS):
+        one = jnp.max(jnp.where(lanes == b * 8 + SEQS + r, best, -jnp.inf), axis=1, keepdims=True)
+        top = jnp.where(four == r, one, top)
+    max_ref[...] = top
 
     for drain in (rows_out, ag_out, part_out, h1_out, h2_out, m1_out, m2_out):
         drain()
@@ -872,8 +961,8 @@
         in_specs=[vmem] * 6 + [pl.BlockSpec(memory_space=pl.ANY)],
         out_specs=[vmem] * 3,
         out_shape=[
-            jax.ShapeDtypeStruct((8, D), BF16),
-            jax.ShapeDtypeStruct((8, 128), F32),
+            jax.ShapeDtypeStruct((1, SEQS, D), BF16),
+            jax.ShapeDtypeStruct((1, SEQS), F32),
             jax.ShapeDtypeStruct((SEQS, width, STATE), F32),
         ],
         scratch_shapes=[
@@ -942,55 +1031,29 @@
     vocab_weight,
 ):
     local_len = conv_input.shape[1]
-    inner = HEADS * CHANNEL_WIDTH
-    count = local_len // BLOCK
     seq_count = lax.axis_size("seq")
-    seq_place = lax.axis_index("seq")
-    req_place = lax.axis_index("req")
-    first = seq_place * local_len
+    req_count = lax.axis_size("req")
     conv = conv_input[0]
     route = [(i, i + 1) for i in range(seq_count - 1)]
     halo = lax.ppermute(conv[local_len - 8 :], "seq", route)
-    bounds = jnp.cumsum(lengths[0]).astype(jnp.int32)
-    meta = jnp.concatenate([first.astype(jnp.int32)[None], bounds])
-
-    step = jax.nn.softplus(step_raw[0] + step_bias)
-    step = step.reshape(count, BLOCK, GROUPS, PER_GROUP)
-    dt = jnp.tile(step.transpose(2, 0, 1, 3), (1, 1, 1, 128 // PER_GROUP))
-    dtt = step.transpose(2, 0, 3, 1)
-    rate = (-jnp.exp(decay_log) * LOG2E).reshape(GROUPS, PER_GROUP)
-    a = jnp.tile(rate, (1, 128 // PER_GROUP))[:, None, :]
-    at = rate[:, :, None]
-    dx = jnp.repeat(head_direct_gain, CHANNEL_WIDTH)[None]
-
     y, states, tails, aux, c, lead = local_pass(
-        meta, conv, halo, conv_weight, convolution_bias[None], dt, dtt, a, at, dx
+        lengths,
+        conv,
+        halo,
+        conv_weight,
+        convolution_bias[None],
+        step_raw[0],
+        step_bias[None],
+        decay_log[None],
+        head_direct_gain[None],
     )
     entering, reached = exchange(states, aux, seq_count)
-    gated = finish(y, c, entering, lead, gate_projected[0], norm_weight[None])
-
-    lasts = []
-    for request in range(SEQS):
-        local_end = bounds[request] - 1 - first
-        owned = (local_end >= 0) & (local_end < local_len)
-        spot = jnp.clip(local_end, 0, local_len - 1)
-        lasts.append(jnp.where(owned, gated[spot].astype(jnp.float32), 0.0))
-    last_local = jnp.stack(lasts)
-    req_count = lax.axis_size("req")
-    rows = last_local.reshape(SEQS, seq_count, 2, 128).transpose(1, 2, 0, 3).reshape(seq_count, 8, 128)
-    resid = lax.dynamic_slice(
-        residual_last,
-        (seq_place // 2, 0, req_place * (D // req_count) + (seq_place % 2) * 256),
-        (1, SEQS, 256),
-    )[0]
-    resid = jnp.concatenate([jnp.zeros_like(resid), resid], axis=0)
+    gated, rows = finish(lengths, y, c, entering, lead, gate_projected[0], norm_weight[None])
     hid, top, final = tail(
-        rows, out_weight, tails, reached, resid, final_gain[None], vocab_weight, seq_count, req_count
+        rows, out_weight, tails, reached, residual_last, final_gain[None], vocab_weight, seq_count, req_count
     )
-    own_hidden = hid[None, SEQS:]
-    max_logit = lax.dynamic_slice(top, (0, req_place * 8 + SEQS), (1, SEQS))
     final_states = final.reshape(SEQS, HEADS // seq_count, CHANNEL_WIDTH, STATE)[None]
-    return (gated[None], final_states, own_hidden, max_logit)
+    return (gated[None], final_states, hid, top)
 
 
 def solution(mesh):

time: 169 us -> 157 us (0.929)
  local copies, waits for them, and re-layouts: 13.5 us -> 7.67 us
  other arithmetic: 4.61 us -> 0 us
  between operations: 3.31 us -> 0.66 us
    unnamed x5 -> x6, local copies, waits for them, and re-layouts: 2.52 us -> 6.77 us
    another operation x7 -> x0, local copies, waits for them, and re-layouts: 3.62 us -> none  [the longest x2 1.43 us: body(): dt = jnp.tile(step.transpose(2, 0, 1, 3), (1, 1, 1, 128 // PER_GROUP))]
    pallas_call x1, Pallas kernels: 41.4 us -> 38.8 us  [exchange(): pl.pallas_call(functools.partial(exchange_kernel, n), in_specs=[vmem, vme...]
    broadcast_in_dim x2 -> x0, local copies, waits for them, and re-layouts: 2.2 us -> none  [the longest x1 1.47 us: body(): own_hidden = hid[None, SEQS:]]
    pallas_call x1, Pallas kernels: 55 us -> 57 us  [tail(): pl.pallas_call(functools.partial(tail_kernel, n, m), in_specs=[vmem] * 6...]
    pallas_call x1, Pallas kernels: 34.4 us -> 36.2 us  [local_pass(): pl.pallas_call(local_kernel, grid=grid, in_specs=in_specs, out_specs=out_...]
  transfers between devices with their start and end apart: 1 -> 1, of which waited for: 0 -> 0; matrix products, arithmetic and copies ran while one was open for 6% -> 1% of each run, Pallas kernels for 0% -> 0%
where the time goes in v4:
time: 157 us; the launch traced here: 156 us
  Pallas kernels  144 us (92%)
  local copies, waits for them, and re-layouts  7.67 us (5%)
  starting transfers between devices  4.35 us (3%)
    pallas_call x1, Pallas kernels, tail(): pl.pallas_call(functools.partial(tail_kernel, n, m), in_specs=[vmem] * 6...  57 us
    pallas_call x1, Pallas kernels, exchange(): pl.pallas_call(functools.partial(exchange_kernel, n), in_specs=[vmem, vme...  38.8 us
    pallas_call x1, Pallas kernels, local_pass(): pl.pallas_call(local_kernel, grid=grid, in_specs=in_specs, out_specs=out_...  36.2 us
    pallas_call x1, Pallas kernels, finish(): pl.pallas_call(finish_kernel, grid=(GROUPS, length // BLOCK), in_specs=[p...  11.7 us
    unnamed x6, local copies, waits for them, and re-layouts  6.77 us
    ppermute x1, starting transfers between devices, body(): halo = lax.ppermute(conv[local_len - 8:], 'seq', route)  4.35 us
  transfers between devices with their start and end apart: 1, of which 0 were waited for; matrix products, arithmetic and copies ran while one was open for 1% of the time, Pallas kernels for 0%

profile of v4, /device:TPU:1, one launch (start us, length us, event | category | flops | bytes accessed | tf_op | source)
XLA Modules:
  0.0 156.3 jit_solution(15278038026190490928)
XLA Ops:
  0.6 0.9 slice_bitcast_fusion
  1.5 4.4 %collective-permute-start = (bf16[8,5120]{1,0:T(8,128)(2,1)S(1)}, bf16[8,5120]{1,0:T(8,128)(2,1)S(1)}, u32[]{:S(2)}, u32[]{:S(2)}) collective-permute-start(bf16[8,5120]{1,0:T(8,128)(2,1)S(1)} %slice_bitcast_fusion), channel_id=1, source_target_pairs={{0,1},{1,2},{2,3},{3,4},{4,5},{5,6},{6,7},{7,8},{8,9},{9,10},{10,1... | collective-permute-start | bytes 245768 | tf_op jit(solution)/shard_map/ppermute | solution.py:1038
  5.9 1.8 %copy.18 = f32[1,512,64]{2,1,0:T(8,128)} copy(f32[1,512,64]{1,2,0:T(8,128)} %param.16) | data formatting | bytes 262144 | tf_op args[2]
  7.6 0.0 collective-permute-done.xh_ref.bh_ref.ch_ref
  7.6 0.0 copy-start
  7.6 0.6 copy-done
  8.3 36.2 %local_pass.1 = (f32[512,4096]{1,0:T(8,128)}, bf16[128,4096]{1,0:T(8,128)(2,1)}, bf16[3,128,4096]{2,1,0:T(8,128)(2,1)}, f32[8,4096]{1,0:T(8,128)}, bf16[512,512]{1,0:T(8,128)(2,1)}, /*index=5*/f32[4,2,256,128]{3,2,1,0:T(8,128)}) custom-call(s32[1,4]{1,0:T(1,128)} %len_ref.3, bf16[512,5120]{1,0:T(8,128)(2,1)} %bitcast.13, bf16[512,5120]{1,0:T(8,128)(2,1)} %bitcast.14, ...), custom_call_target="tpu_custom_call" | custom-call | tf_op jit(solution)/shard_map/local_pass/pallas_call | solution.py:352
  44.5 38.8 %exchange.1 = (bf16[128,4096]{1,0:T(8,128)(2,1)}, f32[4,128,256]{2,1,0:T(8,128)}) custom-call(bf16[128,4096]{1,0:T(8,128)(2,1)} %get-tuple-element.19.st_ref, f32[8,4096]{1,0:T(8,128)} %get-tuple-element.20.aux_ref), custom_call_target="tpu_custom_call" | custom-call | tf_op jit(solution)/shard_map/exchange/pallas_call | solution.py:499
  83.3 11.7 %finish.1 = (bf16[512,4096]{1,0:T(8,128)(2,1)}, f32[16,8,128]{2,1,0:T(8,128)}) custom-call(s32[1,4]{1,0:T(1,128)} %len_ref.3, f32[512,4096]{1,0:T(8,128)} %get-tuple-element.17.y_ref, bf16[512,512]{1,0:T(8,128)(2,1)} %get-tuple-element.18.c_ref, bf16[128,4096]{1,0:T(8,128)(2,1)} %get-tuple-element.21.e_ref, f32[4,2,256,128]{3,2,1,0:T(8,128)} %get-tuple-element.22.ld_ref, ...), custom_call_target="tpu_custom_call" | custom-call | tf_op jit(solution)/shard_map/finish/pallas_call | solution.py:555
  95.0 57.0 %tail.1 = (bf16[1,4,4096]{2,1,0:T(4,128)(2,1)}, f32[1,4]{1,0:T(1,128)}, f32[4,256,128]{2,1,0:T(8,128)}) custom-call(f32[16,8,128]{2,1,0:T(8,128)} %get-tuple-element.24.rows_ref, bf16[32,4096]{1,0:T(8,128)(2,1)} %w_ref.1, bf16[3,128,4096]{2,1,0:T(8,128)(2,1)} %get-tuple-element.25.tails_ref, f32[4,128,256]{2,1,0:T(8,128)} %get-tuple-element.26.reach_ref, ...), custom_call_target="tpu_custom_call" | custom-call | tf_op jit(solution)/shard_map/tail/pallas_call | solution.py:959
  151.9 1.9 %copy.22 = f32[1,4,4,64,128]{4,3,2,1,0:T(8,128)} copy(f32[1,4,4,64,128]{4,3,2,1,0:T(8,128)} %bitcast.18) | data formatting | bytes 1048576
  153.8 1.4 copy.23
  155.2 1.1 copy.24
Async XLA Ops:
  1.5 6.1 %collective-permute-start = (bf16[8,5120]{1,0:T(8,128)(2,1)S(1)}, bf16[8,5120]{1,0:T(8,128)(2,1)S(1)}, u32[]{:S(2)}, u32[]{:S(2)}) collective-permute-start(bf16[8,5120]{1,0:T(8,128)(2,1)S(1)} %slice_bitcast_fusion), channel_id=1, source_target_pairs={{0,1},{1,2},{2,3},{3,4},{4,5},{5,6},{6,7},{7,8},{8,9},{9,10},{10,1... | collective-permute-start | bytes 245768 | tf_op jit(solution)/shard_map/ppermute | solution.py:1038
  7.6 0.6 copy-start

commit v5 on v4

--- a/solution.py
+++ b/solution.py
@@ -12,6 +12,7 @@
 CHANNEL_WIDTH = 64
 GROUPS = 4
 STATE = 128
+CHUNKS = [slice(c * 256, c * 256 + 256) for c in range(4)]
 KERNEL = 4
 BLOCK = 256
 SEQS = 4
@@ -57,13 +58,17 @@
     return jnp.where(hit, 1.0, 0.0).astype(BF16)
 
 
-def spread(v, spread_ref):
+def spread_parts(v):
     hi, mid, lo = split3(v)
     lane = lax.broadcasted_iota(jnp.int32, v.shape, 1)
     parts = jnp.where(
         lane < 16, hi.astype(F32), jnp.where(lane < 32, mid.astype(F32), lo.astype(F32))
     ).astype(BF16)
-    return dot(parts, spread_ref[...])
+    return parts
+
+
+def spread(v, spread_ref):
+    return dot(spread_parts(v), spread_ref[...])
 
 
 def halves(h):
@@ -120,6 +125,7 @@
     lds,
     dxs,
     wst,
+    ow,
 ):
     g = pl.program_id(0)
     j = pl.program_id(1)
@@ -150,7 +156,7 @@
         s_seg = seg_of(i1 + start, b1, b2, b3)
         alw[j] = ((i0 >= i1) & (t_seg == s_seg)).astype(F32)
         tri = jnp.where(i0 >= i1, 1.0, 0.0).astype(BF16)
-        dt = softplus(raw_ref[...] + bias_ref[...])
+        dt = softplus(raw_ref[...].T + bias_ref[...])
         dh, dm, dl = split3(dt * (jnp.exp(log_ref[...]) * -LOG2E))
         cums[j] = (dot(tri, dl) + dot(tri, dm)) + dot(tri, dh)
         lds[j] = jnp.log(dt) * LOG2E
@@ -236,7 +242,9 @@
     def _():
         lead = jnp.where(seg == seg_before, jnp.exp2(cum), 0.0)
         sh, sl = split2(s0[...])
-        y_ref[...] = spread(lead, sp) * (dot(cb, sh) + dot(cb, sl))
+        parts = spread_parts(lead)
+        for cols in CHUNKS:
+            y_ref[:, cols] = dot(parts, sp[:, cols]) * (dot(cb, sh[:, cols]) + dot(cb, sl[:, cols]))
 
     lane = lax.broadcasted_iota(jnp.int32, (BLOCK, 128), 1)
     half = BLOCK // 2
@@ -260,17 +268,22 @@
         intra = jnp.where(lane < CHANNEL_WIDTH, res[0], res[1])
         y_ref[:, cols] = y_ref[:, cols] + (intra + dxs[0:1, cols] * xb.astype(F32))
 
-    bht, blt = split2(bf.T)
-
-    def state_of(weights):
-        xs = xf[:, 0:GW] * spread(weights, sp)
-        xs_h, xs_l = split2(xs)
-        return dot(bht, xs_h) + (dot(blt, xs_h) + dot(bht, xs_l))
+    both = jnp.concatenate(split2(bf.T), axis=0)
+
+    def state_of(weights, put):
+        parts = spread_parts(weights)
+        for cols in CHUNKS:
+            xs = (xf[:, cols] * dot(parts, sp[:, cols])).astype(BF16)
+            two = dot(both, xs)
+            put(cols, two[:STATE] + two[STATE:])
 
     def at_end(seg_e):
         return jnp.where(seg == seg_e, jnp.exp2(last - cum + logdt), 0.0)
 
-    own = state_of(at_end(seg_end))
+    def put_own(cols, value):
+        ow[:, cols] = value
+
+    state_of(at_end(seg_end), put_own)
 
     for r in range(SEQS - 1):
         end = bounds[r] - 1
@@ -283,17 +296,19 @@
             inside = (row <= end) & (seg == r)
             w = jnp.exp2(jnp.where(inside, ce - cum + logdt, -1e30))
             reach = jnp.where(seg_before == r, jnp.exp2(ce), 0.0)
-            tail = state_of(w)
-            keep = jnp.where(j == 1, 1.0, 0.0)
-            reach8 = spread(jnp.broadcast_to(reach * keep, (8, 128)), sp)
-            tail = tail + jnp.where(j == 1, reach8[0:1] * s0[...], 0.0)
-            pt_ref[r] = tail.astype(BF16)
+            reach8 = spread(jnp.broadcast_to(reach, (8, 128)), sp)
+
+            def put_tail(cols, value):
+                before = jnp.where(j == 1, reach8[0:1, cols] * s0[:, cols], 0.0)
+                pt_ref[r, :, cols] = (value + before).astype(BF16)
+
+            state_of(w, put_tail)
             full = jnp.where(seg_before_span == r, jnp.exp2(ce + prior), 0.0)
             aux_ref[1 + r : 2 + r, :] = spread(jnp.broadcast_to(full, (8, 128)), sp)[0:1]
 
     @pl.when(j == 0)
     def _():
-        s0[...] = own
+        s0[...] = ow[...]
         c0[...] = jnp.broadcast_to(last, c0.shape)
 
     @pl.when(j == 1)
@@ -302,7 +317,7 @@
         whole = jnp.where(seg_end == seg_before_span, jnp.exp2(last + prior), 0.0)
         carry8 = spread(jnp.broadcast_to(carry, (8, 128)), sp)
         whole8 = spread(jnp.broadcast_to(whole, (8, 128)), sp)
-        st_ref[...] = (carry8[0:1] * s0[...] + own).astype(BF16)
+        st_ref[...] = (carry8[0:1] * s0[...] + ow[...]).astype(BF16)
         aux_ref[0:1, :] = whole8[0:1]
 
 
@@ -327,7 +342,7 @@
         + xs(KERNEL)
         + xs(1)
         + [
-            pl.BlockSpec((BLOCK, HEADS), lambda g, j: (j, 0)),
+            pl.BlockSpec((HEADS, BLOCK), lambda g, j: (0, j)),
             pl.BlockSpec((1, HEADS), lambda g, j: (0, 0)),
             pl.BlockSpec((1, HEADS), lambda g, j: (0, 0)),
             pl.BlockSpec((1, HEADS), lambda g, j: (0, 0)),
@@ -369,6 +384,7 @@
             pltpu.VMEM((blocks, BLOCK, HEADS), F32),
             pltpu.VMEM((8, GW), F32),
             pltpu.VMEM((8, GW + 256), F32),
+            pltpu.VMEM((STATE, GW), F32),
         ],
         compiler_params=pltpu.CompilerParams(
             vmem_limit_bytes=VMEM_LIMIT, dimension_semantics=("arbitrary", "arbitrary")
@@ -452,30 +468,27 @@
     rs[me] = st_ref[:, cols(me)]
     ra[me] = aux_ref[:, cols(me)]
 
-    def arrive(i, _):
-        for copy in out(peer(i), peer(i)):
-            copy.wait_recv()
-        return 0
-
-    lax.fori_loop(1, n, arrive, 0)
-
     fin_ref[...] = jnp.zeros_like(fin_ref)
 
     def scan(d, _):
+        @pl.when(d != me)
+        def _():
+            for copy in out(d, d):
+                copy.wait_recv()
+
         now = fin_ref[SEQS - 1]
         eb[d] = now.astype(BF16)
+
+        @pl.when(d != me)
+        def _():
+            back(d, me).start()
+
         for r in range(SEQS - 1):
             fin_ref[r] = fin_ref[r] + ra[d, 1 + r : 2 + r, :] * now
         fin_ref[SEQS - 1] = ra[d, 0:1, :] * now + rs[d].astype(F32)
         return 0
 
     lax.fori_loop(0, n, scan, 0)
-
-    def reply(i, _):
-        back(peer(i), me).start()
-        return 0
-
-    lax.fori_loop(1, n, reply, 0)
     ent_ref[:, cols(me)] = eb[me]
 
     def done(i, _):
@@ -517,7 +530,7 @@
     )(states, aux)
 
 
-def finish_kernel(len_ref, y_ref, c_ref, e_ref, ld_ref, gate_ref, nw_ref, out_ref, rows_ref, sp, of):
+def finish_kernel(len_ref, y_ref, c_ref, e_ref, ld_ref, gate_ref, nw_ref, out_ref, rows_ref, sp, of, scales):
     g = pl.program_id(0)
     j = pl.program_id(1)
 
@@ -529,13 +542,20 @@
     def _():
         rows_ref[...] = jnp.zeros_like(rows_ref)
 
-    v = y_ref[...] + spread(ld_ref[0, 0], sp) * dot(c_ref[...], e_ref[...])
-    v = v * halves(0.5 * gate_ref[...].astype(F32))
-    scale = lax.rsqrt(jnp.mean(v * v, axis=1, keepdims=True) + TINY_FLOOR)
-    out = (v * scale * nw_ref[...]).astype(BF16)
-    out_ref[...] = out
-
-    of[...] = out.astype(F32)
+    parts = spread_parts(ld_ref[0, 0])
+    half = BLOCK // 2
+    for lines in (slice(0, half), slice(half, BLOCK)):
+        total = jnp.zeros((half, 128), F32)
+        for cols in CHUNKS:
+            v = y_ref[lines, cols] + dot(parts[lines], sp[:, cols]) * dot(c_ref[lines, :], e_ref[:, cols])
+            v = v * halves(0.5 * gate_ref[lines, cols].astype(F32))
+            of[lines, cols] = v
+            total = total + v[:, :128] * v[:, :128] + v[:, 128:] * v[:, 128:]
+        scale = lax.rsqrt(jnp.sum(total, axis=1, keepdims=True) * (1.0 / GW) + TINY_FLOOR)
+        scales[lines, :] = jnp.broadcast_to(scale, (half, 128))
+        for cols in CHUNKS:
+            out_ref[lines, cols] = (of[lines, cols] * scale * nw_ref[:, cols]).astype(BF16)
+
     start = lax.axis_index("seq") * (pl.num_programs(1) * BLOCK) + j * BLOCK
     bounds = bounds_of(len_ref)
     for r, bound in enumerate(bounds + (bounds[2] + len_ref[0, 3],)):
@@ -543,7 +563,9 @@
 
         @pl.when((local >= 0) & (local < BLOCK))
         def _():
-            line = of[pl.ds(jnp.clip(local, 0, BLOCK - 1), 1), :]
+            spot = jnp.clip(local, 0, BLOCK - 1)
+            line = of[pl.ds(spot, 1), :] * scales[pl.ds(spot, 1), :][:, 0:1] * nw_ref[...]
+            line = line.astype(BF16).astype(F32)
             for c in range(GW // 128):
                 place = c % 2 * SEQS + r
                 rows_ref[c // 2, place : place + 1, :] = line[:, c * 128 : c * 128 + 128]
@@ -569,7 +591,11 @@
             jax.ShapeDtypeStruct((length, D), BF16),
             jax.ShapeDtypeStruct((D // 256, 8, 128), F32),
         ],
-        scratch_shapes=[pltpu.VMEM((128, GW), BF16), pltpu.VMEM((BLOCK, GW), F32)],
+        scratch_shapes=[
+            pltpu.VMEM((128, GW), BF16),
+            pltpu.VMEM((BLOCK, GW), F32),
+            pltpu.VMEM((BLOCK, 128), F32),
+        ],
         compiler_params=pltpu.CompilerParams(
             vmem_limit_bytes=VMEM_LIMIT, dimension_semantics=("arbitrary", "arbitrary")
         ),
@@ -924,8 +950,8 @@
         p4[v] = p4[v] + p3[v, 0]
     for r in range(SEQS - 1):
         share = jnp.concatenate([p4[v, r].astype(F32) for v in range(4)], axis=0)
-        fin_ref[r] = (reach_ref[r] + share).T
-    fin_ref[SEQS - 1] = reach_ref[SEQS - 1].T
+        fin_ref[r] = reach_ref[r] + share
+    fin_ref[SEQS - 1] = reach_ref[SEQS - 1]
     m2_in()
     best = jnp.max(mx2[...], axis=0)[0:1]
     lanes = lax.broadcasted_iota(jnp.int32, (1, 128), 1)
@@ -963,7 +989,7 @@
         out_shape=[
             jax.ShapeDtypeStruct((1, SEQS, D), BF16),
             jax.ShapeDtypeStruct((1, SEQS), F32),
-            jax.ShapeDtypeStruct((SEQS, width, STATE), F32),
+            jax.ShapeDtypeStruct((SEQS, STATE, width), F32),
         ],
         scratch_shapes=[
             pltpu.VMEM(vocab.shape, BF16),
@@ -1014,6 +1040,28 @@
     )(rows, out_weight, tails, reached, resid, gain, vocab)
 
 
+def pack_kernel(fin_ref, hid_ref, top_ref, fin_out, hid_out, top_out):
+    for r in range(SEQS):
+        fin_out[r] = fin_ref[r].T
+    hid_out[...] = hid_ref[...]
+    top_out[...] = top_ref[...]
+
+
+def pack(final, hid, top):
+    vmem = pl.BlockSpec(memory_space=pltpu.VMEM)
+    return pl.pallas_call(
+        pack_kernel,
+        in_specs=[vmem] * 3,
+        out_specs=[vmem] * 3,
+        out_shape=[
+            jax.ShapeDtypeStruct((final.shape[0], final.shape[2], final.shape[1]), F32),
+            jax.ShapeDtypeStruct(hid.shape, BF16),
+            jax.ShapeDtypeStruct(top.shape, F32),
+        ],
+        name="pack",
+    )(final, hid, top)
+
+
 def body(
     conv_input,
     gate_projected,
@@ -1042,7 +1090,7 @@
         halo,
         conv_weight,
         convolution_bias[None],
-        step_raw[0],
+        step_raw[0].T,
         step_bias[None],
         decay_log[None],
         head_direct_gain[None],
@@ -1052,6 +1100,7 @@
     hid, top, final = tail(
         rows, out_weight, tails, reached, residual_last, final_gain[None], vocab_weight, seq_count, req_count
     )
+    final, hid, top = pack(final, hid, top)
     final_states = final.reshape(SEQS, HEADS // seq_count, CHANNEL_WIDTH, STATE)[None]
     return (gated[None], final_states, hid, top)
 

time: 157 us -> 155 us (0.987)
  local copies, waits for them, and re-layouts: 7.67 us -> 1.53 us
  Pallas kernels: 144 us -> 147 us
    unnamed x6 -> x2, local copies, waits for them, and re-layouts: 6.77 us -> 0.63 us
    pallas_call x1, Pallas kernels: 57 us -> 62.8 us  [tail(): pl.pallas_call(functools.partial(tail_kernel, n, m), in_specs=[vmem] * 6...]
    pallas_call x1, Pallas kernels: 38.8 us -> 35.4 us  [exchange(): pl.pallas_call(functools.partial(exchange_kernel, n), in_specs=[vmem, vme...]
    pallas_call x0 -> x1, Pallas kernels: none -> 2.06 us  [pack(): pl.pallas_call(pack_kernel, in_specs=[vmem] * 3, out_specs=[vmem] * 3, ou...]
  transfers between devices with their start and end apart: 1 -> 1, of which waited for: 0 -> 1; matrix products, arithmetic and copies ran while one was open for 1% -> 0% of each run, Pallas kernels for 0% -> 0%
where the time goes in v5:
time: 155 us
  Pallas kernels  147 us (95%)
  starting transfers between devices  4.35 us (3%)
    pallas_call x1, Pallas kernels, tail(): pl.pallas_call(functools.partial(tail_kernel, n, m), in_specs=[vmem] * 6...  62.8 us
    pallas_call x1, Pallas kernels, exchange(): pl.pallas_call(functools.partial(exchange_kernel, n), in_specs=[vmem, vme...  35.4 us
    pallas_call x1, Pallas kernels, local_pass(): pl.pallas_call(local_kernel, grid=grid, in_specs=in_specs, out_specs=out_...  35.1 us
    pallas_call x1, Pallas kernels, finish(): pl.pallas_call(finish_kernel, grid=(GROUPS, length // BLOCK), in_specs=[p...  11.6 us
    ppermute x1, starting transfers between devices, body(): halo = lax.ppermute(conv[local_len - 8:], 'seq', route)  4.35 us
  transfers between devices with their start and end apart: 1, of which 1 were waited for; matrix products, arithmetic and copies ran while one was open for 0% of the time, Pallas kernels for 0%

profile of v5, /device:TPU:1, one launch (start us, length us, event | category | flops | bytes accessed | tf_op | source)
XLA Modules:
  0.0 154.9 jit_solution(1254862969527726405)
XLA Ops:
  0.6 0.9 slice_bitcast_fusion
  1.5 4.4 %collective-permute-start = (bf16[8,5120]{1,0:T(8,128)(2,1)S(1)}, bf16[8,5120]{1,0:T(8,128)(2,1)S(1)}, u32[]{:S(2)}, u32[]{:S(2)}) collective-permute-start(bf16[8,5120]{1,0:T(8,128)(2,1)S(1)} %slice_bitcast_fusion), channel_id=1, source_target_pairs={{0,1},{1,2},{2,3},{3,4},{4,5},{5,6},{6,7},{7,8},{8,9},{9,10},{10,1... | collective-permute-start | bytes 245768 | tf_op jit(solution)/shard_map/ppermute | solution.py:1086
  5.9 1.5 collective-permute-done.xh_ref.bh_ref.ch_ref
  7.3 0.0 copy-start
  7.4 0.6 copy-done
  8.0 35.1 %local_pass.1 = (f32[512,4096]{1,0:T(8,128)}, bf16[128,4096]{1,0:T(8,128)(2,1)}, bf16[3,128,4096]{2,1,0:T(8,128)(2,1)}, f32[8,4096]{1,0:T(8,128)}, bf16[512,512]{1,0:T(8,128)(2,1)}, /*index=5*/f32[4,2,256,128]{3,2,1,0:T(8,128)}) custom-call(s32[1,4]{1,0:T(1,128)} %len_ref.3, bf16[512,5120]{1,0:T(8,128)(2,1)} %bitcast.15, bf16[512,5120]{1,0:T(8,128)(2,1)} %bitcast.16, ...), custom_call_target="tpu_custom_call" | custom-call | tf_op jit(solution)/shard_map/local_pass/pallas_call | solution.py:367
  43.1 35.4 %exchange.1 = (bf16[128,4096]{1,0:T(8,128)(2,1)}, f32[4,128,256]{2,1,0:T(8,128)}) custom-call(bf16[128,4096]{1,0:T(8,128)(2,1)} %get-tuple-element.22.st_ref, f32[8,4096]{1,0:T(8,128)} %get-tuple-element.23.aux_ref), custom_call_target="tpu_custom_call" | custom-call | tf_op jit(solution)/shard_map/exchange/pallas_call | solution.py:512
  78.5 11.6 %finish.1 = (bf16[512,4096]{1,0:T(8,128)(2,1)}, f32[16,8,128]{2,1,0:T(8,128)}) custom-call(s32[1,4]{1,0:T(1,128)} %len_ref.3, f32[512,4096]{1,0:T(8,128)} %get-tuple-element.20.y_ref, bf16[512,512]{1,0:T(8,128)(2,1)} %get-tuple-element.21.c_ref, bf16[128,4096]{1,0:T(8,128)(2,1)} %get-tuple-element.24.e_ref, f32[4,2,256,128]{3,2,1,0:T(8,128)} %get-tuple-element.25.ld_ref, ...), custom_call_target="tpu_custom_call" | custom-call | tf_op jit(solution)/shard_map/finish/pallas_call | solution.py:577
  90.1 62.8 %tail.1 = (bf16[1,4,4096]{2,1,0:T(4,128)(2,1)}, f32[1,4]{1,0:T(1,128)}, f32[4,128,256]{2,1,0:T(8,128)}) custom-call(f32[16,8,128]{2,1,0:T(8,128)} %get-tuple-element.27.rows_ref, bf16[32,4096]{1,0:T(8,128)(2,1)} %w_ref.1, bf16[3,128,4096]{2,1,0:T(8,128)(2,1)} %get-tuple-element.28.tails_ref, f32[4,128,256]{2,1,0:T(8,128)} %get-tuple-element.29.reach_ref, ...), custom_call_target="tpu_custom_call" | custom-call | tf_op jit(solution)/shard_map/tail/pallas_call | solution.py:985
  152.8 2.1 %pack.1 = (f32[4,256,128]{2,1,0:T(8,128)}, bf16[1,4,4096]{2,1,0:T(4,128)(2,1)}, f32[1,4]{1,0:T(1,128)}) custom-call(f32[4,128,256]{2,1,0:T(8,128)} %get-tuple-element.30.fin_ref, bf16[1,4,4096]{2,1,0:T(4,128)(2,1)} %get-tuple-element.31.hid_ref, f32[1,4]{1,0:T(1,128)} %get-tuple-element.32.top_ref), custom_call_target="tpu_custom_call" | custom-call | tf_op jit(solution)/shard_map/pack/pallas_call | solution.py:1052
Async XLA Ops:
  1.5 5.8 %collective-permute-start = (bf16[8,5120]{1,0:T(8,128)(2,1)S(1)}, bf16[8,5120]{1,0:T(8,128)(2,1)S(1)}, u32[]{:S(2)}, u32[]{:S(2)}) collective-permute-start(bf16[8,5120]{1,0:T(8,128)(2,1)S(1)} %slice_bitcast_fusion), channel_id=1, source_target_pairs={{0,1},{1,2},{2,3},{3,4},{4,5},{5,6},{6,7},{7,8},{8,9},{9,10},{10,1... | collective-permute-start | bytes 245768 | tf_op jit(solution)/shard_map/ppermute | solution.py:1086
  7.3 0.6 copy-start

commit v6 on v5

--- a/solution.py
+++ b/solution.py
@@ -396,6 +396,45 @@
     )
 
 
+def halo_kernel(n, conv_ref, out_ref, got, send, recv):
+    me = lax.axis_index("seq")
+    right = lax.rem(me + 1, n)
+    left = lax.rem(me + n - 1, n)
+    barrier = pltpu.get_barrier_semaphore()
+    for p in (left, right):
+        pl.semaphore_signal(barrier, inc=1, device_id={"seq": p}, device_id_type=MESH)
+    pl.semaphore_wait(barrier, 2)
+    copy = pltpu.make_async_remote_copy(
+        src_ref=conv_ref.at[pl.ds(conv_ref.shape[0] - 8, 8), :],
+        dst_ref=got,
+        send_sem=send,
+        recv_sem=recv,
+        device_id={"seq": right},
+        device_id_type=MESH,
+    )
+    copy.start()
+    copy.wait()
+    keep = jnp.where(me == 0, 0.0, 1.0)
+    out_ref[...] = (got[...].astype(F32) * keep).astype(BF16)
+
+
+def halo_rows(conv, n):
+    shape = (8, conv.shape[1])
+    return pl.pallas_call(
+        functools.partial(halo_kernel, n),
+        in_specs=[pl.BlockSpec(memory_space=pl.ANY)],
+        out_specs=pl.BlockSpec(memory_space=pltpu.VMEM),
+        out_shape=jax.ShapeDtypeStruct(shape, BF16),
+        scratch_shapes=[
+            pltpu.VMEM(shape, BF16),
+            pltpu.SemaphoreType.DMA,
+            pltpu.SemaphoreType.DMA,
+        ],
+        compiler_params=pltpu.CompilerParams(collective_id=2, has_side_effects=True),
+        name="halo",
+    )(conv)
+
+
 def exchange_kernel(
     n,
     st_ref,
@@ -1078,12 +1117,10 @@
     final_gain,
     vocab_weight,
 ):
-    local_len = conv_input.shape[1]
     seq_count = lax.axis_size("seq")
     req_count = lax.axis_size("req")
     conv = conv_input[0]
-    route = [(i, i + 1) for i in range(seq_count - 1)]
-    halo = lax.ppermute(conv[local_len - 8 :], "seq", route)
+    halo = halo_rows(conv, seq_count)
     y, states, tails, aux, c, lead = local_pass(
         lengths,
         conv,

time: 155 us -> 153 us (0.987)
  Pallas kernels: 147 us -> 152 us
  starting transfers between devices: 4.35 us -> 0 us
    pallas_call x0 -> x1, Pallas kernels: none -> 9.94 us  [halo_rows(): pl.pallas_call(functools.partial(halo_kernel, n), in_specs=[pl.BlockSpec(...]
    pallas_call x1, Pallas kernels: 62.8 us -> 57.4 us  [tail(): pl.pallas_call(functools.partial(tail_kernel, n, m), in_specs=[vmem] * 6...]
    ppermute x1 -> x0, starting transfers between devices: 4.35 us -> none  [body(): halo = lax.ppermute(conv[local_len - 8:], 'seq', route)]
  transfers between devices with their start and end apart: 1 -> 0, of which waited for: 1 -> 0; matrix products, arithmetic and copies ran while one was open for 0% -> 0% of each run, Pallas kernels for 0% -> 0%
where the time goes in v6:
time: 153 us
  Pallas kernels  152 us (99%)
    pallas_call x1, Pallas kernels, tail(): pl.pallas_call(functools.partial(tail_kernel, n, m), in_specs=[vmem] * 6...  57.4 us
    pallas_call x1, Pallas kernels, exchange(): pl.pallas_call(functools.partial(exchange_kernel, n), in_specs=[vmem, vme...  35.8 us
    pallas_call x1, Pallas kernels, local_pass(): pl.pallas_call(local_kernel, grid=grid, in_specs=in_specs, out_specs=out_...  35.1 us
    pallas_call x1, Pallas kernels, finish(): pl.pallas_call(finish_kernel, grid=(GROUPS, length // BLOCK), in_specs=[p...  11.6 us
    pallas_call x1, Pallas kernels, halo_rows(): pl.pallas_call(functools.partial(halo_kernel, n), in_specs=[pl.BlockSpec(...  9.94 us

profile of v6, /device:TPU:1, one launch (start us, length us, event | category | flops | bytes accessed | tf_op | source)
XLA Modules:
  0.0 152.5 jit_solution(5191286114904860737)
XLA Ops:
  0.6 9.9 %halo.1.xh_ref.bh_ref.ch_ref = bf16[8,5120]{1,0:T(8,128)(2,1)} custom-call(bf16[512,5120]{1,0:T(8,128)(2,1)} %bitcast.13), custom_call_target="tpu_custom_call" | custom-call | tf_op jit(solution)/shard_map/halo/pallas_call | solution.py:423
  10.6 35.1 %local_pass.1 = (f32[512,4096]{1,0:T(8,128)}, bf16[128,4096]{1,0:T(8,128)(2,1)}, bf16[3,128,4096]{2,1,0:T(8,128)(2,1)}, f32[8,4096]{1,0:T(8,128)}, bf16[512,512]{1,0:T(8,128)(2,1)}, /*index=5*/f32[4,2,256,128]{3,2,1,0:T(8,128)}) custom-call(s32[1,4]{1,0:T(1,128)} %len_ref.3, bf16[512,5120]{1,0:T(8,128)(2,1)} %bitcast.14, bf16[512,5120]{1,0:T(8,128)(2,1)} %bitcast.15, ...), custom_call_target="tpu_custom_call" | custom-call | tf_op jit(solution)/shard_map/local_pass/pallas_call | solution.py:367
  45.6 35.8 %exchange.1 = (bf16[128,4096]{1,0:T(8,128)(2,1)}, f32[4,128,256]{2,1,0:T(8,128)}) custom-call(bf16[128,4096]{1,0:T(8,128)(2,1)} %get-tuple-element.22.st_ref, f32[8,4096]{1,0:T(8,128)} %get-tuple-element.23.aux_ref), custom_call_target="tpu_custom_call" | custom-call | tf_op jit(solution)/shard_map/exchange/pallas_call | solution.py:551
  81.4 11.6 %finish.1 = (bf16[512,4096]{1,0:T(8,128)(2,1)}, f32[16,8,128]{2,1,0:T(8,128)}) custom-call(s32[1,4]{1,0:T(1,128)} %len_ref.3, f32[512,4096]{1,0:T(8,128)} %get-tuple-element.20.y_ref, bf16[512,512]{1,0:T(8,128)(2,1)} %get-tuple-element.21.c_ref, bf16[128,4096]{1,0:T(8,128)(2,1)} %get-tuple-element.24.e_ref, f32[4,2,256,128]{3,2,1,0:T(8,128)} %get-tuple-element.25.ld_ref, ...), custom_call_target="tpu_custom_call" | custom-call | tf_op jit(solution)/shard_map/finish/pallas_call | solution.py:616
  93.1 57.4 %tail.1 = (bf16[1,4,4096]{2,1,0:T(4,128)(2,1)}, f32[1,4]{1,0:T(1,128)}, f32[4,128,256]{2,1,0:T(8,128)}) custom-call(f32[16,8,128]{2,1,0:T(8,128)} %get-tuple-element.27.rows_ref, bf16[32,4096]{1,0:T(8,128)(2,1)} %w_ref.1, bf16[3,128,4096]{2,1,0:T(8,128)(2,1)} %get-tuple-element.28.tails_ref, f32[4,128,256]{2,1,0:T(8,128)} %get-tuple-element.29.reach_ref, ...), custom_call_target="tpu_custom_call" | custom-call | tf_op jit(solution)/shard_map/tail/pallas_call | solution.py:1024
  150.4 2.1 %pack.1 = (f32[4,256,128]{2,1,0:T(8,128)}, bf16[1,4,4096]{2,1,0:T(4,128)(2,1)}, f32[1,4]{1,0:T(1,128)}) custom-call(f32[4,128,256]{2,1,0:T(8,128)} %get-tuple-element.30.fin_ref, bf16[1,4,4096]{2,1,0:T(4,128)(2,1)} %get-tuple-element.31.hid_ref, f32[1,4]{1,0:T(1,128)} %get-tuple-element.32.top_ref), custom_call_target="tpu_custom_call" | custom-call | tf_op jit(solution)/shard_map/pack/pallas_call | solution.py:1091

commit v7 on v6

--- a/solution.py
+++ b/solution.py
@@ -112,6 +112,11 @@
     aux_ref,
     co_ref,
     ld_ref,
+    xb_ref,
+    sc_ref,
+    cum_ref,
+    rt_ref,
+    dx_ref,
     xext,
     xf,
     s0,
@@ -123,7 +128,6 @@
     sgs,
     cums,
     lds,
-    dxs,
     wst,
     ow,
 ):
@@ -187,7 +191,7 @@
         pt_ref[...] = jnp.zeros_like(pt_ref)
         aux_ref[...] = jnp.zeros_like(aux_ref)
         c0[...] = jnp.zeros_like(c0)
-        dxs[...] = spread(group(jnp.broadcast_to(gain_ref[...], (8, HEADS))), sp)
+        dx_ref[...] = spread(group(jnp.broadcast_to(gain_ref[...], (8, HEADS))), sp)
 
     @pl.when(j == 1)
     def _():
@@ -234,9 +238,10 @@
     bh, bl = split2(bf)
     sc = dot_nt(cb, bh) * alw[j]
 
-    @pl.when(j == 0)
-    def _():
-        y_ref[...] = jnp.zeros_like(y_ref)
+    xb_ref[0] = xf[:, 0:GW].astype(BF16)
+    sc_ref[0] = sc
+    cum_ref[0] = cum
+    rt_ref[0] = rt
 
     @pl.when(j == 1)
     def _():
@@ -245,28 +250,6 @@
         parts = spread_parts(lead)
         for cols in CHUNKS:
             y_ref[:, cols] = dot(parts, sp[:, cols]) * (dot(cb, sh[:, cols]) + dot(cb, sl[:, cols]))
-
-    lane = lax.broadcasted_iota(jnp.int32, (BLOCK, 128), 1)
-    half = BLOCK // 2
-    sc_t = sc[:half, :half]
-    sc_l = sc[half:, :half]
-    sc_r = sc[half:, half:]
-    for pair in range(PER_GROUP // 2):
-        cols = slice(pair * 128, pair * 128 + 128)
-        xb = xf[:, cols].astype(BF16)
-        res = []
-        for h in (2 * pair, 2 * pair + 1):
-            col = cum[:, h : h + 1]
-            r = rt[h : h + 1, :]
-            top = jnp.exp2(jnp.minimum(col[:half] + r[:, :half], 100.0)) * sc_t
-            left = jnp.exp2(col[half:] + r[:, :half]) * sc_l
-            right = jnp.exp2(jnp.minimum(col[half:] + r[:, half:], 100.0)) * sc_r
-            bottom = jnp.concatenate([left.astype(BF16), right.astype(BF16)], axis=1)
-            res.append(
-                jnp.concatenate([dot(top.astype(BF16), xb[:half]), dot(bottom, xb)], axis=0)
-            )
-        intra = jnp.where(lane < CHANNEL_WIDTH, res[0], res[1])
-        y_ref[:, cols] = y_ref[:, cols] + (intra + dxs[0:1, cols] * xb.astype(F32))
 
     both = jnp.concatenate(split2(bf.T), axis=0)
 
@@ -348,21 +331,33 @@
             pl.BlockSpec((1, HEADS), lambda g, j: (0, 0)),
         ]
     )
+    each = lambda *shape: pl.BlockSpec((1,) + shape, lambda g, j: (g * blocks + j, 0, 0))
     out_specs = [
-        pl.BlockSpec((BLOCK, GW), lambda g, j: (j, g)),
+        pl.BlockSpec((BLOCK, GW), lambda g, j: (0, g)),
         pl.BlockSpec((STATE, GW), lambda g, j: (0, g)),
         pl.BlockSpec((SEQS - 1, STATE, GW), lambda g, j: (0, 0, g)),
         pl.BlockSpec((8, GW), lambda g, j: (0, g)),
         pl.BlockSpec((BLOCK, 128), lambda g, j: (j, g)),
         pl.BlockSpec((1, 1, BLOCK, 128), lambda g, j: (g, j, 0, 0)),
+        each(BLOCK, GW),
+        each(BLOCK, BLOCK),
+        each(BLOCK, 128),
+        each(PER_GROUP, BLOCK),
+        pl.BlockSpec((8, GW), lambda g, j: (0, g)),
     ]
+    steps = GROUPS * blocks
     out_shape = [
-        jax.ShapeDtypeStruct((length, D), F32),
+        jax.ShapeDtypeStruct((BLOCK, D), F32),
         jax.ShapeDtypeStruct((STATE, D), BF16),
         jax.ShapeDtypeStruct((SEQS - 1, STATE, D), BF16),
         jax.ShapeDtypeStruct((8, D), F32),
         jax.ShapeDtypeStruct((length, GROUPS * STATE), BF16),
         jax.ShapeDtypeStruct((GROUPS, blocks, BLOCK, 128), F32),
+        jax.ShapeDtypeStruct((steps, BLOCK, GW), BF16),
+        jax.ShapeDtypeStruct((steps, BLOCK, BLOCK), F32),
+        jax.ShapeDtypeStruct((steps, BLOCK, 128), F32),
+        jax.ShapeDtypeStruct((steps, PER_GROUP, BLOCK), F32),
+        jax.ShapeDtypeStruct((8, D), F32),
     ]
     return pl.pallas_call(
         local_kernel,
@@ -382,7 +377,6 @@
             pltpu.VMEM((blocks, BLOCK, 128), jnp.int32),
             pltpu.VMEM((blocks, BLOCK, HEADS), F32),
             pltpu.VMEM((blocks, BLOCK, HEADS), F32),
-            pltpu.VMEM((8, GW), F32),
             pltpu.VMEM((8, GW + 256), F32),
             pltpu.VMEM((STATE, GW), F32),
         ],
@@ -439,19 +433,47 @@
     n,
     st_ref,
     aux_ref,
+    dx_ref,
+    xb_ref,
+    sc_ref,
+    cum_ref,
+    rt_ref,
     ent_ref,
     fin_ref,
+    y_ref,
     rs,
     ra,
     eb,
+    xbv,
+    scv,
+    cumv,
+    rtv,
+    yv,
     send1,
     recv1,
     send2,
     recv2,
     send3,
     recv3,
+    lsem,
+    ysem,
 ):
     me = lax.axis_index("seq")
+    steps = xb_ref.shape[0]
+
+    def loads(k):
+        pairs = ((xb_ref, xbv), (sc_ref, scv), (cum_ref, cumv), (rt_ref, rtv))
+        return [pltpu.make_async_copy(a.at[k], v.at[k], lsem.at[k, i]) for i, (a, v) in enumerate(pairs)]
+
+    def store(k):
+        return pltpu.make_async_copy(yv.at[k], y_ref.at[k], ysem.at[k])
+
+    def fetch(k, _):
+        for copy in loads(k):
+            copy.start()
+        return 0
+
+    lax.fori_loop(0, steps, fetch, 0)
     width = D // n
     barrier = pltpu.get_barrier_semaphore()
 
@@ -507,6 +529,34 @@
     rs[me] = st_ref[:, cols(me)]
     ra[me] = aux_ref[:, cols(me)]
 
+    lane = lax.broadcasted_iota(jnp.int32, (BLOCK, 128), 1)
+    half = BLOCK // 2
+
+    def mix(k, _):
+        for copy in loads(k):
+            copy.wait()
+        sc_t = scv[k, :half, :half]
+        sc_l = scv[k, half:, :half]
+        sc_r = scv[k, half:, half:]
+        for pair in range(PER_GROUP // 2):
+            span = slice(pair * 128, pair * 128 + 128)
+            xb = xbv[k, :, span]
+            res = []
+            for h in (2 * pair, 2 * pair + 1):
+                col = cumv[k, :, h : h + 1]
+                r = rtv[k, h : h + 1, :]
+                top = jnp.exp2(jnp.minimum(col[:half] + r[:, :half], 100.0)) * sc_t
+                left = jnp.exp2(col[half:] + r[:, :half]) * sc_l
+                right = jnp.exp2(jnp.minimum(col[half:] + r[:, half:], 100.0)) * sc_r
+                bottom = jnp.concatenate([left.astype(BF16), right.astype(BF16)], axis=1)
+                res.append(jnp.concatenate([dot(top.astype(BF16), xb[:half]), dot(bottom, xb)], axis=0))
+            intra = jnp.where(lane < CHANNEL_WIDTH, res[0], res[1])
+            direct = dx_ref[0:1, pl.ds(pl.multiple_of(k // 2 * GW + pair * 128, 128), 128)]
+            yv[k, :, span] = intra + direct * xb.astype(F32)
+        store(k).start()
+        return 0
+
+    lax.fori_loop(0, steps, mix, 0)
     fin_ref[...] = jnp.zeros_like(fin_ref)
 
     def scan(d, _):
@@ -544,32 +594,47 @@
 
     lax.fori_loop(1, n, drain, 0)
 
-
-def exchange(states, aux, n):
+    def stored(k, _):
+        store(k).wait()
+        return 0
+
+    lax.fori_loop(0, steps, stored, 0)
+
+
+def exchange(states, aux, dx, xb, sc, cum, rt, n):
     width = D // n
+    steps = xb.shape[0]
+    far = pl.BlockSpec(memory_space=pl.ANY)
     vmem = pl.BlockSpec(memory_space=pltpu.VMEM)
     return pl.pallas_call(
         functools.partial(exchange_kernel, n),
-        in_specs=[vmem, vmem],
-        out_specs=[vmem, vmem],
+        in_specs=[vmem] * 3 + [far] * 4,
+        out_specs=[vmem, vmem, far],
         out_shape=[
             jax.ShapeDtypeStruct((STATE, D), BF16),
             jax.ShapeDtypeStruct((SEQS, STATE, width), F32),
+            jax.ShapeDtypeStruct((steps, BLOCK, GW), F32),
         ],
         scratch_shapes=[
             pltpu.VMEM((n, STATE, width), BF16),
             pltpu.VMEM((n, 8, width), F32),
             pltpu.VMEM((n, STATE, width), BF16),
+            pltpu.VMEM(xb.shape, BF16),
+            pltpu.VMEM(sc.shape, F32),
+            pltpu.VMEM(cum.shape, F32),
+            pltpu.VMEM(rt.shape, F32),
+            pltpu.VMEM((steps, BLOCK, GW), F32),
         ]
-        + [pltpu.SemaphoreType.DMA((n,)) for _ in range(6)],
+        + [pltpu.SemaphoreType.DMA((n,)) for _ in range(6)]
+        + [pltpu.SemaphoreType.DMA((steps, 4)), pltpu.SemaphoreType.DMA((steps,))],
         compiler_params=pltpu.CompilerParams(
             collective_id=0, has_side_effects=True, vmem_limit_bytes=VMEM_LIMIT
         ),
         name="exchange",
-    )(states, aux)
-
-
-def finish_kernel(len_ref, y_ref, c_ref, e_ref, ld_ref, gate_ref, nw_ref, out_ref, rows_ref, sp, of, scales):
+    )(states, aux, dx, xb, sc, cum, rt)
+
+
+def finish_kernel(len_ref, y_ref, yb_ref, c_ref, e_ref, ld_ref, gate_ref, nw_ref, out_ref, rows_ref, sp, of, scales):
     g = pl.program_id(0)
     j = pl.program_id(1)
 
@@ -582,11 +647,13 @@
         rows_ref[...] = jnp.zeros_like(rows_ref)
 
     parts = spread_parts(ld_ref[0, 0])
+    later = (j > 0).astype(F32)
     half = BLOCK // 2
     for lines in (slice(0, half), slice(half, BLOCK)):
         total = jnp.zeros((half, 128), F32)
         for cols in CHUNKS:
-            v = y_ref[lines, cols] + dot(parts[lines], sp[:, cols]) * dot(c_ref[lines, :], e_ref[:, cols])
+            v = y_ref[0, lines, cols] + later * yb_ref[lines, cols]
+            v = v + dot(parts[lines], sp[:, cols]) * dot(c_ref[lines, :], e_ref[:, cols])
             v = v * halves(0.5 * gate_ref[lines, cols].astype(F32))
             of[lines, cols] = v
             total = total + v[:, :128] * v[:, :128] + v[:, 128:] * v[:, 128:]
@@ -610,15 +677,17 @@
                 rows_ref[c // 2, place : place + 1, :] = line[:, c * 128 : c * 128 + 128]
 
 
-def finish(lengths, y, c, entering, lead, gate, norm_weight):
-    length = y.shape[0]
+def finish(lengths, y, yb, c, entering, lead, gate, norm_weight):
+    length = gate.shape[0]
+    blocks = length // BLOCK
     block = lambda width: pl.BlockSpec((BLOCK, width), lambda g, j: (j, g))
     return pl.pallas_call(
         finish_kernel,
         grid=(GROUPS, length // BLOCK),
         in_specs=[
             pl.BlockSpec(memory_space=pltpu.SMEM),
-            block(GW),
+            pl.BlockSpec((1, BLOCK, GW), lambda g, j: (g * blocks + j, 0, 0)),
+            pl.BlockSpec((BLOCK, GW), lambda g, j: (0, g)),
             block(STATE),
             pl.BlockSpec((STATE, GW), lambda g, j: (0, g)),
             pl.BlockSpec((1, 1, BLOCK, 128), lambda g, j: (g, j, 0, 0)),
@@ -639,7 +708,7 @@
             vmem_limit_bytes=VMEM_LIMIT, dimension_semantics=("arbitrary", "arbitrary")
         ),
         name="finish",
-    )(lengths, y, c, entering, lead, gate, norm_weight)
+    )(lengths, y, yb, c, entering, lead, gate, norm_weight)
 
 
 def tail_kernel(
@@ -1121,7 +1190,7 @@
     req_count = lax.axis_size("req")
     conv = conv_input[0]
     halo = halo_rows(conv, seq_count)
-    y, states, tails, aux, c, lead = local_pass(
+    yb, states, tails, aux, c, lead, xb, sc, cum, rt, dx = local_pass(
         lengths,
         conv,
         halo,
@@ -1132,8 +1201,8 @@
         decay_log[None],
         head_direct_gain[None],
     )
-    entering, reached = exchange(states, aux, seq_count)
-    gated, rows = finish(lengths, y, c, entering, lead, gate_projected[0], norm_weight[None])
+    entering, reached, y = exchange(states, aux, dx, xb, sc, cum, rt, seq_count)
+    gated, rows = finish(lengths, y, yb, c, entering, lead, gate_projected[0], norm_weight[None])
     hid, top, final = tail(
         rows, out_weight, tails, reached, residual_last, final_gain[None], vocab_weight, seq_count, req_count
     )

time: 153 us -> 153 us (level)
    pallas_call x1, Pallas kernels: 35.8 us -> 41.5 us  [exchange(): pl.pallas_call(functools.partial(exchange_kernel, n), in_specs=[vmem] * 3...]
    pallas_call x1, Pallas kernels: 35.1 us -> 29.9 us  [local_pass(): pl.pallas_call(local_kernel, grid=grid, in_specs=in_specs, out_specs=out_...]
    pallas_call x1, Pallas kernels: 57.4 us -> 55.6 us  [tail(): pl.pallas_call(functools.partial(tail_kernel, n, m), in_specs=[vmem] * 6...]
where the time goes in v7:
time: 153 us
  Pallas kernels  152 us (99%)
    pallas_call x1, Pallas kernels, tail(): pl.pallas_call(functools.partial(tail_kernel, n, m), in_specs=[vmem] * 6...  55.6 us
    pallas_call x1, Pallas kernels, exchange(): pl.pallas_call(functools.partial(exchange_kernel, n), in_specs=[vmem] * 3...  41.5 us
    pallas_call x1, Pallas kernels, local_pass(): pl.pallas_call(local_kernel, grid=grid, in_specs=in_specs, out_specs=out_...  29.9 us
    pallas_call x1, Pallas kernels, finish(): pl.pallas_call(finish_kernel, grid=(GROUPS, length // BLOCK), in_specs=[p...  13.1 us
    pallas_call x1, Pallas kernels, halo_rows(): pl.pallas_call(functools.partial(halo_kernel, n), in_specs=[pl.BlockSpec(...  9.93 us

profile of v7, /device:TPU:1, one launch (start us, length us, event | category | flops | bytes accessed | tf_op | source)
XLA Modules:
  0.0 152.7 jit_solution(7763887084317531788)
XLA Ops:
  0.6 9.9 %halo.1.xh_ref.bh_ref.ch_ref = bf16[8,5120]{1,0:T(8,128)(2,1)} custom-call(bf16[512,5120]{1,0:T(8,128)(2,1)} %bitcast.13), custom_call_target="tpu_custom_call" | custom-call | tf_op jit(solution)/shard_map/halo/pallas_call | solution.py:417
  10.6 29.9 %local_pass.1 = (f32[256,4096]{1,0:T(8,128)}, bf16[128,4096]{1,0:T(8,128)(2,1)}, bf16[3,128,4096]{2,1,0:T(8,128)(2,1)}, f32[8,4096]{1,0:T(8,128)}, bf16[512,512]...) custom-call(s32[1,4]{1,0:T(1,128)} %len_ref.3, ...), custom_call_target="tpu_custom_call" | custom-call | tf_op jit(solution)/shard_map/local_pass/pallas_call | solution.py:362
  40.4 41.5 %exchange.1 = (bf16[128,4096]{1,0:T(8,128)(2,1)}, f32[4,128,256]{2,1,0:T(8,128)}, f32[8,256,1024]{2,1,0:T(8,128)}) custom-call(bf16[128,4096]{1,0:T(8,128)(2,1)} %get-tuple-element.26.st_ref, f32[8,4096]{1,0:T(8,128)} %get-tuple-element.27.aux_ref, f32[8,4096]{1,0:T(8,128)} %get-tuple-element.28.dx_ref, bf16[8,256,1024]{2,1,0:T(8,128)(2,1)} %get-tuple-element.29.xb_ref, ...), custom_call_target="tpu_custom_call" | custom-call | tf_op jit(solution)/shard_map/exchange/pallas_call | solution.py:609
  82.0 13.1 %finish.1 = (bf16[512,4096]{1,0:T(8,128)(2,1)}, f32[16,8,128]{2,1,0:T(8,128)}) custom-call(s32[1,4]{1,0:T(1,128)} %len_ref.3, f32[8,256,1024]{2,1,0:T(8,128)} %get-tuple-element.33.y_ref, f32[256,4096]{1,0:T(8,128)} %get-tuple-element.34.yb_ref, bf16[512,512]{1,0:T(8,128)(2,1)} %get-tuple-element.35.c_ref, bf16[128,4096]{1,0:T(8,128)(2,1)} %get-tuple-element.36.e_ref, ...), custom_call_target="tpu_custom_call" | custom-call | tf_op jit(solution)/shard_map/finish/pallas_call | solution.py:684
  95.0 55.6 %tail.1 = (bf16[1,4,4096]{2,1,0:T(4,128)(2,1)}, f32[1,4]{1,0:T(1,128)}, f32[4,128,256]{2,1,0:T(8,128)}) custom-call(f32[16,8,128]{2,1,0:T(8,128)} %get-tuple-element.39.rows_ref, bf16[32,4096]{1,0:T(8,128)(2,1)} %w_ref.1, bf16[3,128,4096]{2,1,0:T(8,128)(2,1)} %get-tuple-element.40.tails_ref, f32[4,128,256]{2,1,0:T(8,128)} %get-tuple-element.41.reach_ref, ...), custom_call_target="tpu_custom_call" | custom-call | tf_op jit(solution)/shard_map/tail/pallas_call | solution.py:1093
  150.6 2.1 %pack.1 = (f32[4,256,128]{2,1,0:T(8,128)}, bf16[1,4,4096]{2,1,0:T(4,128)(2,1)}, f32[1,4]{1,0:T(1,128)}) custom-call(f32[4,128,256]{2,1,0:T(8,128)} %get-tuple-element.42.fin_ref, bf16[1,4,4096]{2,1,0:T(4,128)(2,1)} %get-tuple-element.43.hid_ref, f32[1,4]{1,0:T(1,128)} %get-tuple-element.44.top_ref), custom_call_target="tpu_custom_call" | custom-call | tf_op jit(solution)/shard_map/pack/pallas_call | solution.py:1160

commit v8 on v7

--- a/solution.py
+++ b/solution.py
@@ -106,7 +106,8 @@
     bias_ref,
     log_ref,
     gain_ref,
-    y_ref,
+    lp_ref,
+    sh_ref,
     st_ref,
     pt_ref,
     aux_ref,
@@ -162,12 +163,16 @@
         tri = jnp.where(i0 >= i1, 1.0, 0.0).astype(BF16)
         dt = softplus(raw_ref[...].T + bias_ref[...])
         dh, dm, dl = split3(dt * (jnp.exp(log_ref[...]) * -LOG2E))
-        cums[j] = (dot(tri, dl) + dot(tri, dm)) + dot(tri, dh)
-        lds[j] = jnp.log(dt) * LOG2E
-
-    l0 = lax.broadcasted_iota(jnp.int32, (HEADS, 128), 0)
-    l1 = lax.broadcasted_iota(jnp.int32, (HEADS, 128), 1)
-    pick = jnp.where(l0 == g * PER_GROUP + l1 % PER_GROUP, 1.0, 0.0).astype(BF16)
+        run = (dot(tri, dl) + dot(tri, dm)) + dot(tri, dh)
+        logs = jnp.log(dt) * LOG2E
+        cums[j] = jnp.concatenate([run, logs], axis=1)
+        lds[j] = logs - run
+
+    l0 = lax.broadcasted_iota(jnp.int32, (2 * HEADS, 256), 0)
+    l1 = lax.broadcasted_iota(jnp.int32, (2 * HEADS, 256), 1)
+    pick = jnp.where(
+        l0 == l1 // 128 * HEADS + g * PER_GROUP + l1 % PER_GROUP, 1.0, 0.0
+    ).astype(BF16)
     t0 = lax.broadcasted_iota(jnp.int32, (PER_GROUP, HEADS), 0)
     t1 = lax.broadcasted_iota(jnp.int32, (PER_GROUP, HEADS), 1)
     pickt = jnp.where(t1 == g * PER_GROUP + t0, 1.0, 0.0).astype(BF16)
@@ -191,7 +196,8 @@
         pt_ref[...] = jnp.zeros_like(pt_ref)
         aux_ref[...] = jnp.zeros_like(aux_ref)
         c0[...] = jnp.zeros_like(c0)
-        dx_ref[...] = spread(group(jnp.broadcast_to(gain_ref[...], (8, HEADS))), sp)
+        gains = jnp.broadcast_to(gain_ref[...], (8, HEADS))
+        dx_ref[...] = spread(group(jnp.concatenate([gains, gains], axis=1))[:, 0:128], sp)
 
     @pl.when(j == 1)
     def _():
@@ -222,9 +228,10 @@
     cb = xf[:, GW + 128 : GW + 256].astype(BF16)
     co_ref[...] = cb
 
-    cum = group(cums[j])
-    logdt = group(lds[j])
-    rh, rm, rl = split3(lds[j] - cums[j])
+    grouped = group(cums[j])
+    cum = grouped[:, 0:128]
+    logdt = grouped[:, 128:256]
+    rh, rm, rl = split3(lds[j])
     rt = (dot_nt(pickt, rl) + dot_nt(pickt, rm)) + dot_nt(pickt, rh)
     cumr[...] = cum
     last = cum[BLOCK - 1 : BLOCK, :]
@@ -246,10 +253,10 @@
     @pl.when(j == 1)
     def _():
         lead = jnp.where(seg == seg_before, jnp.exp2(cum), 0.0)
+        lp_ref[0] = spread_parts(lead)
         sh, sl = split2(s0[...])
-        parts = spread_parts(lead)
-        for cols in CHUNKS:
-            y_ref[:, cols] = dot(parts, sp[:, cols]) * (dot(cb, sh[:, cols]) + dot(cb, sl[:, cols]))
+        sh_ref[0] = sh
+        sh_ref[1] = sl
 
     both = jnp.concatenate(split2(bf.T), axis=0)
 
@@ -333,7 +340,8 @@
     )
     each = lambda *shape: pl.BlockSpec((1,) + shape, lambda g, j: (g * blocks + j, 0, 0))
     out_specs = [
-        pl.BlockSpec((BLOCK, GW), lambda g, j: (0, g)),
+        pl.BlockSpec((1, BLOCK, 128), lambda g, j: (g, 0, 0)),
+        pl.BlockSpec((2, STATE, GW), lambda g, j: (0, 0, g)),
         pl.BlockSpec((STATE, GW), lambda g, j: (0, g)),
         pl.BlockSpec((SEQS - 1, STATE, GW), lambda g, j: (0, 0, g)),
         pl.BlockSpec((8, GW), lambda g, j: (0, g)),
@@ -347,7 +355,8 @@
     ]
     steps = GROUPS * blocks
     out_shape = [
-        jax.ShapeDtypeStruct((BLOCK, D), F32),
+        jax.ShapeDtypeStruct((GROUPS, BLOCK, 128), BF16),
+        jax.ShapeDtypeStruct((2, STATE, D), BF16),
         jax.ShapeDtypeStruct((STATE, D), BF16),
         jax.ShapeDtypeStruct((SEQS - 1, STATE, D), BF16),
         jax.ShapeDtypeStruct((8, D), F32),
@@ -375,7 +384,7 @@
             pltpu.VMEM((blocks, 3, BLOCK, 128), F32),
             pltpu.VMEM((blocks, BLOCK, BLOCK), F32),
             pltpu.VMEM((blocks, BLOCK, 128), jnp.int32),
-            pltpu.VMEM((blocks, BLOCK, HEADS), F32),
+            pltpu.VMEM((blocks, BLOCK, 2 * HEADS), F32),
             pltpu.VMEM((blocks, BLOCK, HEADS), F32),
             pltpu.VMEM((8, GW + 256), F32),
             pltpu.VMEM((STATE, GW), F32),
@@ -438,6 +447,9 @@
     sc_ref,
     cum_ref,
     rt_ref,
+    lp_ref,
+    sh_ref,
+    c_ref,
     ent_ref,
     fin_ref,
     y_ref,
@@ -448,6 +460,10 @@
     scv,
     cumv,
     rtv,
+    lpv,
+    shv,
+    cv,
+    sp,
     yv,
     send1,
     recv1,
@@ -456,6 +472,7 @@
     send3,
     recv3,
     lsem,
+    wsem,
     ysem,
 ):
     me = lax.axis_index("seq")
@@ -473,6 +490,12 @@
             copy.start()
         return 0
 
+    wholes = [
+        pltpu.make_async_copy(a, v, wsem.at[i])
+        for i, (a, v) in enumerate(((lp_ref, lpv), (sh_ref, shv), (c_ref, cv)))
+    ]
+    for copy in wholes:
+        copy.start()
     lax.fori_loop(0, steps, fetch, 0)
     width = D // n
     barrier = pltpu.get_barrier_semaphore()
@@ -531,6 +554,9 @@
 
     lane = lax.broadcasted_iota(jnp.int32, (BLOCK, 128), 1)
     half = BLOCK // 2
+    sp[...] = spread_matrix()
+    for copy in wholes:
+        copy.wait()
 
     def mix(k, _):
         for copy in loads(k):
@@ -553,6 +579,18 @@
             intra = jnp.where(lane < CHANNEL_WIDTH, res[0], res[1])
             direct = dx_ref[0:1, pl.ds(pl.multiple_of(k // 2 * GW + pair * 128, 128), 128)]
             yv[k, :, span] = intra + direct * xb.astype(F32)
+
+        @pl.when(lax.rem(k, 2) == 1)
+        def _():
+            g = k // 2
+            cb = cv[BLOCK : 2 * BLOCK, pl.ds(pl.multiple_of(g * STATE, STATE), STATE)]
+            parts = lpv[g]
+            for c in range(4):
+                span = slice(c * 256, c * 256 + 256)
+                at = pl.ds(pl.multiple_of(g * GW + c * 256, 256), 256)
+                passed = dot(cb, shv[0, :, at]) + dot(cb, shv[1, :, at])
+                yv[k, :, span] = yv[k, :, span] + dot(parts, sp[:, span]) * passed
+
         store(k).start()
         return 0
 
@@ -601,14 +639,14 @@
     lax.fori_loop(0, steps, stored, 0)
 
 
-def exchange(states, aux, dx, xb, sc, cum, rt, n):
+def exchange(states, aux, dx, xb, sc, cum, rt, lead, passed, c, n):
     width = D // n
     steps = xb.shape[0]
     far = pl.BlockSpec(memory_space=pl.ANY)
     vmem = pl.BlockSpec(memory_space=pltpu.VMEM)
     return pl.pallas_call(
         functools.partial(exchange_kernel, n),
-        in_specs=[vmem] * 3 + [far] * 4,
+        in_specs=[vmem] * 3 + [far] * 7,
         out_specs=[vmem, vmem, far],
         out_shape=[
             jax.ShapeDtypeStruct((STATE, D), BF16),
@@ -623,18 +661,22 @@
             pltpu.VMEM(sc.shape, F32),
             pltpu.VMEM(cum.shape, F32),
             pltpu.VMEM(rt.shape, F32),
+            pltpu.VMEM(lead.shape, BF16),
+            pltpu.VMEM(passed.shape, BF16),
+            pltpu.VMEM(c.shape, BF16),
+            pltpu.VMEM((128, GW), BF16),
             pltpu.VMEM((steps, BLOCK, GW), F32),
         ]
         + [pltpu.SemaphoreType.DMA((n,)) for _ in range(6)]
-        + [pltpu.SemaphoreType.DMA((steps, 4)), pltpu.SemaphoreType.DMA((steps,))],
+        + [pltpu.SemaphoreType.DMA((k,)) if k != 4 else pltpu.SemaphoreType.DMA((steps, 4)) for k in (4, 3, steps)],
         compiler_params=pltpu.CompilerParams(
             collective_id=0, has_side_effects=True, vmem_limit_bytes=VMEM_LIMIT
         ),
         name="exchange",
-    )(states, aux, dx, xb, sc, cum, rt)
-
-
-def finish_kernel(len_ref, y_ref, yb_ref, c_ref, e_ref, ld_ref, gate_ref, nw_ref, out_ref, rows_ref, sp, of, scales):
+    )(states, aux, dx, xb, sc, cum, rt, lead, passed, c)
+
+
+def finish_kernel(len_ref, y_ref, c_ref, e_ref, ld_ref, gate_ref, nw_ref, out_ref, rows_ref, sp, of, scales):
     g = pl.program_id(0)
     j = pl.program_id(1)
 
@@ -647,13 +689,11 @@
         rows_ref[...] = jnp.zeros_like(rows_ref)
 
     parts = spread_parts(ld_ref[0, 0])
-    later = (j > 0).astype(F32)
     half = BLOCK // 2
     for lines in (slice(0, half), slice(half, BLOCK)):
         total = jnp.zeros((half, 128), F32)
         for cols in CHUNKS:
-            v = y_ref[0, lines, cols] + later * yb_ref[lines, cols]
-            v = v + dot(parts[lines], sp[:, cols]) * dot(c_ref[lines, :], e_ref[:, cols])
+            v = y_ref[0, lines, cols] + dot(parts[lines], sp[:, cols]) * dot(c_ref[lines, :], e_ref[:, cols])
             v = v * halves(0.5 * gate_ref[lines, cols].astype(F32))
             of[lines, cols] = v
             total = total + v[:, :128] * v[:, :128] + v[:, 128:] * v[:, 128:]
@@ -677,7 +717,7 @@
                 rows_ref[c // 2, place : place + 1, :] = line[:, c * 128 : c * 128 + 128]
 
 
-def finish(lengths, y, yb, c, entering, lead, gate, norm_weight):
+def finish(lengths, y, c, entering, lead, gate, norm_weight):
     length = gate.shape[0]
     blocks = length // BLOCK
     block = lambda width: pl.BlockSpec((BLOCK, width), lambda g, j: (j, g))
@@ -687,7 +727,6 @@
         in_specs=[
             pl.BlockSpec(memory_space=pltpu.SMEM),
             pl.BlockSpec((1, BLOCK, GW), lambda g, j: (g * blocks + j, 0, 0)),
-            pl.BlockSpec((BLOCK, GW), lambda g, j: (0, g)),
             block(STATE),
             pl.BlockSpec((STATE, GW), lambda g, j: (0, g)),
             pl.BlockSpec((1, 1, BLOCK, 128), lambda g, j: (g, j, 0, 0)),
@@ -708,7 +747,7 @@
             vmem_limit_bytes=VMEM_LIMIT, dimension_semantics=("arbitrary", "arbitrary")
         ),
         name="finish",
-    )(lengths, y, yb, c, entering, lead, gate, norm_weight)
+    )(lengths, y, c, entering, lead, gate, norm_weight)
 
 
 def tail_kernel(
@@ -733,6 +772,7 @@
     h1,
     h2,
     hf,
+    tv,
     mx1,
     mx2,
     p1,
@@ -740,6 +780,7 @@
     p3,
     p4,
     vsem,
+    tsem,
     rs_s,
     rs_r,
     ag_s,
@@ -776,6 +817,8 @@
     from_s = 8 * lax.rem(s, 2)
 
     load = pltpu.make_async_copy(vocab_ref, vbuf, vsem)
+    tload = pltpu.make_async_copy(tails_ref, tv, tsem)
+    tload.start()
     load.start()
 
     barrier = pltpu.get_barrier_semaphore()
@@ -936,7 +979,7 @@
             for i in range(2):
 
                 def step(q, _):
-                    p1[v, i, q] = p1[v, i, q] + tails_ref[block(v, c if i == 0 else far(c), q)]
+                    p1[v, i, q] = p1[v, i, q] + tv[block(v, c if i == 0 else far(c), q)]
                     return 0
 
                 lax.fori_loop(0, 4, step, 0)
@@ -1009,6 +1052,7 @@
     part_go()
     precv[s] = part[s // 2, :, pl.ds(pl.multiple_of(lax.rem(s, 2) * 256, 256), 256)]
     each(1, got)
+    tload.wait()
     add1()
     each(2, go)
     part_in()
@@ -1092,7 +1136,10 @@
     dma = pltpu.SemaphoreType.DMA
     return pl.pallas_call(
         functools.partial(tail_kernel, n, m),
-        in_specs=[vmem] * 6 + [pl.BlockSpec(memory_space=pl.ANY)],
+        in_specs=[vmem] * 2
+        + [pl.BlockSpec(memory_space=pl.ANY)]
+        + [vmem] * 3
+        + [pl.BlockSpec(memory_space=pl.ANY)],
         out_specs=[vmem] * 3,
         out_shape=[
             jax.ShapeDtypeStruct((1, SEQS, D), BF16),
@@ -1109,12 +1156,14 @@
             pltpu.VMEM((m, 8, 128), BF16),
             pltpu.VMEM((n // 2, 2, m, 8, 128), BF16),
             pltpu.VMEM((8 * m, D), F32),
+            pltpu.VMEM(tails.shape, BF16),
             pltpu.VMEM((m, 8, 128), F32),
             pltpu.VMEM((n, 8, 128), F32),
             pltpu.VMEM((4, 2, 4, SEQS - 1, 32, width), BF16),
             pltpu.VMEM((4, 4, SEQS - 1, 32, width), BF16),
             pltpu.VMEM((4, 2, SEQS - 1, 32, width), BF16),
             pltpu.VMEM((4, SEQS - 1, 32, width), BF16),
+            dma,
             dma,
             dma((n,)),
             dma((n,)),
@@ -1190,7 +1239,7 @@
     req_count = lax.axis_size("req")
     conv = conv_input[0]
     halo = halo_rows(conv, seq_count)
-    yb, states, tails, aux, c, lead, xb, sc, cum, rt, dx = local_pass(
+    lead_parts, passed, states, tails, aux, c, lead, xb, sc, cum, rt, dx = local_pass(
         lengths,
         conv,
         halo,
@@ -1201,8 +1250,10 @@
         decay_log[None],
         head_direct_gain[None],
     )
-    entering, reached, y = exchange(states, aux, dx, xb, sc, cum, rt, seq_count)
-    gated, rows = finish(lengths, y, yb, c, entering, lead, gate_projected[0], norm_weight[None])
+    entering, reached, y = exchange(
+        states, aux, dx, xb, sc, cum, rt, lead_parts, passed, c, seq_count
+    )
+    gated, rows = finish(lengths, y, c, entering, lead, gate_projected[0], norm_weight[None])
     hid, top, final = tail(
         rows, out_weight, tails, reached, residual_last, final_gain[None], vocab_weight, seq_count, req_count
     )

time: 153 us -> 146 us (0.954)
  Pallas kernels: 152 us -> 144 us
    pallas_call x1, Pallas kernels: 41.5 us -> 36.3 us  [exchange(): pl.pallas_call(functools.partial(exchange_kernel, n), in_specs=[vmem] * 3...]
where the time goes in v8:
time: 146 us; the launch traced here: 145 us
  Pallas kernels  144 us (99%)
    pallas_call x1, Pallas kernels, tail(): pl.pallas_call(functools.partial(tail_kernel, n, m), in_specs=[vmem] * 2...  55.6 us
    pallas_call x1, Pallas kernels, exchange(): pl.pallas_call(functools.partial(exchange_kernel, n), in_specs=[vmem] * 3...  36.3 us
    pallas_call x1, Pallas kernels, local_pass(): pl.pallas_call(local_kernel, grid=grid, in_specs=in_specs, out_specs=out_...  28.5 us
    pallas_call x1, Pallas kernels, finish(): pl.pallas_call(finish_kernel, grid=(GROUPS, length // BLOCK), in_specs=[p...  11.6 us
    pallas_call x1, Pallas kernels, halo_rows(): pl.pallas_call(functools.partial(halo_kernel, n), in_specs=[pl.BlockSpec(...  9.94 us

profile of v8, /device:TPU:1, one launch (start us, length us, event | category | flops | bytes accessed | tf_op | source)
XLA Modules:
  0.0 144.7 jit_solution(9083353408158468146)
XLA Ops:
  0.6 9.9 %halo.1.xh_ref.bh_ref.ch_ref = bf16[8,5120]{1,0:T(8,128)(2,1)} custom-call(bf16[512,5120]{1,0:T(8,128)(2,1)} %bitcast.13), custom_call_target="tpu_custom_call" | custom-call | tf_op jit(solution)/shard_map/halo/pallas_call | solution.py:426
  10.6 28.5 %local_pass.1 = (bf16[4,256,128]{2,1,0:T(8,128)(2,1)}, bf16[2,128,4096]{2,1,0:T(8,128)(2,1)}, bf16[128,4096]{1,0:T(8,128)(2,1)}, bf16[3,128,4096]{2,1,0:T(8,128)...) custom-call(s32[1,4]{1,0:T(1,128)} %len_ref.3, ...), custom_call_target="tpu_custom_call" | custom-call | tf_op jit(solution)/shard_map/local_pass/pallas_call | solution.py:371
  39.1 36.3 %exchange.1 = (bf16[128,4096]{1,0:T(8,128)(2,1)}, f32[4,128,256]{2,1,0:T(8,128)}, f32[8,256,1024]{2,1,0:T(8,128)}) custom-call(bf16[128,4096]{1,0:T(8,128)(2,1)} %get-tuple-element.27.st_ref, f32[8,4096]{1,0:T(8,128)} %get-tuple-element.28.aux_ref, f32[8,4096]{1,0:T(8,128)} %get-tuple-element.29.dx_ref, bf16[8,256,1024]{2,1,0:T(8,128)(2,1)} %get-tuple-element.30.xb_ref, ...), custom_call_target="tpu_custom_call" | custom-call | tf_op jit(solution)/shard_map/exchange/pallas_call | solution.py:647
  75.4 11.6 %finish.1 = (bf16[512,4096]{1,0:T(8,128)(2,1)}, f32[16,8,128]{2,1,0:T(8,128)}) custom-call(s32[1,4]{1,0:T(1,128)} %len_ref.3, f32[8,256,1024]{2,1,0:T(8,128)} %get-tuple-element.37.y_ref, bf16[512,512]{1,0:T(8,128)(2,1)} %get-tuple-element.36.c_ref, bf16[128,4096]{1,0:T(8,128)(2,1)} %get-tuple-element.38.e_ref, f32[4,2,256,128]{3,2,1,0:T(8,128)} %get-tuple-element.39.ld_ref, ...), custom_call_target="tpu_custom_call" | custom-call | tf_op jit(solution)/shard_map/finish/pallas_call | solution.py:724
  87.0 55.6 %tail.1 = (bf16[1,4,4096]{2,1,0:T(4,128)(2,1)}, f32[1,4]{1,0:T(1,128)}, f32[4,128,256]{2,1,0:T(8,128)}) custom-call(f32[16,8,128]{2,1,0:T(8,128)} %get-tuple-element.41.rows_ref, bf16[32,4096]{1,0:T(8,128)(2,1)} %w_ref.1, bf16[3,128,4096]{2,1,0:T(8,128)(2,1)} %get-tuple-element.42.tails_ref, f32[4,128,256]{2,1,0:T(8,128)} %get-tuple-element.43.reach_ref, ...), custom_call_target="tpu_custom_call" | custom-call | tf_op jit(solution)/shard_map/tail/pallas_call | solution.py:1137
  142.7 2.1 %pack.1 = (f32[4,256,128]{2,1,0:T(8,128)}, bf16[1,4,4096]{2,1,0:T(4,128)(2,1)}, f32[1,4]{1,0:T(1,128)}) custom-call(f32[4,128,256]{2,1,0:T(8,128)} %get-tuple-element.44.fin_ref, bf16[1,4,4096]{2,1,0:T(4,128)(2,1)} %get-tuple-element.45.hid_ref, f32[1,4]{1,0:T(1,128)} %get-tuple-element.46.top_ref), custom_call_target="tpu_custom_call" | custom-call | tf_op jit(solution)/shard_map/pack/pallas_call | solution.py:1209
